TPU v7x, 32 devices: a whole 2x2x4 slice. The times are simulated.
32 devices in a mesh: section: 2 (over y), dp: 16 (over z, x, core).
Axes of the slice: x: 2, y: 2, z: 4, core: 2. Of those that a mesh axis runs over, the one named last changes fastest.
Arguments:
- boundary: bfloat16 [2, 16384, 768], P('section', 'dp'), may hold values from -10 to 10
- lengths: int32 [32], P('dp'), may hold values from 128 to 512, as said below
- neighbours: int32 [16384, 40], P('dp'), may hold values from 0 to 511, as said below
- counts: int32 [16384], P('dp'), may hold values from 1 to 40, as said below
- coords: float32 [16384], P('dp'), may hold values from 0 to 16
- square_weights: bfloat16 [2, 4, 768, 768], P('section'), may hold values from -2 to 2
- up_weight: bfloat16 [2, 768, 3072], P('section'), may hold values from -0.21875 to 0.21875
- down_weight: bfloat16 [2, 3072, 768], P('section'), may hold values from -0.109375 to 0.109375
- up_bias: float32 [2, 3072], P('section'), may hold values from -1.5 to 1.5
- norm_gain: float32 [2, 2, 768], P('section'), may hold values from 0.5 to 1.5
- norm_bias: float32 [2, 2, 768], P('section'), may hold values from -0.5 to 0.5
- rich_terms: float32 [2, 12], replicated, may hold values from -1 to 1
Outputs:
- boundary_out: bfloat16 [2, 16384, 768], P('section', 'dp')
- grad_squares: float32 [2, 4, 768, 768], P('section')
- grad_up: float32 [2, 768, 3072], P('section')
- grad_down: float32 [2, 3072, 768], P('section')
- grad_up_bias: float32 [2, 3072], P('section')
- grad_gain: float32 [2, 2, 768], P('section')
- grad_bias: float32 [2, 2, 768], P('section')
- grad_rich: float32 [2, 12], replicated
- rms: float32 [2, 4], replicated
Inputs may be any that keep to these rules, and one draw needn't show every extreme that they name: `lengths`: at least a quarter of a slot; some document fills its slot. `neighbours`: positions of the token's own document at most 64 from it; a live token's neighbours are live, a padding token's are padding; slots at or past the count hold 0. `counts`: some token uses all 40 slots.
All inputs are finite; a program needn't handle non-finite values.
Results may differ from a plain program's by a relative error of at most 0.013.
Values may be sent and summed in bfloat16 or wider, within the bound.
No kernel may reach another device: no remote copies, remote signals or barrier semaphores. Data moves between devices by JAX's collectives and lax.ppermute only.
A program may use at most 448 MiB of HBM per device.

v0:
```python
import jax
import jax.numpy as jnp
from jax import lax
from jax.sharding import PartitionSpec as P

RADIUS = 128
BLOCK = 512


EPSILON = 1e-05
NEG_FILL = -1e30


def passed_along(block, axis, distance):
    devices = range(lax.axis_size(axis))
    route = [(i - distance, i) for i in devices if i - distance in devices]
    return lax.ppermute(block, axis, route)


def norm_forward(vector, gain_row, shift_row):
    center = vector - jnp.mean(vector, axis=-1, keepdims=True)
    inverse = lax.rsqrt(jnp.mean(center * center, axis=-1, keepdims=True) + EPSILON)
    return center * inverse * gain_row + shift_row


def norm_backward(vector, gain_row, shift_row, grad_normed):
    return jax.vjp(norm_forward, vector, gain_row, shift_row)[1](grad_normed)


def round_low(vector):
    return vector.astype(jnp.bfloat16)


def product(left, right):
    return jnp.dot(left, right, preferred_element_type=jnp.float32)


def product_left(left, right):
    return lax.dot_general(
        left, right, (((0,), (0,)), ((), ())), preferred_element_type=jnp.float32
    )


def product_right(left, right):
    return lax.dot_general(
        left, right, (((1,), (1,)), ((), ())), preferred_element_type=jnp.float32
    )


def gate_mix(pre_sum, gate_pre):
    return pre_sum * jax.nn.sigmoid(gate_pre)


def mlp_forward(resid, gain_row, shift_row, up_matrix, bias_row, down_matrix):
    normed_low = round_low(norm_forward(resid, gain_row, shift_row))
    pre_act = product(normed_low, up_matrix) + bias_row
    active_low = round_low(jax.nn.gelu(pre_act))
    branch = product(active_low, down_matrix)
    return (branch, (resid, normed_low, pre_act, active_low))


def mlp_backward(kept, grad_resid, gain_row, shift_row, up_matrix, down_matrix):
    resid, normed_low, pre_act, active_low = kept
    grad_low = round_low(grad_resid)
    grad_down = product_left(active_low, grad_low)
    grad_active = product_right(grad_low, down_matrix)
    grad_pre = round_low(jax.vjp(jax.nn.gelu, pre_act)[1](grad_active)[0])
    grad_up = product_left(normed_low, grad_pre)
    grad_bias_up = jnp.sum(grad_pre.astype(jnp.float32), axis=0)
    grad_normed = product_right(grad_pre, up_matrix)
    grad_input, grad_gain, grad_shift = norm_backward(resid, gain_row, shift_row, grad_normed)
    return (grad_resid + grad_input, (grad_up, grad_bias_up, grad_down, grad_gain, grad_shift))


def adjacency_rows(neighbours, counts, total_rows):
    index_rows = neighbours
    slot_ids = jnp.arange(index_rows.shape[1])
    index_rows = jnp.where(slot_ids[None, :] < counts[:, None], index_rows, -1)
    columns = jnp.arange(total_rows)
    matches = index_rows[:, :, None] == columns[None, None, :]
    return jnp.sum(matches, axis=1, dtype=jnp.int32).astype(jnp.bfloat16)


def graph_forward(inputs, neighbours, counts, squares, gain_row, shift_row):
    total_rows = inputs.shape[0]
    normed_low = round_low(norm_forward(inputs, gain_row, shift_row))
    adjacency = adjacency_rows(neighbours, counts, total_rows)
    divisor = counts.astype(jnp.float32)[:, None]
    mean_low = round_low(product(adjacency, normed_low) / divisor)
    pre_sum = product(normed_low, squares[0]) + product(mean_low, squares[1])
    gate_pre = product(mean_low, squares[2])
    mixed_low = round_low(gate_mix(pre_sum, gate_pre))
    branch = product(mixed_low, squares[3])
    return (
        branch,
        (inputs, normed_low, adjacency, divisor, mean_low, pre_sum, gate_pre, mixed_low),
    )


def graph_backward(kept, grad_resid, squares, gain_row, shift_row):
    inputs, normed_low, adjacency, divisor, mean_low, pre_sum, gate_pre, mixed_low = kept
    grad_low = round_low(grad_resid)
    grad_output_w = product_left(mixed_low, grad_low)
    grad_mixed = product_right(grad_low, squares[3])
    grad_pre, grad_gate = jax.vjp(gate_mix, pre_sum, gate_pre)[1](grad_mixed)
    grad_pre = round_low(grad_pre)
    grad_gate = round_low(grad_gate)
    grad_self_w = product_left(normed_low, grad_pre)
    grad_near_w = product_left(mean_low, grad_pre)
    grad_gate_w = product_left(mean_low, grad_gate)
    grad_mean = product_right(grad_pre, squares[1]) + product_right(grad_gate, squares[2])
    grad_total = round_low(grad_mean / divisor)
    grad_normed = product_right(grad_pre, squares[0]) + product_left(adjacency, grad_total)
    grad_input, grad_gain, grad_shift = norm_backward(inputs, gain_row, shift_row, grad_normed)
    return (
        grad_resid + grad_input,
        (jnp.stack([grad_self_w, grad_near_w, grad_gate_w, grad_output_w]), grad_gain, grad_shift),
    )


def band_terms(row_start, block_rows, radius, total_rows, length, coords_pad, rich_terms):
    query_pos = row_start + jnp.arange(block_rows)
    key_pos = row_start - radius + jnp.arange(block_rows + 2 * radius)
    nearby = jnp.abs(query_pos[:, None] - key_pos[None, :]) <= radius
    inside = (key_pos >= 0) & (key_pos < total_rows)
    living = (key_pos < length)[None, :] | (key_pos[None, :] == query_pos[:, None])
    allowed = nearby & inside[None, :] & living
    query_coord = coords_pad[row_start + radius : row_start + radius + block_rows]
    offset = query_coord[:, None] - coords_pad[None, :]
    spread = jnp.log1p(jnp.abs(offset))
    order_term = jnp.tanh(-offset)
    rich_bias = (
        rich_terms[0][:, None, None] * spread[None]
        + rich_terms[1][:, None, None] * order_term[None]
    )
    return (allowed, spread, order_term, rich_bias)


def attention_forward(
    inputs, length, coords, squares, gain_row, shift_row, rich_terms, head_count, radius, block_rows
):
    total_rows, model_width = inputs.shape
    head_width = model_width // head_count
    score_scale = head_width ** (-0.5)
    normed_low = round_low(norm_forward(inputs, gain_row, shift_row))
    query_rows = round_low(product(normed_low, squares[0])).reshape(
        total_rows, head_count, head_width
    )
    key_rows = round_low(product(normed_low, squares[1])).reshape(
        total_rows, head_count, head_width
    )
    value_rows = round_low(product(normed_low, squares[2])).reshape(
        total_rows, head_count, head_width
    )
    margin = ((radius, radius), (0, 0), (0, 0))
    key_pad = jnp.pad(key_rows, margin)
    value_pad = jnp.pad(value_rows, margin)
    coords_pad = jnp.pad(coords, (radius, radius))
    allowed, spread, order_term, rich_bias = band_terms(
        0, block_rows, radius, total_rows, length, coords_pad, rich_terms
    )
    raw_scores = jnp.einsum("qhd,khd->hqk", query_rows, key_pad, preferred_element_type=jnp.float32)
    scores = jnp.where(allowed[None], raw_scores * score_scale + rich_bias, NEG_FILL)
    highest = jnp.max(scores, axis=-1, keepdims=True)
    weights = jnp.exp(scores - highest)
    row_total = jnp.sum(weights, axis=-1, keepdims=True)
    probs_low = round_low(weights / row_total)
    context = jnp.einsum("hqk,khd->qhd", probs_low, value_pad, preferred_element_type=jnp.float32)
    contexts = [context.reshape(block_rows, model_width)]
    log_totals = [highest + jnp.log(row_total)]
    context_low = round_low(jnp.concatenate(contexts, axis=0))
    branch = product(context_low, squares[3])
    return (
        branch,
        (inputs, normed_low, query_rows, key_pad, value_pad, coords_pad, context_low, log_totals),
    )


def attention_backward(
    kept,
    grad_resid,
    length,
    squares,
    gain_row,
    shift_row,
    rich_terms,
    head_count,
    radius,
    block_rows,
):
    inputs, normed_low, query_rows, key_pad, value_pad, coords_pad, context_low, log_totals = kept
    total_rows, model_width = inputs.shape
    head_width = model_width // head_count
    score_scale = head_width ** (-0.5)
    grad_low = round_low(grad_resid)
    grad_output_w = product_left(context_low, grad_low)
    grad_context = round_low(product_right(grad_low, squares[3])).reshape(
        total_rows, head_count, head_width
    )
    grad_queries = []
    grad_key_pad = jnp.zeros(key_pad.shape, jnp.float32)
    grad_value_pad = jnp.zeros(value_pad.shape, jnp.float32)
    grad_rich = jnp.zeros((2, head_count), jnp.float32)
    for block_index, row_start in enumerate(range(0, total_rows, block_rows)):
        window_end = row_start + block_rows + 2 * radius
        allowed, spread, order_term, rich_bias = band_terms(
            row_start, block_rows, radius, total_rows, length, coords_pad, rich_terms
        )
        raw_scores = jnp.einsum(
            "qhd,khd->hqk", query_rows, key_pad, preferred_element_type=jnp.float32
        )
        scores = jnp.where(allowed[None], raw_scores * score_scale + rich_bias, NEG_FILL)
        probs = jnp.exp(scores - log_totals[block_index])
        probs_low = round_low(probs)
        grad_probs = jnp.einsum(
            "qhd,khd->hqk", grad_context, value_pad, preferred_element_type=jnp.float32
        )
        inner = jnp.sum(probs * grad_probs, axis=-1, keepdims=True)
        grad_scores = probs * (grad_probs - inner)
        grad_rich = grad_rich + jnp.stack(
            [
                jnp.sum(grad_scores * spread[None], axis=(1, 2)),
                jnp.sum(grad_scores * order_term[None], axis=(1, 2)),
            ]
        )
        grad_raw = round_low(grad_scores * score_scale)
        grad_queries.append(
            jnp.einsum("hqk,khd->qhd", grad_raw, key_pad, preferred_element_type=jnp.float32)
        )
        grad_key_pad = grad_key_pad.at[row_start:window_end].add(
            jnp.einsum("hqk,qhd->khd", grad_raw, query_rows, preferred_element_type=jnp.float32)
        )
        grad_value_pad = grad_value_pad.at[row_start:window_end].add(
            jnp.einsum("hqk,qhd->khd", probs_low, grad_context, preferred_element_type=jnp.float32)
        )
    grad_query = round_low(jnp.concatenate(grad_queries, axis=0).reshape(total_rows, model_width))
    grad_key = round_low(
        grad_key_pad[radius : radius + total_rows].reshape(total_rows, model_width)
    )
    grad_value = round_low(
        grad_value_pad[radius : radius + total_rows].reshape(total_rows, model_width)
    )
    grad_square = jnp.stack(
        [
            product_left(normed_low, grad_query),
            product_left(normed_low, grad_key),
            product_left(normed_low, grad_value),
            grad_output_w,
        ]
    )
    grad_normed = (
        product_right(grad_query, squares[0])
        + product_right(grad_key, squares[1])
        + product_right(grad_value, squares[2])
    )
    grad_input, grad_gain, grad_shift = norm_backward(inputs, gain_row, shift_row, grad_normed)
    return (grad_resid + grad_input, (grad_square, grad_gain, grad_shift), grad_rich)


def live_squares(length, quantities):
    live_rows = (jnp.arange(quantities[0].shape[0]) < length).astype(jnp.float32)[:, None]
    return jnp.stack([jnp.sum(live_rows * item * item) for item in quantities])


def add_mlp(gradients, mlp_grads):
    grad_square, grad_up, grad_bias_up, grad_down, grad_gain, grad_shift = gradients
    part_up, part_bias, part_down, part_gain, part_shift = mlp_grads
    return (
        grad_square,
        grad_up + part_up,
        grad_bias_up + part_bias,
        grad_down + part_down,
        grad_gain.at[1].add(part_gain),
        grad_shift.at[1].add(part_shift),
    )


def add_first(gradients, first_grads):
    grad_square, grad_up, grad_bias_up, grad_down, grad_gain, grad_shift = gradients
    part_square, part_gain, part_shift = first_grads
    return (
        grad_square + part_square,
        grad_up,
        grad_bias_up,
        grad_down,
        grad_gain.at[0].add(part_gain),
        grad_shift.at[0].add(part_shift),
    )


def empty_keep(total_rows, model_width, hidden):

    def blank(columns, kind):
        return jnp.zeros((total_rows, columns), kind)

    graph_keep = (
        blank(model_width, jnp.float32),
        blank(model_width, jnp.bfloat16),
        blank(total_rows, jnp.bfloat16),
        blank(1, jnp.float32),
        blank(model_width, jnp.bfloat16),
        blank(model_width, jnp.float32),
        blank(model_width, jnp.float32),
        blank(model_width, jnp.bfloat16),
    )
    mlp_keep = (
        blank(model_width, jnp.float32),
        blank(model_width, jnp.bfloat16),
        blank(hidden, jnp.float32),
        blank(hidden, jnp.bfloat16),
    )
    return (graph_keep, mlp_keep)


def local(
    boundary,
    lengths,
    neighbours,
    counts,
    coords,
    square_weights,
    up_weight,
    down_weight,
    up_bias,
    norm_gain,
    norm_bias,
    rich_terms,
):
    section_index = lax.axis_index("section")
    first_section = section_index == 0
    micro_count = lengths.shape[0]
    local_rows = boundary[0]
    total_rows = local_rows.shape[0] // micro_count
    model_width = local_rows.shape[1]
    hidden = up_weight.shape[2]
    head_count = rich_terms.shape[1]
    square_local = square_weights[0]
    up_local = up_weight[0]
    down_local = down_weight[0]
    bias_local = up_bias[0]
    gains = norm_gain[0]
    shifts = norm_bias[0]

    def rows_of(array, doc_index):
        return array[doc_index * total_rows : (doc_index + 1) * total_rows]

    zero_rows = jnp.zeros((total_rows, model_width), jnp.bfloat16)
    gradients = (
        jnp.zeros(square_local.shape, jnp.float32),
        jnp.zeros(up_local.shape, jnp.float32),
        jnp.zeros(bias_local.shape, jnp.float32),
        jnp.zeros(down_local.shape, jnp.float32),
        jnp.zeros(gains.shape, jnp.float32),
        jnp.zeros(shifts.shape, jnp.float32),
    )
    grad_rich = jnp.zeros((2, head_count), jnp.float32)
    stat_sums = jnp.zeros((4,), jnp.float32)
    kept_list = [None] * micro_count
    grad_rows = [zero_rows] * micro_count
    act_rows = [zero_rows] * micro_count
    inbound_act = zero_rows
    inbound_grad = zero_rows
    for tick_index in range(micro_count + 1):

        def first_branch():
            new_grads = gradients
            finished = zero_rows
            if tick_index >= 2:
                graph_keep, mlp_keep = kept_list[tick_index - 2]
                grad_middle, mlp_grads = mlp_backward(
                    mlp_keep,
                    inbound_grad.astype(jnp.float32),
                    gains[1],
                    shifts[1],
                    up_local,
                    down_local,
                )
                grad_input, first_grads = graph_backward(
                    graph_keep, grad_middle, square_local, gains[0], shifts[0]
                )
                new_grads = add_first(add_mlp(gradients, mlp_grads), first_grads)
                finished = round_low(grad_input)
            send_act = zero_rows
            new_stats = stat_sums
            new_keep = None
            if tick_index < micro_count:
                inputs = rows_of(local_rows, tick_index).astype(jnp.float32)
                branch_one, graph_keep = graph_forward(
                    inputs,
                    rows_of(neighbours, tick_index),
                    rows_of(counts, tick_index),
                    square_local,
                    gains[0],
                    shifts[0],
                )
                resid_one = inputs + branch_one
                branch_two, mlp_keep = mlp_forward(
                    resid_one, gains[1], shifts[1], up_local, bias_local, down_local
                )
                resid_two = resid_one + branch_two
                new_stats = stat_sums + live_squares(
                    lengths[tick_index], (branch_one, resid_one, branch_two, resid_two)
                )
                send_act = round_low(resid_two)
                new_keep = (graph_keep, mlp_keep)
            return (send_act, zero_rows, finished, new_grads, grad_rich, new_stats, new_keep)

        def second_branch():
            new_grads = gradients
            new_rich = grad_rich
            new_stats = stat_sums
            finished = zero_rows
            send_grad = zero_rows
            if 1 <= tick_index <= micro_count:
                doc_index = tick_index - 1
                length = lengths[doc_index]
                inputs = inbound_act.astype(jnp.float32)
                branch_one, attend_keep = attention_forward(
                    inputs,
                    length,
                    rows_of(coords, doc_index),
                    square_local,
                    gains[0],
                    shifts[0],
                    rich_terms,
                    head_count,
                    RADIUS,
                    BLOCK,
                )
                resid_one = inputs + branch_one
                branch_two, mlp_keep = mlp_forward(
                    resid_one, gains[1], shifts[1], up_local, bias_local, down_local
                )
                resid_two = resid_one + branch_two
                new_stats = stat_sums + live_squares(
                    length, (branch_one, resid_one, branch_two, resid_two)
                )
                finished = round_low(resid_two)
                grad_middle, mlp_grads = mlp_backward(
                    mlp_keep,
                    rows_of(local_rows, doc_index).astype(jnp.float32),
                    gains[1],
                    shifts[1],
                    up_local,
                    down_local,
                )
                grad_input, first_grads, rich_part = attention_backward(
                    attend_keep,
                    grad_middle,
                    length,
                    square_local,
                    gains[0],
                    shifts[0],
                    rich_terms,
                    head_count,
                    RADIUS,
                    BLOCK,
                )
                new_grads = add_first(add_mlp(gradients, mlp_grads), first_grads)
                new_rich = grad_rich + rich_part
                send_grad = round_low(grad_input)
            new_keep = (
                empty_keep(total_rows, model_width, hidden) if tick_index < micro_count else None
            )
            return (zero_rows, send_grad, finished, new_grads, new_rich, new_stats, new_keep)

        send_act, send_grad, finished, gradients, grad_rich, stat_sums, new_keep = lax.cond(
            first_section, first_branch, second_branch
        )
        if tick_index < micro_count:
            kept_list[tick_index] = new_keep
            inbound_act = passed_along(send_act, "section", 1)
        if tick_index >= 1:
            act_rows[tick_index - 1] = finished
            inbound_grad = passed_along(send_grad, "section", -1)
        if tick_index >= 2:
            grad_rows[tick_index - 2] = finished
    count_term = jnp.where(section_index == 1, jnp.sum(lengths).astype(jnp.float32), 0.0)
    stat_rows = jnp.where(jnp.arange(2)[:, None] == section_index, stat_sums[None, :], 0.0)
    rich_total, stat_total, count_total = lax.psum(
        (grad_rich, stat_rows, count_term), ("section", "dp")
    )
    rms = jnp.sqrt(stat_total / (count_total * model_width))

    def tail_mlp():
        grad_middle, mlp_grads = mlp_backward(
            kept_list[micro_count - 1][1],
            inbound_grad.astype(jnp.float32),
            gains[1],
            shifts[1],
            up_local,
            down_local,
        )
        return (grad_middle, add_mlp(gradients, mlp_grads))

    def tail_spare():
        return (jnp.zeros((total_rows, model_width), jnp.float32), gradients)

    grad_middle, gradients = lax.cond(first_section, tail_mlp, tail_spare)

    def tail_graph():
        grad_input, first_grads = graph_backward(
            kept_list[micro_count - 1][0], grad_middle, square_local, gains[0], shifts[0]
        )
        return (round_low(grad_input), add_first(gradients, first_grads))

    def tail_rest():
        return (zero_rows, gradients)

    finished, gradients = lax.cond(first_section, tail_graph, tail_rest)
    grad_rows[micro_count - 1] = finished
    square_total, up_total, bias_total, down_total, gain_total, shift_total = lax.psum(
        (gradients[0], gradients[1], gradients[2], gradients[3], gradients[4], gradients[5]), "dp"
    )
    rows_out = [
        jnp.where(first_section, grad_rows[doc_index], act_rows[doc_index])
        for doc_index in range(micro_count)
    ]
    boundary_out = jnp.concatenate(rows_out, axis=0)[None]
    return (
        boundary_out,
        square_total[None],
        up_total[None],
        down_total[None],
        bias_total[None],
        gain_total[None],
        shift_total[None],
        rich_total,
        rms,
    )


def solution(mesh):
    in_specs = (
        P("section", "dp", None),
        P("dp"),
        P("dp", None),
        P("dp"),
        P("dp"),
        P("section", None, None, None),
        P("section", None, None),
        P("section", None, None),
        P("section", None),
        P("section", None, None),
        P("section", None, None),
        P(),
    )
    out_specs = (
        P("section", "dp", None),
        P("section", None, None, None),
        P("section", None, None),
        P("section", None, None),
        P("section", None),
        P("section", None, None),
        P("section", None, None),
        P(),
        P(),
    )
    return jax.shard_map(local, mesh=mesh, in_specs=in_specs, out_specs=out_specs, check_vma=False)
```

profile of v0, /device:TPU:0, one launch (start us, length us, event | category | flops | bytes accessed | tf_op | source)
XLA Modules:
  0.0 1181.4 jit_solution(14346457519551695484)
XLA Ops:
  7.3 53.1 %conditional.7 = (bf16[512,768]{1,0:T(8,128)(2,1)}, f32[4]{0:T(128)S(1)}, f32[512,768]{1,0:T(8,128)S(1)}, bf16[512,768]{1,0:T(8,128)(2,1)}, bf16[512,512]{1,0:T(...) conditional(s32[]{:T(128)} %convert_element_type.338, ...), branch_computations={%region_0.0_spmd, %region_1.11_spmd} | conditional | flops 7714155008 | bytes 125708952 | solution.py:467
  10.6 15.6 %convert_reduce_fusion = s32[512,512]{1,0:T(8,128)S(1)} fusion(s32[512,40]{1,0:T(8,128)S(1)} %slice_select_fusion), kind=kLoop, calls=%fused_computation | loop fusion | flops 31195136 | bytes 1130496 | tf_op jit(solution)/shard_map/cond/branch_1_fun/reduce_sum | solution.py:81
  27.2 3.3 divide_convert_fusion
  30.5 3.4 fusion.14
  36.0 2.6 multiply_convert_fusion
  44.3 6.5 fusion.7
  50.9 6.8 fusion.9
  57.7 2.7 pad_maximum_fusion
  62.9 18.0 %collective-permute-done = bf16[512,768]{1,0:T(8,128)(2,1)S(1)} collective-permute-done((bf16[512,768]{1,0:T(8,128)(2,1)}, bf16[512,768]{1,0:T(8,128)(2,1)S(1)}, u32[]{:S(2)}, u32[]{:S(2)}) %collective-permute-start) | collective-permute-done | bytes 786464 | tf_op jit(solution)/shard_map/ppermute | solution.py:17
  80.8 64.9 %conditional.8 = (bf16[512,768]{1,0:T(8,128)(2,1)S(1)}, bf16[512,768]{1,0:T(8,128)(2,1)S(1)}, bf16[512,768]{1,0:T(8,128)(2,1)}, f32[4,768,768]{2,1,0:T(8,128)}, ...) conditional(s32[]{:T(128)} %convert_element_type.338, ...), branch_computations={%region_11.34_spmd, %region_34.44_spmd} | conditional | flops 25623932928 | bytes 664969856 | solution.py:467
  93.3 15.6 %convert_reduce_fusion.3 = s32[512,512]{1,0:T(8,128)S(1)} fusion(s32[512,40]{1,0:T(8,128)S(1)} %slice_select_fusion.1), kind=kLoop, calls=%fused_computation.207 | loop fusion | flops 31195136 | bytes 1130496 | tf_op jit(solution)/shard_map/cond/branch_1_fun/reduce_sum | solution.py:81
  109.7 2.9 fusion.138
  117.4 6.4 fusion.131
  125.1 6.2 fusion.133
  131.3 2.7 maximum_add_fusion.1
  134.1 4.6 broadcast_in_dim.141
  138.7 4.9 broadcast_in_dim.142
  145.7 142.4 %collective-permute-start.1 = (bf16[512,768]{1,0:T(8,128)(2,1)S(1)}, bf16[512,768]{1,0:T(8,128)(2,1)S(1)}, u32[]{:S(2)}, u32[]{:S(2)}) collective-permute-start(bf16[512,768]{1,0:T(8,128)(2,1)S(1)} %get-tuple-element.700), channel_id=1, source_target_pairs={{0,16},{1,17},{2,18},{3,19},{4,20},{5,21},{6,22},{7,23},{8,24},{9,... | collective-permute-start | bytes 2359304 | tf_op jit(solution)/shard_map/ppermute | solution.py:17
  289.4 15.5 %collective-permute-done.1 = bf16[512,768]{1,0:T(8,128)(2,1)S(1)} collective-permute-done((bf16[512,768]{1,0:T(8,128)(2,1)S(1)}, bf16[512,768]{1,0:T(8,128)(2,1)S(1)}, u32[]{:S(2)}, u32[]{:S(2)}) %collective-permute-start.1) | collective-permute-done | bytes 786464 | tf_op jit(solution)/shard_map/ppermute | solution.py:17
  304.9 4.2 collective-permute-done.2
  309.0 139.4 %conditional.12 = (bf16[512,768]{1,0:T(8,128)(2,1)S(1)}, f32[4,768,768]{2,1,0:T(8,128)}, f32[768,3072]{1,0:T(8,128)}, f32[3072]{0:T(1024)S(1)}, f32[3072,768]{1,...) conditional(s32[]{:T(128)} %convert_element_type.338, ...), branch_computations={%region_44.67_spmd, %region_67.81_spmd} | conditional | flops 25631012864 | bytes 758499200
  317.7 3.6 copy-done.15
  327.6 9.7 convert_reduce_fusion.6
  337.4 5.4 multiply_reduce_fusion.19
  346.9 3.4 multiply_convert_fusion.22
  354.5 5.7 multiply_reduce_fusion.16
  360.2 2.1 fusion.305
  364.1 3.3 convolution_bitcast_fusion.10
  367.4 3.5 convolution_bitcast_fusion.11
  370.9 3.5 convolution_bitcast_fusion.9
  374.4 2.2 convolution_bitcast_fusion.8
  376.7 9.6 copy.91
  386.3 11.0 maximum_add_fusion.5
  397.2 9.6 copy.85
  406.8 9.7 copy.92
  416.6 11.0 bitcast_add_fusion
  427.6 9.7 copy.86
  437.3 10.9 convolution_add_fusion.6
  449.8 100.1 %collective-permute-done.3 = bf16[512,768]{1,0:T(8,128)(2,1)} collective-permute-done((bf16[512,768]{1,0:T(8,128)(2,1)S(1)}, bf16[512,768]{1,0:T(8,128)(2,1)}, u32[]{:S(2)}, u32[]{:S(2)}) %collective-permute-start.3) | collective-permute-done | bytes 786464 | tf_op jit(solution)/shard_map/ppermute | solution.py:17
  549.9 60.4 %conditional.10 = (f32[512,768]{1,0:T(8,128)}, f32[3072]{0:T(1024)S(1)}, f32[3072,768]{1,0:T(8,128)}, f32[2,768]{1,0:T(2,128)S(1)}, f32[2,768]{1,0:T(2,128)S(1)}, /*index=5*/f32[768,3072]{1,0:T(8,128)}) conditional(s32[]{:T(128)} %convert_element_type.338, (f32[768,3072]{1,0:T(8,128)}, f32[3072]{0:T(1024)S(1)}, f32[3072,768]{1,0:T(8,128)}, ...), branch_computations={%region_81.82_spmd, %region_82.90_spmd} | conditional | flops 9711652864 | bytes 151158960 | solution.py:499
  550.4 9.2 convert_reduce_fusion.7
  559.7 4.0 multiply_reduce_fusion.22
  566.1 2.5 add_add_fusion.12
  568.6 9.7 copy.94
  578.2 11.0 bitcast_add_fusion.2
  589.3 9.6 copy.104
  598.9 11.2 convolution_add_fusion.7
  610.3 56.1 %conditional.11 = (bf16[512,768]{1,0:T(8,128)(2,1)}, f32[2,768]{1,0:T(2,128)S(1)}, f32[2,768]{1,0:T(2,128)S(1)}, f32[4,768,768]{2,1,0:T(8,128)}) conditional(s32[]{:T(128)} %convert_element_type.338, (f32[4,768,768]{2,1,0:T(8,128)}, f32[2,768]{1,0:T(2,128)S(1)}, f32[2,768]{1,0:T(2,128)S(1)}) %tuple.158, (f32[512,768]{1,0:T(8,128)}, ...), branch_computations={%region_90.91_spmd, %region_91.98_spmd} | conditional | flops 5258874368 | bytes 155572512 | solution.py:510
  610.4 4.8 fusion.281
  619.9 4.7 multiply_reduce_fusion.25
  625.4 2.8 add_convert_fusion.17
  628.1 2.2 convolution_bitcast_fusion.14
  630.4 2.2 convolution_bitcast_fusion.15
  632.6 2.2 convolution_bitcast_fusion.13
  634.8 2.2 convolution_bitcast_fusion.12
  637.0 9.6 copy.97
  646.6 10.3 maximum_add_fusion.6
  656.9 9.6 copy.106
  668.5 41.2 %all-reduce.6 = (f32[2,12]{1,0:T(2,128)}, f32[2,4]{1,0:T(2,128)S(1)}, f32[]{:T(128)}) all-reduce(f32[2,12]{1,0:T(2,128)S(1)} %get-tuple-element.753, f32[2,4]{1,0:T(2,128)S(1)} %broadcast_select_fusion.2, f32[]{:T(128)S(6)} %select_n.40), channel_id=1, replica_groups=mesh['section'=2,'dp'=16] {'section','dp'}, use_global_device_ids=true, to_apply=%region_104.105 | all-reduce | flops 33 | bytes 264 | tf_op jit(solution)/shard_map/psum | solution.py:480
  710.9 63.8 %all-reduce.7 = (f32[1,3072]{1,0:T(1,128)}, f32[1,2,768]{2,1,0:T(2,128)}, f32[1,2,768]{2,1,0:T(2,128)}) all-reduce(f32[1,3072]{1,0:T(1,128)S(1)} %bitcast.421, f32[1,2,768]{2,1,0:T(2,128)S(1)} %bitcast.420, f32[1,2,768]{2,1,0:T(2,128)S(1)} %bitcast.419), channel_id=1, replica_groups=mesh['section'=2,'dp'=16] {'dp'}, use_global_device_ids=true, to_apply=%region_101.102 | all-reduce | flops 6144 | bytes 49152 | tf_op jit(solution)/shard_map/psum | solution.py:512
  777.2 377.2 %all-reduce.11.cloned.1.call-done = (f32[1,4,768,768]{3,2,1,0:T(8,128)}, f32[1,768,3072]{2,1,0:T(8,128)}, f32[1,3072,768]{2,1,0:T(8,128)}) async-done(((f32[1,4,768,768]{3,2,1,0:T(8,128)}, f32[1,768,3072]{2,1,0:T(8,128)}, f32[1,3072,768]{2,1,0:T(8,128)}), (f32[1,4,768,768]{3,2,1,0:T(8,128)}, f32[1,768,3072]{2,1,0:T(8,128)}, f32[1,3072,768]{2,1,0:T(8,128)})) %all-reduce.11.cloned.1.call-update) | async-done | bytes 28311568 | tf_op jit(solution)/shard_map/psum | solution.py:512
  1154.4 9.3 copy.237
  1163.7 4.8 copy.238
  1170.3 3.7 copy.239
  (302 shorter events, 59.6 us)
Async XLA Ops:
  7.2 1147.3 %all-reduce.11.cloned.1.call-start = ((), (), s32[]{:S(2)}) async-start(), calls=%async_computation | async-start | bytes 56623104 | tf_op jit(solution)/shard_map/psum | solution.py:512
  7.2 73.6 %copy-start.132 = (f32[1024]{0:T(1024)S(1)}, f32[1024]{0:T(1024)}, u32[]{:S(2)}) copy-start(f32[1024]{0:T(1024)} %param.74) | copy-start | bytes 12292
  7.2 73.6 %copy-start.134 = (f32[2,12]{1,0:T(2,128)S(1)}, f32[2,12]{1,0:T(2,128)}, u32[]{:S(2)}) copy-start(f32[2,12]{1,0:T(2,128)} %param.81) | copy-start | bytes 292
  8.6 30.0 %copy-start.4 = (f32[512,768]{1,0:T(8,128)}, f32[512,768]{1,0:T(8,128)S(1)}, u32[]{:S(2)}) copy-start(f32[512,768]{1,0:T(8,128)S(1)} %get-tuple-element.1275) | copy-start | bytes 4718596 | tf_op jit(solution)/shard_map/cond
  10.2 17.0 %copy-start.136 = (f32[512]{0:T(512)}, f32[512]{0:T(512)S(1)}, u32[]{:S(2)}) copy-start(f32[512]{0:T(512)S(1)} %get-tuple-element.1194) | copy-start | bytes 6148 | tf_op jit(solution)/shard_map/cond
  26.2 7.7 slice-start.3
  27.2 6.7 slice-start.4
  33.9 10.3 slice-start.24
  36.0 8.3 slice-start.25
  38.6 5.6 copy-start.51
  42.3 8.5 slice-start.16
  44.2 6.6 copy-start.65
  44.3 6.5 copy-start.120
  44.3 6.6 slice-start.17
  50.9 9.4 copy-start.5
  61.5 19.3 %copy-start.6 = (f32[512,768]{1,0:T(8,128)}, f32[512,768]{1,0:T(8,128)S(1)}, u32[]{:S(2)}) copy-start(f32[512,768]{1,0:T(8,128)S(1)} %get-tuple-element.719) | copy-start | bytes 4718596
  61.5 19.3 %collective-permute-start = (bf16[512,768]{1,0:T(8,128)(2,1)}, bf16[512,768]{1,0:T(8,128)(2,1)S(1)}, u32[]{:S(2)}, u32[]{:S(2)}) collective-permute-start(bf16[512,768]{1,0:T(8,128)(2,1)} %get-tuple-element.698), channel_id=1, source_target_pairs={{0,16},{1,17},{2,18},{3,19},{4,20},{5,21},{6,22},{7,23},{8,24},{9,... | collective-permute-start | bytes 2359304 | tf_op jit(solution)/shard_map/ppermute | solution.py:17
  80.8 228.2 %copy-start.133 = (f32[1024]{0:T(1024)S(1)}, f32[1024]{0:T(1024)}, u32[]{:S(2)}) copy-start(f32[1024]{0:T(1024)} %param.74) | copy-start | bytes 12292
  91.5 24.0 %copy-start.2 = (f32[512,768]{1,0:T(8,128)}, f32[512,768]{1,0:T(8,128)S(1)}, u32[]{:S(2)}) copy-start(f32[512,768]{1,0:T(8,128)S(1)} %get-tuple-element.1321) | copy-start | bytes 4718596 | tf_op jit(solution)/shard_map/cond
  92.2 20.4 %copy-start.77 = (bf16[512,768]{1,0:T(8,128)(2,1)}, bf16[512,768]{1,0:T(8,128)(2,1)S(1)}, u32[]{:S(2)}) copy-start(bf16[512,768]{1,0:T(8,128)(2,1)S(1)} %add_convert_fusion.9) | copy-start | bytes 2359300 | tf_op jit(solution)/shard_map/cond
  109.0 3.7 slice-start.7
  109.1 3.5 copy-start.87
  109.1 3.5 slice-start.8
  109.7 5.8 copy-start.79
  112.7 4.4 slice-start.28
  113.5 3.6 slice-start.29
  116.3 8.7 copy-start.8
  116.7 8.4 slice-start.20
  117.0 6.8 copy-start.63
  117.4 6.4 copy-start.122
  117.4 7.7 slice-start.21
  145.7 163.3 %copy-start.70 = (f32[512,1]{1,0:T(8,128)}, f32[512,1]{1,0:T(8,128)S(1)}, u32[]{:S(2)}) copy-start(f32[512,1]{1,0:T(8,128)S(1)} %get-tuple-element.740) | copy-start | bytes 6148
  145.7 159.2 %collective-permute-start.1 = (bf16[512,768]{1,0:T(8,128)(2,1)S(1)}, bf16[512,768]{1,0:T(8,128)(2,1)S(1)}, u32[]{:S(2)}, u32[]{:S(2)}) collective-permute-start(bf16[512,768]{1,0:T(8,128)(2,1)S(1)} %get-tuple-element.700), channel_id=1, source_target_pairs={{0,16},{1,17},{2,18},{3,19},{4,20},{5,21},{6,22},{7,23},{8,24},{9,... | collective-permute-start | bytes 2359304 | tf_op jit(solution)/shard_map/ppermute | solution.py:17
  288.1 20.9 %collective-permute-start.2 = (bf16[512,768]{1,0:T(8,128)(2,1)S(1)}, bf16[512,768]{1,0:T(8,128)(2,1)S(1)}, u32[]{:S(2)}, u32[]{:S(2)}) collective-permute-start(bf16[512,768]{1,0:T(8,128)(2,1)S(1)} %get-tuple-element.709), channel_id=1, source_target_pairs={{16,0},{17,1},{18,2},{19,3},{20,4},{21,5},{22,6},{23,7},{24,8},{25... | collective-permute-start | bytes 2359304 | tf_op jit(solution)/shard_map/ppermute | solution.py:17
  309.0 240.9 %copy-start.9 = (f32[512,768]{1,0:T(8,128)S(1)}, f32[512,768]{1,0:T(8,128)}, u32[]{:S(2)}) copy-start(f32[512,768]{1,0:T(8,128)} %get-tuple-element.732) | copy-start | bytes 4718596
  317.7 3.6 copy-start.15
  325.5 11.8 %slice-start.32 = ((s8[4718592]{0:T(1024)(128)(4,1)}), s8[4194304]{0:T(1024)(128)(4,1)S(1)}, s32[]{:S(2)}) async-start(s8[4718592]{0:T(1024)(128)(4,1)} %bitcast.465), calls=%async_computation.33 | async-start | bytes 8388608
  325.5 20.6 %slice-start.11 = ((s8[4718592]{0:T(1024)(128)(4,1)}), s8[4194304]{0:T(1024)(128)(4,1)S(1)}, s32[]{:S(2)}) async-start(s8[4718592]{0:T(1024)(128)(4,1)} %bitcast.376), calls=%async_computation.12 | async-start | bytes 8388608
  327.6 9.7 copy-start.92
  327.6 9.8 slice-start.33
  327.6 18.5 %slice-start.12 = ((s8[4718592]{0:T(1024)(128)(4,1)}), s8[524288]{0:T(1024)(128)(4,1)S(1)}, s32[]{:S(2)}) async-start(s8[4718592]{0:T(1024)(128)(4,1)} %bitcast.376), calls=%async_computation.13 | async-start | bytes 1048576
  337.3 5.5 copy-start.41
  346.1 4.3 copy-start.83
  367.4 3.5 copy-start.150
  370.9 3.5 copy-start.52
  370.9 3.5 copy-start.84
  406.8 9.8 copy-start.66
  427.6 9.7 copy-start.110
  427.6 9.7 copy-start.40
  448.5 101.4 %collective-permute-start.3 = (bf16[512,768]{1,0:T(8,128)(2,1)S(1)}, bf16[512,768]{1,0:T(8,128)(2,1)}, u32[]{:S(2)}, u32[]{:S(2)}) collective-permute-start(bf16[512,768]{1,0:T(8,128)(2,1)S(1)} %get-tuple-element.730), channel_id=1, source_target_pairs={{16,0},{17,1},{18,2},{19,3},{20,4},{21,5},{22,6},{23,7},{24,8},{25... | collective-permute-start | bytes 2359304 | tf_op jit(solution)/shard_map/ppermute | solution.py:17
  549.9 60.4 %copy-start.3 = (f32[512,768]{1,0:T(8,128)S(1)}, f32[512,768]{1,0:T(8,128)}, u32[]{:S(2)}) copy-start(f32[512,768]{1,0:T(8,128)} %get-tuple-element.742) | copy-start | bytes 4718596
  549.9 60.4 %copy-start.71 = (f32[512,1]{1,0:T(8,128)S(1)}, f32[512,1]{1,0:T(8,128)}, u32[]{:S(2)}) copy-start(f32[512,1]{1,0:T(8,128)} %copy-done.70) | copy-start | bytes 6148
  550.1 9.6 slice-start.34
  550.4 9.2 copy-start.93
  550.4 9.2 slice-start.35
  559.6 4.1 copy-start.42
  568.6 9.7 copy-start.64
  610.4 4.8 copy-start.32
  666.5 108.2 %copy-start.81 = (bf16[512,768]{1,0:T(8,128)(2,1)S(1)}, bf16[512,768]{1,0:T(8,128)(2,1)}, u32[]{:S(2)}) copy-start(bf16[512,768]{1,0:T(8,128)(2,1)} %get-tuple-element.723) | copy-start | bytes 2359300
  666.5 108.2 %copy-start.82 = (bf16[512,768]{1,0:T(8,128)(2,1)S(1)}, bf16[512,768]{1,0:T(8,128)(2,1)}, u32[]{:S(2)}) copy-start(bf16[512,768]{1,0:T(8,128)(2,1)} %get-tuple-element.1085) | copy-start | bytes 2359300
  1154.4 9.3 copy-start.33
  1154.4 14.1 %slice-start.13 = ((s8[9437184]{0:T(1024)(128)(4,1)}), s8[4194304]{0:T(1024)(128)(4,1)S(1)}, s32[]{:S(2)}) async-start(s8[9437184]{0:T(1024)(128)(4,1)} %bitcast.378), calls=%async_computation.14 | async-start | bytes 8388608
  1154.4 15.6 %slice-start.14 = ((s8[9437184]{0:T(1024)(128)(4,1)}), s8[4194304]{0:T(1024)(128)(4,1)S(1)}, s32[]{:S(2)}) async-start(s8[9437184]{0:T(1024)(128)(4,1)} %bitcast.378), calls=%async_computation.15 | async-start | bytes 8388608
  1163.7 6.6 slice-start.15
  (33 other events, 59.3 us)
Sparse Core Ops, SparseCore 0:
  666.6 487.7 all-reduce.10
where the time goes:
time: 1190 us; the launch traced here: 1180 us
  waiting for transfers between devices  515 us (43%)
  matrix products  167 us (14%)
  starting transfers between devices  146 us (12%)
  local copies, waits for them, and re-layouts  120 us (10%)
  blocking collectives  105 us (9%)
  other arithmetic  92.6 us (8%)
  loops' own time  19.8 us (2%)
  between operations  16 us (1%)
    psum x1, waiting for transfers between devices, local(): lax.psum((gradients[0], gradients[1], gradients[2], gradients[3], gradien...  377 us
    ppermute x4, starting transfers between devices, passed_along(): return lax.ppermute(block, axis, route)  146 us
    ppermute x4, waiting for transfers between devices, passed_along(): return lax.ppermute(block, axis, route)  138 us
    dot_general x14, matrix products, product_left(): lax.dot_general(left, right, (((0,), (0,)), ((), ())), preferred_element_...  76 us
    psum x1, blocking collectives, local(): lax.psum((gradients[0], gradients[1], gradients[2], gradients[3], gradien...  63.8 us
    unnamed x87, local copies, waits for them, and re-layouts  47.1 us
    dot_general x14, matrix products, product(): return jnp.dot(left, right, preferred_element_type=jnp.float32)  46.3 us
    dot_general x10, matrix products, product_right(): lax.dot_general(left, right, (((1,), (1,)), ((), ())), preferred_element_...  44.5 us
  transfers between devices with their start and end apart: 5, of which 5 were waited for; matrix products, arithmetic and copies ran while one was open for 0% of the time, Pallas kernels for 0%

commit v1 on v0

v1 whole, which is shorter than its diff:
```python
import jax
import jax.numpy as jnp
from jax import lax
from jax.sharding import Mesh, PartitionSpec as P

RADIUS = 128
EPSILON = 1e-05
NEG_FILL = -1e30
GELU_C = 0.7978845608028654


def passed_along(block, axis, distance):
    devices = range(lax.axis_size(axis))
    route = [(i - distance, i) for i in devices if i - distance in devices]
    return lax.ppermute(block, axis, route)


def low(vector):
    return vector.astype(jnp.bfloat16)


def product(left, right):
    return jnp.dot(left, right, preferred_element_type=jnp.float32)


def product_left(left, right):
    return lax.dot_general(
        left, right, (((0,), (0,)), ((), ())), preferred_element_type=jnp.float32
    )


def product_right(left, right):
    return lax.dot_general(
        left, right, (((1,), (1,)), ((), ())), preferred_element_type=jnp.float32
    )


def norm_forward(vector, gain_row, shift_row):
    center = vector - jnp.mean(vector, axis=-1, keepdims=True)
    inverse = lax.rsqrt(jnp.mean(center * center, axis=-1, keepdims=True) + EPSILON)
    return center * inverse * gain_row + shift_row


def norm_backward(vector, gain_row, grad_normed):
    center = vector - jnp.mean(vector, axis=-1, keepdims=True)
    inverse = lax.rsqrt(jnp.mean(center * center, axis=-1, keepdims=True) + EPSILON)
    normed = center * inverse
    scaled = grad_normed * gain_row
    mean_scaled = jnp.mean(scaled, axis=-1, keepdims=True)
    mean_mixed = jnp.mean(scaled * normed, axis=-1, keepdims=True)
    grad_input = inverse * (scaled - mean_scaled - normed * mean_mixed)
    return grad_input, jnp.sum(grad_normed * normed, axis=0), jnp.sum(grad_normed, axis=0)


def mlp_forward(resid, gain_row, shift_row, up_matrix, bias_row, down_matrix):
    normed_low = low(norm_forward(resid, gain_row, shift_row))
    pre_act = product(normed_low, up_matrix) + bias_row
    curve = jnp.tanh(GELU_C * (pre_act + 0.044715 * pre_act * pre_act * pre_act))
    active_low = low(0.5 * pre_act * (1.0 + curve))
    slope = 0.5 * (1.0 + curve) + 0.5 * pre_act * (1.0 - curve * curve) * GELU_C * (
        1.0 + 3.0 * 0.044715 * pre_act * pre_act
    )
    branch = product(active_low, down_matrix)
    return branch, (resid, normed_low, active_low, low(slope))


def mlp_backward(kept, grad_low, grad_resid, gain_row, up_matrix, down_matrix):
    resid, normed_low, active_low, slope = kept
    grad_active = product_right(grad_low, down_matrix)
    grad_pre = low(slope.astype(jnp.float32) * grad_active)
    grad_bias = jnp.sum(grad_pre.astype(jnp.float32), axis=0)
    grad_normed = product_right(grad_pre, up_matrix)
    grad_input, grad_gain, grad_shift = norm_backward(resid, gain_row, grad_normed)
    return grad_resid + grad_input, grad_pre, grad_bias, grad_gain, grad_shift


def adjacency_rows(neighbours, counts, total_rows):
    slot_ids = jnp.arange(neighbours.shape[1])
    index_rows = jnp.where(slot_ids[None, :] < counts[:, None], neighbours, -1)
    columns = jnp.arange(total_rows)
    matches = index_rows[:, :, None] == columns[None, None, :]
    return jnp.sum(matches, axis=1, dtype=jnp.int32).astype(jnp.bfloat16)


def graph_forward(inputs, neighbours, counts, squares, gain_row, shift_row):
    normed_low = low(norm_forward(inputs, gain_row, shift_row))
    adjacency = adjacency_rows(neighbours, counts, inputs.shape[0])
    divisor = counts.astype(jnp.float32)[:, None]
    near = low(product(adjacency, normed_low) / divisor)
    pre = product(normed_low, squares[0]) + product(near, squares[1])
    sigma = jax.nn.sigmoid(product(near, squares[2]))
    mixed = low(pre * sigma)
    branch = product(mixed, squares[3])
    return branch, (inputs, normed_low, adjacency, divisor, near, pre, sigma, mixed)


def graph_backward(kept, grad_resid, squares, gain_row):
    inputs, normed_low, adjacency, divisor, near, pre, sigma, mixed = kept
    grad_low = low(grad_resid)
    grad_mixed = product_right(grad_low, squares[3])
    grad_pre = low(sigma * grad_mixed)
    grad_gate = low(pre * sigma * (1.0 - sigma) * grad_mixed)
    grad_mean = product_right(grad_pre, squares[1]) + product_right(grad_gate, squares[2])
    grad_total = low(grad_mean / divisor)
    grad_normed = product_right(grad_pre, squares[0]) + product_left(adjacency, grad_total)
    grad_input, grad_gain, grad_shift = norm_backward(inputs, gain_row, grad_normed)
    lefts = (normed_low, near, near, mixed)
    rights = (grad_pre, grad_pre, grad_gate, grad_low)
    return grad_resid + grad_input, lefts, rights, grad_gain, grad_shift


def attention_terms(length, coords, rich_terms):
    rows = coords.shape[0]
    position = jnp.arange(rows)
    nearby = jnp.abs(position[:, None] - position[None, :]) <= RADIUS
    living = (position < length)[None, :] | (position[None, :] == position[:, None])
    offset = coords[:, None] - coords[None, :]
    return nearby & living, jnp.log1p(jnp.abs(offset)), jnp.tanh(-offset)


def attention_forward(inputs, terms, squares, gain_row, shift_row, rich_terms):
    rows, width = inputs.shape
    heads = rich_terms.shape[1]
    allowed, spread, order = terms
    scale = (width // heads) ** (-0.5)
    normed_low = low(norm_forward(inputs, gain_row, shift_row))
    queries, keys, values = (
        low(product(normed_low, squares[c])).reshape(rows, heads, -1) for c in range(3)
    )
    raw = jnp.einsum("qhd,khd->hqk", queries, keys, preferred_element_type=jnp.float32)
    bias = rich_terms[0][:, None, None] * spread + rich_terms[1][:, None, None] * order
    scores = jnp.where(allowed[None], raw * scale + bias, NEG_FILL)
    weights = jnp.exp(scores - jnp.max(scores, axis=-1, keepdims=True))
    probs = weights / jnp.sum(weights, axis=-1, keepdims=True)
    context = jnp.einsum("hqk,khd->qhd", low(probs), values, preferred_element_type=jnp.float32)
    context = low(context.reshape(rows, width))
    branch = product(context, squares[3])
    return branch, (inputs, normed_low, queries, keys, values, probs, context)


def attention_backward(kept, terms, grad_resid, squares, gain_row, rich_terms):
    inputs, normed_low, queries, keys, values, probs, context = kept
    rows, width = inputs.shape
    heads = rich_terms.shape[1]
    allowed, spread, order = terms
    scale = (width // heads) ** (-0.5)
    grad_low = low(grad_resid)
    grad_context = low(product_right(grad_low, squares[3])).reshape(rows, heads, -1)
    grad_probs = jnp.einsum("qhd,khd->hqk", grad_context, values, preferred_element_type=jnp.float32)
    inner = jnp.sum(probs * grad_probs, axis=-1, keepdims=True)
    grad_scores = probs * (grad_probs - inner)
    grad_rich = jnp.stack(
        [
            jnp.sum(grad_scores * spread[None], axis=(1, 2)),
            jnp.sum(grad_scores * order[None], axis=(1, 2)),
        ]
    )
    grad_raw = low(grad_scores * scale)
    grad_q = jnp.einsum("hqk,khd->qhd", grad_raw, keys, preferred_element_type=jnp.float32)
    grad_k = jnp.einsum("hqk,qhd->khd", grad_raw, queries, preferred_element_type=jnp.float32)
    grad_v = jnp.einsum("hqk,qhd->khd", low(probs), grad_context, preferred_element_type=jnp.float32)
    grad_q, grad_k, grad_v = (low(item).reshape(rows, width) for item in (grad_q, grad_k, grad_v))
    grad_normed = (
        product_right(grad_q, squares[0])
        + product_right(grad_k, squares[1])
        + product_right(grad_v, squares[2])
    )
    grad_input, grad_gain, grad_shift = norm_backward(inputs, gain_row, grad_normed)
    lefts = (normed_low, normed_low, normed_low, context)
    rights = (grad_q, grad_k, grad_v, grad_low)
    return grad_resid + grad_input, lefts, rights, grad_gain, grad_shift, grad_rich


def live_squares(length, quantities):
    live_rows = (jnp.arange(quantities[0].shape[0]) < length).astype(jnp.float32)[:, None]
    return jnp.stack([jnp.sum(live_rows * item * item) for item in quantities])


def exchanged_sum(block, axis):
    size = lax.axis_size(axis)
    step = 1
    while step < size:
        route = [(i, i ^ step) for i in range(size)]
        block = block + lax.ppermute(block, axis, route)
        step *= 2
    return block


def summed_over_documents(block):
    core = lax.axis_index("core")
    swap = [(0, 1), (1, 0)]
    half = block.shape[0] // 2
    own = lax.dynamic_slice_in_dim(block, core * half, half, 0)
    other = lax.dynamic_slice_in_dim(block, (1 - core) * half, half, 0)
    part = own + lax.ppermute(other, "core", swap)
    part = lax.psum(part, "chip")
    other = lax.ppermute(part, "core", swap)
    return jnp.concatenate(
        [jnp.where(core == 0, part, other), jnp.where(core == 0, other, part)], axis=0
    )


def local(
    boundary,
    lengths,
    neighbours,
    counts,
    coords,
    square_weights,
    up_weight,
    down_weight,
    up_bias,
    norm_gain,
    norm_bias,
    rich_terms,
):
    first = lax.axis_index("section") == 0
    documents = lengths.shape[0]
    rows = boundary.shape[1] // documents
    width = boundary.shape[2]
    hidden = up_weight.shape[2]
    squares = square_weights[0]
    up, down, bias = up_weight[0], down_weight[0], up_bias[0]
    gains, shifts = norm_gain[0], norm_bias[0]

    def rows_of(array, doc):
        return lax.slice_in_dim(array, doc * rows, (doc + 1) * rows)

    inputs = [rows_of(boundary[0], doc) for doc in range(documents)]

    def layer_one_forward(doc, source):
        x = source.astype(jnp.float32)
        branch_a, graph_kept = graph_forward(
            x, rows_of(neighbours, doc), rows_of(counts, doc), squares, gains[0], shifts[0]
        )
        resid_a = x + branch_a
        branch_f, mlp_kept = mlp_forward(resid_a, gains[1], shifts[1], up, bias, down)
        resid_b = resid_a + branch_f
        stats = live_squares(lengths[doc], (branch_a, resid_a, branch_f, resid_b))
        return low(resid_b), graph_kept, mlp_kept, stats

    def layer_two(doc, mid, cotangent):
        x = mid.astype(jnp.float32)
        terms = attention_terms(lengths[doc], rows_of(coords, doc), rich_terms)
        branch_c, attend_kept = attention_forward(x, terms, squares, gains[0], shifts[0], rich_terms)
        resid_c = x + branch_c
        branch_f, mlp_kept = mlp_forward(resid_c, gains[1], shifts[1], up, bias, down)
        resid_d = resid_c + branch_f
        stats = live_squares(lengths[doc], (branch_c, resid_c, branch_f, resid_d))
        grad_c, grad_pre, grad_bias, gain_f, shift_f = mlp_backward(
            mlp_kept, cotangent, cotangent.astype(jnp.float32), gains[1], up, down
        )
        grad_b, lefts, rights, gain_c, shift_c, grad_rich = attention_backward(
            attend_kept, terms, grad_c, squares, gains[0], rich_terms
        )
        small = jnp.concatenate([grad_bias, gain_c, gain_f, shift_c, shift_f])
        operands = (mlp_kept[2], mlp_kept[1], grad_pre, lefts, rights)
        return low(grad_b), low(resid_d), operands, small, stats, grad_rich

    def layer_one_backward(graph_kept, mlp_kept, grad_mid):
        grad_a, grad_pre, grad_bias, gain_f, shift_f = mlp_backward(
            mlp_kept, grad_mid, grad_mid.astype(jnp.float32), gains[1], up, down
        )
        grad_x, lefts, rights, gain_a, shift_a = graph_backward(graph_kept, grad_a, squares, gains[0])
        small = jnp.concatenate([grad_bias, gain_a, gain_f, shift_a, shift_f])
        operands = (mlp_kept[2], mlp_kept[1], grad_pre, lefts, rights)
        return low(grad_x), operands, small

    kept_one, arrived, stats_one = [], [], 0.0
    for doc in range(documents):
        source = inputs[doc]
        if doc:
            source, _ = lax.optimization_barrier((source, sent))
        sent, graph_kept, mlp_kept, stats = layer_one_forward(doc, source)
        kept_one.append((graph_kept, mlp_kept))
        stats_one = stats_one + stats
        arrived.append(passed_along(sent, "section", 1))

    back, out_two, small_two, stats_two, rich_two, operands_two = [], [], 0.0, 0.0, 0.0, []
    for doc in range(documents):
        grad_mid, result, operands, small, stats, rich = layer_two(doc, arrived[doc], inputs[doc])
        operands_two.append(operands)
        out_two.append(result)
        small_two, stats_two, rich_two = small_two + small, stats_two + stats, rich_two + rich
        back.append(passed_along(grad_mid, "section", -1))
        last_sent = grad_mid

    small_one, out_one, operands_one = 0.0, [], []
    for doc in range(documents):
        grad_mid = back[doc]
        if doc < documents - 1:
            grad_mid, _ = lax.optimization_barrier((grad_mid, last_sent))
        result, operands, small = layer_one_backward(*kept_one[doc], grad_mid)
        out_one.append(result)
        small_one = small_one + small
        operands_one.append(operands)

    def both(pick_one, pick_two):
        one = jnp.concatenate([pick_one(doc) for doc in range(documents)], axis=0)
        two = jnp.concatenate([pick_two(doc) for doc in range(documents)], axis=0)
        return jnp.where(first, one, two)

    def side(index):
        return both(lambda d: operands_one[d][index], lambda d: operands_two[d][index])

    grad_down = low(product_left(side(0), both(lambda d: back[d], lambda d: inputs[d])))
    grad_up = low(product_left(side(1), side(2)))
    grad_squares = jnp.concatenate(
        [
            low(
                product_left(
                    both(lambda d: operands_one[d][3][c], lambda d: operands_two[d][3][c]),
                    both(lambda d: operands_one[d][4][c], lambda d: operands_two[d][4][c]),
                )
            )
            for c in range(4)
        ],
        axis=0,
    )
    down_total = summed_over_documents(grad_down).astype(jnp.float32)
    up_total = summed_over_documents(grad_up).astype(jnp.float32)
    square_total = summed_over_documents(grad_squares).astype(jnp.float32)

    heads = rich_terms.shape[1]
    small = jnp.where(first, small_one, small_two)
    count = jnp.sum(lengths).astype(jnp.float32)[None]
    shared = jnp.concatenate(
        [
            jnp.where(first, stats_one, 0.0),
            jnp.where(first, 0.0, stats_two),
            jnp.where(first, 0.0, rich_two).reshape(-1),
            jnp.where(first, 0.0, count),
        ]
    )
    packed = jnp.concatenate([small, shared])
    packed = jnp.pad(packed, (0, -packed.shape[0] % 1024))
    packed = exchanged_sum(exchanged_sum(packed, "core"), "chip")
    crossed = lax.ppermute(packed, "section", [(0, 1), (1, 0)])
    start = small.shape[0]
    shared = packed[start : start + shared.shape[0]] + crossed[start : start + shared.shape[0]]
    rms = jnp.sqrt(shared[:8].reshape(2, 4) / (shared[8 + 2 * heads] * width))
    rich_total = shared[8 : 8 + 2 * heads].reshape(2, heads)
    boundary_out = jnp.concatenate(
        [jnp.where(first, out_one[doc], out_two[doc]) for doc in range(documents)], axis=0
    )[None]
    return (
        boundary_out,
        square_total.reshape(1, 4, width, width),
        up_total[None],
        down_total[None],
        packed[:hidden][None],
        packed[hidden : hidden + 2 * width].reshape(1, 2, width),
        packed[hidden + 2 * width : hidden + 4 * width].reshape(1, 2, width),
        rich_total,
        rms,
    )


def solution(mesh):
    sections, dp = mesh.devices.shape
    split = Mesh(mesh.devices.reshape(sections, dp // 2, 2), ("section", "chip", "core"))
    data = ("chip", "core")
    in_specs = (
        P("section", data, None),
        P(data),
        P(data, None),
        P(data),
        P(data),
        P("section", None, None, None),
        P("section", None, None),
        P("section", None, None),
        P("section", None),
        P("section", None, None),
        P("section", None, None),
        P(),
    )
    out_specs = (
        P("section", data, None),
        P("section", None, None, None),
        P("section", None, None),
        P("section", None, None),
        P("section", None),
        P("section", None, None),
        P("section", None, None),
        P(),
        P(),
    )
    return jax.shard_map(local, mesh=split, in_specs=in_specs, out_specs=out_specs, check_vma=False)
```

time: 1190 us -> 816 us (0.69)
  waiting for transfers between devices: 515 us -> 234 us
  matrix products: 167 us -> 341 us
  starting transfers between devices: 146 us -> 15.7 us
  blocking collectives: 105 us -> 0 us
  local copies, waits for them, and re-layouts: 120 us -> 57.9 us
  other arithmetic: 92.6 us -> 145 us
  loops' own time: 19.8 us -> 0 us
    psum x1, waiting for transfers between devices: 377 us -> 205 us  [summed_over_documents(): part = lax.psum(part, 'chip')]
    ppermute x4, starting transfers between devices: 146 us -> 10.2 us  [passed_along(): return lax.ppermute(block, axis, route)]
    ppermute x4, waiting for transfers between devices: 138 us -> 20.2 us  [passed_along(): return lax.ppermute(block, axis, route)]
    psum x2 -> x0, blocking collectives: 105 us -> none  [the longest x1 63.8 us: local(): lax.psum((gradients[0], gradients[1], gradients[2], gradients[3], gradien...]
    dot_general x0 -> x10, matrix products: none -> 88.1 us  [the longest x2 26.3 us: attention_forward(): jnp.einsum('qhd,khd->hqk', queries, keys, preferred_element_type=jnp.floa...]
    dot_general x10 -> x22, matrix products: 44.5 us -> 94.1 us  [product_right(): lax.dot_general(left, right, (((1,), (1,)), ((), ())), preferred_element_...]
    dot_general x14 -> x8, matrix products: 76 us -> 35.5 us  [product_left(): lax.dot_general(left, right, (((0,), (0,)), ((), ())), preferred_element_...]
    another operation x14 -> x0, local copies, waits for them, and re-layouts: 40.3 us -> none
  transfers between devices with their start and end apart: 5 -> 16, of which waited for: 5 -> 7; matrix products, arithmetic and copies ran while one was open for 0% -> 18% of each run, Pallas kernels for 0% -> 0%
where the time goes in v1:
time: 816 us; the launch traced here: 811 us
  matrix products  341 us (42%)
  waiting for transfers between devices  234 us (29%)
  other arithmetic  145 us (18%)
  local copies, waits for them, and re-layouts  57.9 us (7%)
  between operations  18 us (2%)
  starting transfers between devices  15.7 us (2%)
    psum x1, waiting for transfers between devices, summed_over_documents(): part = lax.psum(part, 'chip')  205 us
    dot_general x22, matrix products, product_right(): lax.dot_general(left, right, (((1,), (1,)), ((), ())), preferred_element_...  94.1 us
    dot_general x26, matrix products, product(): return jnp.dot(left, right, preferred_element_type=jnp.float32)  84.4 us
    sub x2, matrix products, attention_backward(): grad_scores = probs * (grad_probs - inner)  39.1 us
    dot_general x8, matrix products, product_left(): lax.dot_general(left, right, (((0,), (0,)), ((), ())), preferred_element_...  35.5 us
    reduce_sum x2, other arithmetic, adjacency_rows(): return jnp.sum(matches, axis=1, dtype=jnp.int32).astype(jnp.bfloat16)  32.3 us
    sub x2, other arithmetic, attention_forward(): weights = jnp.exp(scores - jnp.max(scores, axis=-1, keepdims=True))  30.5 us
    dot_general x2, matrix products, attention_forward(): jnp.einsum('qhd,khd->hqk', queries, keys, preferred_element_type=jnp.floa...  26.3 us
  transfers between devices with their start and end apart: 16, of which 7 were waited for; matrix products, arithmetic and copies ran while one was open for 18% of the time, Pallas kernels for 0%

profile of v1, /device:TPU:0, one launch (start us, length us, event | category | flops | bytes accessed | tf_op | source)
XLA Modules:
  0.0 811.4 jit_solution(16323718098009423567)
XLA Ops:
  13.7 15.6 %convert_reduce_fusion.1 = s32[512,512]{1,0:T(8,128)S(1)} fusion(s32[512,40]{1,0:T(8,128)S(1)} %copy.81), kind=kLoop, calls=%fused_computation.6 | loop fusion | flops 31195136 | bytes 1130496 | tf_op jit(solution)/shard_map/reduce_sum | solution.py:82
  39.7 5.8 multiply_convert_fusion.9
  45.5 4.0 add_convert_fusion.6
  49.5 5.3 collective-permute-start
  66.0 16.7 %convert_reduce_fusion = s32[512,512]{1,0:T(8,128)} fusion(s32[512,40]{1,0:T(8,128)S(1)} %copy.90), kind=kLoop, calls=%fused_computation.4 | loop fusion | flops 31195136 | bytes 1130496 | tf_op jit(solution)/shard_map/reduce_sum | solution.py:82
  84.7 3.2 convolution_convert_fusion.5
  88.0 2.9 convolution_convert_fusion.6
  90.9 2.9 convolution_convert_fusion.7
  103.3 2.8 add_divide_fusion
  111.6 16.0 %add_select_fusion.1 = f32[12,512,512]{1,2,0:T(8,128)} fusion(f32[512,512]{0,1:T(8,128)S(1)} %copy-done.58, f32[12]{0:T(128)S(1)} %get-tuple-element.149, f32[512,512]{0,1:T(8,128)S(1)} %copy-done.56, f32[12]{0:T(128)S(1)} %get-tuple-element.148, pred[512,512]{0,1:T(8,128)(4,1)S(1)} %copy-done.101, bf16[512,12,64]{0,2,1:T(8,128)(2,1)S(1)} %bitcast.352, ...), kind=kOutput, calls=%fused_computation.23 | convolution fusion | flops 421527552 | bytes 16515168 | tf_op jit(solution)/shard_map/qhd,khd->hqk/dot_general | solution.py:130
  127.6 15.2 %fusion.365 = (f32[12,512]{1,0:T(8,128)S(1)}, f32[12,512,512]{1,2,0:T(8,128)}) fusion(f32[12,512,512]{1,2,0:T(8,128)} %add_select_fusion.1), kind=kOutput, calls=%fused_computation.586 | output fusion | flops 6291967 | bytes 25190400 | tf_op jit(solution)/shard_map/sub | solution.py:133
  142.8 12.2 %fusion.219 = bf16[12,64,512]{2,1,0:T(8,128)(2,1)} fusion(bf16[512,12,64]{0,2,1:T(8,128)(2,1)S(1)} %bitcast.373, f32[12,512]{1,0:T(8,128)S(1)} %get-tuple-element.162, f32[12,512,512]{1,2,0:T(8,128)} %add_select_fusion.1), kind=kOutput, calls=%fused_computation.361 | convolution fusion | flops 412490240 | bytes 14180352 | tf_op jit(solution)/shard_map/hqk,khd->qhd/dot_general | solution.py:135
  155.0 3.8 fusion.353
  159.8 5.6 fusion.70
  165.4 7.5 multiply_convert_fusion.4
  172.9 4.1 add_convert_fusion.5
  179.1 8.1 %convert_reduce_fusion.3 = (f32[3072]{0:T(1024)}, bf16[512,3072]{1,0:T(8,128)(2,1)}) fusion(bf16[1,3072,768]{2,1,0:T(8,128)(2,1)S(1)} %bitcast.390, bf16[1,1024,768]{2,1,0:T(8,128)(2,1)S(1)} %copy-done.4, f32[512,3072]{1,0:T(8,128)S(1)} %get-tuple-element.165, f32[3072]{0:T(1024)S(1)} %bitcast.395), kind=kOutput, calls=%fused_computation.71 | convolution fusion | flops 2453664768 | bytes 14966784 | tf_op jit(solution)/shard_map/dot_general | solution.py:33
  189.6 7.3 fusion.72
  213.4 10.3 %add_select_fusion = f32[12,512,512]{1,2,0:T(8,128)} fusion(f32[512,512]{0,1:T(8,128)} %get-tuple-element.147, f32[512,512]{0,1:T(8,128)} %get-tuple-element.146, f32[12]{0:T(128)S(1)} %get-tuple-element.149, f32[12]{0:T(128)S(1)} %get-tuple-element.148, pred[512,512]{0,1:T(8,128)(4,1)S(1)} %copy-done.100, bf16[512,12,64]{0,2,1:T(8,128)(2,1)} %bitcast.356, ...), kind=kOutput, calls=%fused_computation.17 | convolution fusion | flops 421527552 | bytes 16515168 | tf_op jit(solution)/shard_map/qhd,khd->hqk/dot_general | solution.py:130
  223.6 15.4 %fusion.366 = (f32[12,512]{1,0:T(8,128)S(1)}, f32[12,512,512]{1,2,0:T(8,128)}) fusion(f32[12,512,512]{1,2,0:T(8,128)} %add_select_fusion), kind=kOutput, calls=%fused_computation.587 | output fusion | flops 6291967 | bytes 25190400 | tf_op jit(solution)/shard_map/sub | solution.py:133
  239.0 12.4 %fusion.225 = bf16[12,64,512]{2,1,0:T(8,128)(2,1)} fusion(bf16[512,12,64]{0,2,1:T(8,128)(2,1)} %bitcast.374, f32[12,512]{1,0:T(8,128)S(1)} %get-tuple-element.168, f32[12,512,512]{1,2,0:T(8,128)} %add_select_fusion), kind=kOutput, calls=%fused_computation.363 | convolution fusion | flops 412490240 | bytes 14180352 | tf_op jit(solution)/shard_map/hqk,khd->qhd/dot_general | solution.py:135
  253.7 3.9 fusion.356
  258.0 8.8 %fusion.159 = (f32[]{:T(128)}, f32[]{:T(128)}, f32[]{:T(128)}, f32[512]{0:T(512)S(1)}, f32[512]{0:T(512)S(1)}, /*index=5*/f32[768]{0:T(1024)}, f32[768]{0:T(1024...) fusion(f32[512,768]{1,0:T(8,128)S(1)} %get-tuple-element.89, f32[512]{0:T(512)S(1)} %fusion.349, ...), kind=kOutput, calls=%fused_computation.239 | convolution fusion | flops 2426533376 | bytes 16541712 | tf_op jit(solution)/shard_map/dot_general | solution.py:23
  266.8 4.0 multiply_convert_fusion.2
  270.9 7.0 convert_reduce_fusion.2
  280.6 5.3 fusion.163
  291.8 11.1 %fusion.222 = bf16[12,64,512]{2,1,0:T(8,128)(2,1)} fusion(bf16[512,12,64]{0,2,1:T(8,128)(2,1)S(1)} %bitcast.378, f32[12,512]{1,0:T(8,128)S(1)} %get-tuple-element.162, f32[12,512,512]{1,2,0:T(8,128)} %add_select_fusion.1), kind=kOutput, calls=%fused_computation.362 | convolution fusion | flops 412490240 | bytes 14180352 | tf_op jit(solution)/shard_map/hqk,qhd->khd/dot_general | solution.py:161
  302.9 20.2 %multiply_reduce_fusion.3 = (f32[12]{0:T(128)}, f32[12]{0:T(128)}, f32[12,512,512]{1,2,0:T(8,128)}) fusion(f32[512,512]{0,1:T(8,128)S(1)} %copy-done.57, f32[512,512]{0,1:T(8,128)S(1)} %copy-done.59, bf16[512,12,64]{0,2,1:T(8,128)(2,1)} %bitcast.379, bf16[512,12,64]{0,2,1:T(8,128)(2,1)} %bitcast.372, f32[12,512,512]{1,2,0:T(8,128)} %get-tuple-element.163, ...), kind=kOutput, calls=%fused_computation.11 | convolution fusion | flops 833624576 | bytes 28860512 | tf_op jit(solution)/shard_map/sub | solution.py:151
  323.2 6.7 fusion.218
  333.8 3.3 fusion.276
  338.3 3.3 fusion.263
  343.9 10.2 %fusion.228 = bf16[12,64,512]{2,1,0:T(8,128)(2,1)S(1)} fusion(bf16[512,12,64]{0,2,1:T(8,128)(2,1)S(1)} %bitcast.380, f32[12,512]{1,0:T(8,128)S(1)} %get-tuple-element.168, f32[12,512,512]{1,2,0:T(8,128)} %add_select_fusion), kind=kOutput, calls=%fused_computation.364 | convolution fusion | flops 412490240 | bytes 14180352 | tf_op jit(solution)/shard_map/hqk,qhd->khd/dot_general | solution.py:161
  354.2 18.9 %multiply_reduce_fusion.1 = (f32[12]{0:T(128)S(1)}, f32[12]{0:T(128)S(1)}, f32[12,512,512]{1,2,0:T(8,128)}) fusion(f32[512,512]{0,1:T(8,128)S(1)} %copy-done.55, f32[512,512]{0,1:T(8,128)} %get-tuple-element.147, bf16[512,12,64]{0,2,1:T(8,128)(2,1)} %bitcast.381, bf16[512,12,64]{0,2,1:T(8,128)(2,1)S(1)} %bitcast.375, ...), kind=kOutput, calls=%fused_computation.9 | convolution fusion | flops 833624576 | bytes 28860512 | tf_op jit(solution)/shard_map/sub | solution.py:151
  373.1 6.8 fusion.216
  383.8 3.3 fusion.271
  388.3 3.3 fusion.259
  392.8 4.7 fusion.148
  399.2 2.8 add_add_fusion
  402.0 2.7 fusion.130
  409.2 18.0 %collective-permute-done.1 = bf16[512,768]{1,0:T(8,128)(2,1)S(1)} collective-permute-done((bf16[512,768]{1,0:T(8,128)(2,1)S(1)}, bf16[512,768]{1,0:T(8,128)(2,1)S(1)}, u32[]{:S(2)}, u32[]{:S(2)}) %collective-permute-start.1) | collective-permute-done | bytes 786464 | tf_op jit(solution)/shard_map/ppermute | solution.py:15
  427.3 9.0 %convert_reduce_fusion.5 = (f32[3072]{0:T(1024)S(1)}, bf16[512,3072]{1,0:T(8,128)(2,1)S(1)}) fusion(bf16[512,768]{1,0:T(8,128)(2,1)S(1)} %collective-permute-done.1, bf16[1,3072,768]{2,1,0:T(8,128)(2,1)} %param.19, f32[512,3072]{1,0:T(8,128)} %get-tuple-element.156, f32[3072]{0:T(1024)S(1)} %bitcast.398), kind=kOutput, calls=%fused_computation.73 | convolution fusion | flops 2453664768 | bytes 14966784 | tf_op jit(solution)/shard_map/dot_general | solution.py:33
  436.4 3.9 fusion.151
  442.6 8.8 %convert_reduce_fusion.4 = (f32[3072]{0:T(1024)S(1)}, bf16[512,3072]{1,0:T(8,128)(2,1)}) fusion(bf16[512,768]{1,0:T(8,128)(2,1)S(1)} %collective-permute-done.3, bf16[1,3072,768]{2,1,0:T(8,128)(2,1)} %param.19, f32[512,3072]{1,0:T(8,128)S(1)} %bitcast.341, f32[3072]{0:T(1024)S(1)} %bitcast.399), kind=kOutput, calls=%fused_computation.72 | convolution fusion | flops 2453664768 | bytes 14966784 | tf_op jit(solution)/shard_map/dot_general | solution.py:33
  451.5 7.6 fusion.351
  478.6 8.1 %fusion.48 = bf16[3072,768]{1,0:T(8,128)(2,1)S(1)} fusion(bf16[512,3072]{1,0:T(8,128)(2,1)} %copy-done.156, bf16[512,3072]{1,0:T(8,128)(2,1)} %copy-done.154, bf16[512,3072]{1,0:T(8,128)(2,1)} %copy-done.151, bf16[512,3072]{1,0:T(8,128)(2,1)S(1)} %copy-done.148, pred[]{:T(512)S(6)} %eq.27, bf16[512,768]{1,0:T(8,128)(2,1)S(1)} %collective-permute-done.3, ...), kind=kOutput, calls=%fused_computation.86 | convolution fusion | flops 4869586944 | bytes 20447232 | tf_op jit(solution)/shard_map/dot_general | solution.py:27
  490.8 8.1 %fusion.49 = bf16[768,3072]{1,0:T(8,128)(2,1)S(1)} fusion(bf16[512,3072]{1,0:T(8,128)(2,1)} %get-tuple-element.186, bf16[512,3072]{1,0:T(8,128)(2,1)S(1)} %copy-done.150, bf16[512,3072]{1,0:T(8,128)(2,1)} %copy-done.152, bf16[512,3072]{1,0:T(8,128)(2,1)} %get-tuple-element.180, pred[]{:T(512)S(6)} %eq.27, bf16[512,768]{1,0:T(8,128)(2,1)S(1)} %copy-done.30, ...), kind=kOutput, calls=%fused_computation.87 | convolution fusion | flops 4869586944 | bytes 20447232 | tf_op jit(solution)/shard_map/dot_general | solution.py:27
  501.9 4.4 dynamic-slice_add_fusion
  506.3 3.8 dynamic-slice_add_fusion.2
  510.1 4.0 dynamic-slice_add_fusion.1
  516.8 3.2 fusion.255
  520.1 3.4 fusion.267
  523.5 3.3 fusion.257
  526.8 3.3 fusion.269
  530.1 6.0 convolution_add_fusion
  536.1 7.2 fusion.121
  544.8 205.2 %all-reduce.4.cloned.1.call-done = (bf16[1536,768]{1,0:T(8,128)(2,1)}, bf16[384,3072]{1,0:T(8,128)(2,1)}, bf16[1536,768]{1,0:T(8,128)(2,1)}) async-done(((bf16[1536,768]{1,0:T(8,128)(2,1)}, bf16[384,3072]{1,0:T(8,128)(2,1)}, bf16[1536,768]{1,0:T(8,128)(2,1)}), (bf16[1536,768]{1,0:T(8,128)(2,1)}, bf16[384,3072]{1,0:T(8,128)(2,1)}, bf16[1536,768]{1,0:T(8,128)(2,1)})) %all-reduce.4.cloned.1.call-update) | async-done | bytes 7077904 | tf_op jit(solution)/shard_map/psum | solution.py:196
  750.0 9.9 %broadcast_select_fusion.2 = (f32[4]{0:T(128)S(1)}, f32[4]{0:T(128)S(1)}) fusion(pred[]{:T(512)S(6)} %eq.27, f32[1]{0:T(128)} %bitcast.63, f32[1]{0:T(128)} %bitcast.62, f32[1]{0:T(128)} %bitcast.61, f32[1]{0:T(128)} %bitcast.60, f32[1]{0:T(128)} %bitcast.67, f32[1]{0:T(128)} %bitcast.66, f32[1]{0:T(128)} %bitcast.65, f32[1]{0:T(128)} %bitcast.64, ...), kind=kLoop, calls=%fused_computation.549 | loop fusion | flops 64 | bytes 97 | tf_op jit(solution)/shard_map/jit(_where)/select_n | solution.py:330
  761.2 3.6 fusion.291
  769.9 2.9 collective-permute-done.12
  784.0 2.7 broadcast_select_fusion.1
  787.2 4.6 convert.1
  791.8 2.7 select_bitcast_fusion.1
  794.5 4.5 maximum_convert_fusion.1
  799.3 5.0 maximum_convert_fusion
  (563 shorter events, 147.0 us)
Async XLA Ops:
  7.2 22.1 %copy-start.4 = (bf16[1,1024,768]{2,1,0:T(8,128)(2,1)S(1)}, bf16[1,1024,768]{2,1,0:T(8,128)(2,1)}, u32[]{:S(2)}) copy-start(bf16[1,1024,768]{2,1,0:T(8,128)(2,1)} %param.12) | copy-start | bytes 4718596
  7.2 742.8 %all-reduce.4.cloned.1.call-start = ((), (), s32[]{:S(2)}) async-start(), calls=%async_computation | async-start | bytes 14155776 | tf_op jit(solution)/shard_map/psum | solution.py:196
  8.7 23.5 %copy-start.106 = (f32[512]{0:T(512)}, f32[512]{0:T(512)S(1)}, u32[]{:S(2)}) copy-start(f32[512]{0:T(512)S(1)} %broadcast_multiply_fusion.23) | copy-start | bytes 6148
  10.2 22.0 %copy-start.116 = (f32[512]{0:T(512)}, f32[512]{0:T(512)S(1)}, u32[]{:S(2)}) copy-start(f32[512]{0:T(512)S(1)} %add_rsqrt_fusion.7) | copy-start | bytes 6148
  11.0 21.3 %copy-start.141 = (f32[512]{0:T(512)}, f32[512]{0:T(512)S(1)}, u32[]{:S(2)}) copy-start(f32[512]{0:T(512)S(1)} %get-tuple-element.141) | copy-start | bytes 6148
  11.0 91.7 %copy-start.142 = (f32[512]{0:T(512)}, f32[512]{0:T(512)S(1)}, u32[]{:S(2)}) copy-start(f32[512]{0:T(512)S(1)} %get-tuple-element.142) | copy-start | bytes 6148
  11.8 188.0 %copy-start.102 = (f32[768]{0:T(1024)}, f32[768]{0:T(1024)S(1)}, u32[]{:S(2)}) copy-start(f32[768]{0:T(1024)S(1)} %get-tuple-element.74) | copy-start | bytes 9220
  13.6 19.2 %slice-start = ((s8[4718592]{0:T(1024)(128)(4,1)}), s8[524288]{0:T(1024)(128)(4,1)S(1)}, s32[]{:S(2)}) async-start(s8[4718592]{0:T(1024)(128)(4,1)} %bitcast.331), calls=%async_computation.1 | async-start | bytes 1048576
  49.5 33.2 %collective-permute-start = (bf16[512,768]{1,0:T(8,128)(2,1)}, bf16[512,768]{1,0:T(8,128)(2,1)S(1)}, u32[]{:S(2)}, u32[]{:S(2)}) collective-permute-start(bf16[512,768]{1,0:T(8,128)(2,1)} %get-tuple-element.157), channel_id=1, source_target_pairs={{0,16},{1,17},{2,18},{3,19},{4,20},{5,21},{6,22},{7,23},{8,24},{9,... | collective-permute-start | bytes 2359304 | tf_op jit(solution)/shard_map/ppermute | solution.py:15
  55.8 52.3 %copy-start.6 = (bf16[512,768]{1,0:T(8,128)(2,1)}, bf16[512,768]{1,0:T(8,128)(2,1)S(1)}, u32[]{:S(2)}) copy-start(bf16[512,768]{1,0:T(8,128)(2,1)S(1)} %get-tuple-element.11) | copy-start | bytes 2359300
  63.6 21.2 %copy-start.108 = (f32[512]{0:T(512)}, f32[512]{0:T(512)S(1)}, u32[]{:S(2)}) copy-start(f32[512]{0:T(512)S(1)} %broadcast_multiply_fusion.15) | copy-start | bytes 6148
  64.0 20.8 %copy-start.118 = (f32[512]{0:T(512)}, f32[512]{0:T(512)S(1)}, u32[]{:S(2)}) copy-start(f32[512]{0:T(512)S(1)} %add_rsqrt_fusion.3) | copy-start | bytes 6148
  66.0 192.0 %copy-start.137 = (f32[512]{0:T(512)}, f32[512]{0:T(512)S(1)}, u32[]{:S(2)}) copy-start(f32[512]{0:T(512)S(1)} %fusion.349) | copy-start | bytes 6148
  95.3 16.3 %copy-start.31 = (bf16[512,768]{0,1:T(8,128)(2,1)}, bf16[512,768]{0,1:T(8,128)(2,1)S(1)}, u32[]{:S(2)}) copy-start(bf16[512,768]{0,1:T(8,128)(2,1)S(1)} %copy.84) | copy-start | bytes 2359300
  110.1 49.1 %copy-start.110 = (f32[512]{0:T(512)}, f32[512]{0:T(512)S(1)}, u32[]{:S(2)}) copy-start(f32[512]{0:T(512)S(1)} %broadcast_multiply_fusion.14) | copy-start | bytes 6148
  111.5 47.6 %copy-start.122 = (f32[512]{0:T(512)}, f32[512]{0:T(512)S(1)}, u32[]{:S(2)}) copy-start(f32[512]{0:T(512)S(1)} %add_rsqrt_fusion.2) | copy-start | bytes 6148
  127.6 15.2 %copy-start.84 = (bf16[512,768]{0,1:T(8,128)(2,1)S(1)}, bf16[512,768]{0,1:T(8,128)(2,1)}, u32[]{:S(2)}) copy-start(bf16[512,768]{0,1:T(8,128)(2,1)} %copy.82) | copy-start | bytes 2359300
  158.8 127.1 %copy-start.2 = (f32[512,768]{1,0:T(8,128)}, f32[512,768]{1,0:T(8,128)S(1)}, u32[]{:S(2)}) copy-start(f32[512,768]{1,0:T(8,128)S(1)} %get-tuple-element.89) | copy-start | bytes 4718596
  159.8 13.1 %slice-start.20 = ((s8[4718592]{0:T(1024)(128)(4,1)}), s8[4194304]{0:T(1024)(128)(4,1)S(1)}, s32[]{:S(2)}) async-start(s8[4718592]{0:T(1024)(128)(4,1)} %bitcast.389), calls=%async_computation.21 | async-start | bytes 8388608
  177.0 19.9 %collective-permute-start.2 = (bf16[512,768]{1,0:T(8,128)(2,1)}, bf16[512,768]{1,0:T(8,128)(2,1)}, u32[]{:S(2)}, u32[]{:S(2)}) collective-permute-start(bf16[512,768]{1,0:T(8,128)(2,1)} %get-tuple-element.166), channel_id=1, source_target_pairs={{0,16},{1,17},{2,18},{3,19},{4,20},{5,21},{6,22},{7,23},{8,24},{9,... | collective-permute-start | bytes 2359304 | tf_op jit(solution)/shard_map/ppermute | solution.py:15
  189.6 11.6 %slice-start.4 = ((s8[4718592]{0:T(1024)(128)(4,1)}), s8[4194304]{0:T(1024)(128)(4,1)S(1)}, s32[]{:S(2)}) async-start(s8[4718592]{0:T(1024)(128)(4,1)} %bitcast.335), calls=%async_computation.5 | async-start | bytes 8388608
  189.6 11.6 %slice-start.5 = ((s8[4718592]{0:T(1024)(128)(4,1)}), s8[524288]{0:T(1024)(128)(4,1)S(1)}, s32[]{:S(2)}) async-start(s8[4718592]{0:T(1024)(128)(4,1)} %bitcast.335), calls=%async_computation.6 | async-start | bytes 1048576
  253.7 13.1 %slice-start.14 = ((s8[4718592]{0:T(1024)(128)(4,1)}), s8[4194304]{0:T(1024)(128)(4,1)S(1)}, s32[]{:S(2)}) async-start(s8[4718592]{0:T(1024)(128)(4,1)} %bitcast.346), calls=%async_computation.15 | async-start | bytes 8388608
  257.6 28.2 %copy-start.8 = (f32[512,768]{1,0:T(8,128)}, f32[512,768]{1,0:T(8,128)S(1)}, u32[]{:S(2)}) copy-start(f32[512,768]{1,0:T(8,128)S(1)} %get-tuple-element.95) | copy-start | bytes 4718596
  258.0 12.9 %slice-start.22 = ((s8[4718592]{0:T(1024)(128)(4,1)}), s8[4194304]{0:T(1024)(128)(4,1)S(1)}, s32[]{:S(2)}) async-start(s8[4718592]{0:T(1024)(128)(4,1)} %bitcast.391), calls=%async_computation.23 | async-start | bytes 8388608
  270.9 9.7 %copy-start.151 = (bf16[512,3072]{1,0:T(8,128)(2,1)}, bf16[512,3072]{1,0:T(8,128)(2,1)S(1)}, u32[]{:S(2)}) copy-start(bf16[512,3072]{1,0:T(8,128)(2,1)S(1)} %get-tuple-element.172) | copy-start | bytes 9437188
  291.8 11.2 %copy-start.91 = (bf16[512,768]{0,1:T(8,128)(2,1)}, bf16[512,768]{0,1:T(8,128)(2,1)S(1)}, u32[]{:S(2)}) copy-start(bf16[512,768]{0,1:T(8,128)(2,1)S(1)} %copy.86) | copy-start | bytes 2359300
  291.8 11.1 %copy-start.57 = (f32[512,512]{0,1:T(8,128)S(1)}, f32[512,512]{0,1:T(8,128)}, u32[]{:S(2)}) copy-start(f32[512,512]{0,1:T(8,128)} %get-tuple-element.144) | copy-start | bytes 3145732
  291.8 11.1 %copy-start.59 = (f32[512,512]{0,1:T(8,128)S(1)}, f32[512,512]{0,1:T(8,128)}, u32[]{:S(2)}) copy-start(f32[512,512]{0,1:T(8,128)} %get-tuple-element.145) | copy-start | bytes 3145732
  302.9 20.2 %copy-start.34 = (bf16[512,768]{0,1:T(8,128)(2,1)S(1)}, bf16[512,768]{0,1:T(8,128)(2,1)}, u32[]{:S(2)}) copy-start(bf16[512,768]{0,1:T(8,128)(2,1)} %copy.83) | copy-start | bytes 2359300
  343.9 10.3 %copy-start.92 = (bf16[512,768]{0,1:T(8,128)(2,1)}, bf16[512,768]{0,1:T(8,128)(2,1)S(1)}, u32[]{:S(2)}) copy-start(bf16[512,768]{0,1:T(8,128)(2,1)S(1)} %copy.95) | copy-start | bytes 2359300
  343.9 10.3 %copy-start.55 = (f32[512,512]{0,1:T(8,128)S(1)}, f32[512,512]{0,1:T(8,128)}, u32[]{:S(2)}) copy-start(f32[512,512]{0,1:T(8,128)} %get-tuple-element.146) | copy-start | bytes 3145732
  343.9 10.3 %copy-start.89 = (bf16[512,768]{0,1:T(8,128)(2,1)S(1)}, bf16[512,768]{0,1:T(8,128)(2,1)}, u32[]{:S(2)}) copy-start(bf16[512,768]{0,1:T(8,128)(2,1)} %copy.91) | copy-start | bytes 2359300
  354.2 18.9 %copy-start.36 = (bf16[512,768]{0,1:T(8,128)(2,1)S(1)}, bf16[512,768]{0,1:T(8,128)(2,1)}, u32[]{:S(2)}) copy-start(bf16[512,768]{0,1:T(8,128)(2,1)} %copy.92) | copy-start | bytes 2359300
  402.0 34.3 %slice-start.16 = ((s8[4718592]{0:T(1024)(128)(4,1)}), s8[4194304]{0:T(1024)(128)(4,1)S(1)}, s32[]{:S(2)}) async-start(s8[4718592]{0:T(1024)(128)(4,1)} %bitcast.348), calls=%async_computation.17 | async-start | bytes 8388608
  402.0 40.6 %slice-start.8 = ((s8[6291456]{0:T(1024)(128)(4,1)}), s8[4194304]{0:T(1024)(128)(4,1)S(1)}, s32[]{:S(2)}) async-start(s8[6291456]{0:T(1024)(128)(4,1)} %bitcast.340), calls=%async_computation.9 | async-start | bytes 8388608
  404.7 22.5 %collective-permute-start.1 = (bf16[512,768]{1,0:T(8,128)(2,1)S(1)}, bf16[512,768]{1,0:T(8,128)(2,1)S(1)}, u32[]{:S(2)}, u32[]{:S(2)}) collective-permute-start(bf16[512,768]{1,0:T(8,128)(2,1)S(1)} %get-tuple-element.136), channel_id=1, source_target_pairs={{16,0},{17,1},{18,2},{19,3},{20,4},{21,5},{22,6},{23,7},{24,8},{25... | collective-permute-start | bytes 2359304 | tf_op jit(solution)/shard_map/ppermute | solution.py:15
  407.9 34.7 %collective-permute-start.3 = (bf16[512,768]{1,0:T(8,128)(2,1)S(1)}, bf16[512,768]{1,0:T(8,128)(2,1)S(1)}, u32[]{:S(2)}, u32[]{:S(2)}) collective-permute-start(bf16[512,768]{1,0:T(8,128)(2,1)S(1)} %fusion.129), channel_id=1, source_target_pairs={{16,0},{17,1},{18,2},{19,3},{20,4},{21,5},{22,6},{23,7},{24,8},{25... | collective-permute-start | bytes 2359304 | tf_op jit(solution)/shard_map/ppermute | solution.py:15
  427.3 9.1 %copy-start.129 = (f32[512]{0:T(512)S(1)}, f32[512]{0:T(512)}, u32[]{:S(2)}) copy-start(f32[512]{0:T(512)} %copy-done.128) | copy-start | bytes 6148
  427.3 9.1 %copy-start.138 = (f32[512]{0:T(512)S(1)}, f32[512]{0:T(512)}, u32[]{:S(2)}) copy-start(f32[512]{0:T(512)} %copy-done.137) | copy-start | bytes 6148
  427.3 15.3 %slice-start.9 = ((s8[6291456]{0:T(1024)(128)(4,1)}), s8[2097152]{0:T(1024)(128)(4,1)S(1)}, s32[]{:S(2)}) async-start(s8[6291456]{0:T(1024)(128)(4,1)} %bitcast.340), calls=%async_computation.10 | async-start | bytes 4194304
  436.4 22.7 %slice-start.6 = ((s8[4718592]{0:T(1024)(128)(4,1)}), s8[4194304]{0:T(1024)(128)(4,1)S(1)}, s32[]{:S(2)}) async-start(s8[4718592]{0:T(1024)(128)(4,1)} %bitcast.337), calls=%async_computation.7 | async-start | bytes 8388608
  440.4 11.1 %copy-start.11 = (f32[512,768]{1,0:T(8,128)S(1)}, f32[512,768]{1,0:T(8,128)}, u32[]{:S(2)}) copy-start(f32[512,768]{1,0:T(8,128)} %copy-done.9) | copy-start | bytes 4718596
  440.4 11.1 %copy-start.46 = (f32[512,768]{1,0:T(8,128)S(1)}, f32[512,768]{1,0:T(8,128)}, u32[]{:S(2)}) copy-start(f32[512,768]{1,0:T(8,128)} %get-tuple-element.170) | copy-start | bytes 4718596
  440.4 11.1 %copy-start.111 = (f32[512]{0:T(512)S(1)}, f32[512]{0:T(512)}, u32[]{:S(2)}) copy-start(f32[512]{0:T(512)} %copy-done.110) | copy-start | bytes 6148
  440.4 11.1 %copy-start.123 = (f32[512]{0:T(512)S(1)}, f32[512]{0:T(512)}, u32[]{:S(2)}) copy-start(f32[512]{0:T(512)} %copy-done.122) | copy-start | bytes 6148
  440.4 11.1 %copy-start.136 = (f32[512]{0:T(512)S(1)}, f32[512]{0:T(512)}, u32[]{:S(2)}) copy-start(f32[512]{0:T(512)} %fusion.350) | copy-start | bytes 6148
  440.4 11.1 %copy-start.155 = (f32[512,768]{1,0:T(8,128)S(1)}, f32[512,768]{1,0:T(8,128)}, u32[]{:S(2)}) copy-start(f32[512,768]{1,0:T(8,128)} %get-tuple-element.167) | copy-start | bytes 4718596
  440.4 18.7 %slice-start.7 = ((s8[4718592]{0:T(1024)(128)(4,1)}), s8[524288]{0:T(1024)(128)(4,1)S(1)}, s32[]{:S(2)}) async-start(s8[4718592]{0:T(1024)(128)(4,1)} %bitcast.337), calls=%async_computation.8 | async-start | bytes 1048576
  460.0 9.8 %copy-start.71 = (bf16[512,768]{1,0:T(8,128)(2,1)}, bf16[512,768]{1,0:T(8,128)(2,1)S(1)}, u32[]{:S(2)}) copy-start(bf16[512,768]{1,0:T(8,128)(2,1)S(1)} %get-tuple-element.107) | copy-start | bytes 2359300
  460.0 11.6 %copy-start.66 = (bf16[512,768]{1,0:T(8,128)(2,1)}, bf16[512,768]{1,0:T(8,128)(2,1)S(1)}, u32[]{:S(2)}) copy-start(bf16[512,768]{1,0:T(8,128)(2,1)S(1)} %get-tuple-element.106) | copy-start | bytes 2359300
  478.6 12.1 %copy-start.150 = (bf16[512,3072]{1,0:T(8,128)(2,1)S(1)}, bf16[512,3072]{1,0:T(8,128)(2,1)}, u32[]{:S(2)}) copy-start(bf16[512,3072]{1,0:T(8,128)(2,1)} %copy-done.149) | copy-start | bytes 9437188
  490.1 11.7 %collective-permute-start.8 = (bf16[1536,768]{1,0:T(8,128)(2,1)}, bf16[1536,768]{1,0:T(8,128)(2,1)}, u32[]{:S(2)}, u32[]{:S(2)}) collective-permute-start(bf16[1536,768]{1,0:T(8,128)(2,1)} %constant_dynamic-slice_fusion), channel_id=1, source_target_pairs={{0,1},{1,0},{2,3},{3,2},{4,5},{5,4},{6,7},{7,6},{8,9},{9,8},{10,11... | collective-permute-start | bytes 7077896 | tf_op jit(solution)/shard_map/ppermute | solution.py:195
  490.1 16.2 %collective-permute-start.4 = (bf16[1536,768]{1,0:T(8,128)(2,1)}, bf16[1536,768]{1,0:T(8,128)(2,1)S(1)}, u32[]{:S(2)}, u32[]{:S(2)}) collective-permute-start(bf16[1536,768]{1,0:T(8,128)(2,1)} %constant_dynamic-slice_fusion.2), channel_id=1, source_target_pairs={{0,1},{1,0},{2,3},{3,2},{4,5},{5,4},{6,7},{7,6},{8,9},{9,8},{10,11... | collective-permute-start | bytes 7077896 | tf_op jit(solution)/shard_map/ppermute | solution.py:195
  501.9 8.2 %collective-permute-start.6 = (bf16[384,3072]{1,0:T(8,128)(2,1)}, bf16[384,3072]{1,0:T(8,128)(2,1)}, u32[]{:S(2)}, u32[]{:S(2)}) collective-permute-start(bf16[384,3072]{1,0:T(8,128)(2,1)} %constant_dynamic-slice_fusion.1), channel_id=1, source_target_pairs={{0,1},{1,0},{2,3},{3,2},{4,5},{5,4},{6,7},{7,6},{8,9},{9,8},{10,11... | collective-permute-start | bytes 7077896 | tf_op jit(solution)/shard_map/ppermute | solution.py:195
  750.0 34.0 %collective-permute-start.5 = (bf16[1536,768]{1,0:T(8,128)(2,1)}, bf16[1536,768]{1,0:T(8,128)(2,1)}, u32[]{:S(2)}, u32[]{:S(2)}) collective-permute-start(bf16[1536,768]{1,0:T(8,128)(2,1)} %get-tuple-element.81), channel_id=1, source_target_pairs={{0,1},{1,0},{2,3},{3,2},{4,5},{5,4},{6,7},{7,6},{8,9},{9,8},{10,11... | collective-permute-start | bytes 7077896 | tf_op jit(solution)/shard_map/ppermute | solution.py:197
  760.7 4.2 collective-permute-start.10
  764.9 3.9 collective-permute-start.11
  768.8 3.9 collective-permute-start.12
  768.9 22.9 %collective-permute-start.9 = (bf16[1536,768]{1,0:T(8,128)(2,1)}, bf16[1536,768]{1,0:T(8,128)(2,1)}, u32[]{:S(2)}, u32[]{:S(2)}) collective-permute-start(bf16[1536,768]{1,0:T(8,128)(2,1)} %get-tuple-element.83), channel_id=1, source_target_pairs={{0,1},{1,0},{2,3},{3,2},{4,5},{5,4},{6,7},{7,6},{8,9},{9,8},{10,11... | collective-permute-start | bytes 7077896 | tf_op jit(solution)/shard_map/ppermute | solution.py:197
  769.8 14.1 %copy-start.41 = (bf16[384,3072]{1,0:T(8,128)(2,1)S(1)}, bf16[384,3072]{1,0:T(8,128)(2,1)}, u32[]{:S(2)}) copy-start(bf16[384,3072]{1,0:T(8,128)(2,1)} %get-tuple-element.82) | copy-start | bytes 7077892
  772.7 4.8 collective-permute-start.13
  777.5 3.9 collective-permute-start.14
  784.0 15.0 %collective-permute-start.7 = (bf16[384,3072]{1,0:T(8,128)(2,1)S(1)}, bf16[384,3072]{1,0:T(8,128)(2,1)S(1)}, u32[]{:S(2)}, u32[]{:S(2)}) collective-permute-start(bf16[384,3072]{1,0:T(8,128)(2,1)S(1)} %copy-done.41), channel_id=1, source_target_pairs={{0,1},{1,0},{2,3},{3,2},{4,5},{5,4},{6,7},{7,6},{8,9},{9,8},{10,11... | collective-permute-start | bytes 7077896 | tf_op jit(solution)/shard_map/ppermute | solution.py:197
  (135 other events, 570.7 us)
Sparse Core Ops, SparseCore 0:
  514.3 235.6 all-reduce.3

commit v2 on v1

v2 whole, which is shorter than its diff:
```python
import functools
import jax
import jax.numpy as jnp
from jax import lax
from jax.sharding import Mesh, PartitionSpec as P
from jax.experimental import pallas as pl
from jax.experimental.pallas import tpu as pltpu

RADIUS = 128
REACH = 64
QUERY_BLOCK = 128
EPSILON = 1e-05
NEG_FILL = -1e30
GELU_C = 0.7978845608028654
F32, BF16 = jnp.float32, jnp.bfloat16
MIB = 1024 * 1024


def low(vector):
    return vector.astype(BF16)


def dot_nn(left, right):
    return jnp.dot(left, right, preferred_element_type=F32)


def dot_nt(left, right):
    return lax.dot_general(left, right, (((1,), (1,)), ((), ())), preferred_element_type=F32)


def dot_tn(left, right):
    return lax.dot_general(left, right, (((0,), (0,)), ((), ())), preferred_element_type=F32)


def normalized(vector):
    center = vector - jnp.mean(vector, axis=-1, keepdims=True)
    inverse = lax.rsqrt(jnp.mean(center * center, axis=-1, keepdims=True) + EPSILON)
    return center * inverse, inverse


def norm_backward(vector, gain_row, grad_normed):
    normed, inverse = normalized(vector)
    scaled = grad_normed * gain_row
    mean_scaled = jnp.mean(scaled, axis=-1, keepdims=True)
    mean_mixed = jnp.mean(scaled * normed, axis=-1, keepdims=True)
    grad_input = inverse * (scaled - mean_scaled - normed * mean_mixed)
    grad_gain = jnp.sum(grad_normed * normed, axis=0, keepdims=True)
    return grad_input, grad_gain, jnp.sum(grad_normed, axis=0, keepdims=True)


def live_sums(length, start, items):
    rows = items[0].shape[0]
    live = start + lax.broadcasted_iota(jnp.int32, (rows, 1), 0) < length
    return [jnp.sum(jnp.where(live, v * v, 0.0), axis=0, keepdims=True) for v in items]


def whole(shape):
    return pl.BlockSpec(shape, lambda *_: (0,) * len(shape))


def part_of(shape, doc, axis):
    place = tuple(doc if d == axis else 0 for d in range(len(shape)))
    return pl.BlockSpec(shape, lambda *_: place)


def column(row):
    return jnp.broadcast_to(row, (row.shape[1], row.shape[1])).T[:, 0:1]


def kernel_call(body, grid, in_specs, outs, scratch, limit, flops, moved, name, transcendentals=0):
    return pl.pallas_call(
        body,
        out_shape=[jax.ShapeDtypeStruct(shape, kind) for shape, kind, _ in outs],
        grid_spec=pltpu.PrefetchScalarGridSpec(
            num_scalar_prefetch=1,
            grid=grid,
            in_specs=in_specs,
            out_specs=[spec for _, _, spec in outs],
            scratch_shapes=scratch,
        ),
        compiler_params=pltpu.CompilerParams(
            dimension_semantics=("arbitrary",) * len(grid), vmem_limit_bytes=limit * MIB
        ),
        cost_estimate=pl.CostEstimate(
            flops=int(flops), bytes_accessed=int(moved), transcendentals=int(transcendentals)
        ),
        name=name,
    )


def feed_forward_body(
    length_ref, resid_ref, gain_ref, shift_ref, up_ref, bias_ref, down_ref,
    normed_ref, active_ref, slope_ref, out_ref, stat_ref, sum_ref,
):
    step = pl.program_id(0)
    rows = resid_ref.shape[0]

    @pl.when(step == 0)
    def _():
        normed_ref[...] = low(normalized(resid_ref[...])[0] * gain_ref[1:2, :] + shift_ref[1:2, :])
        sum_ref[...] = jnp.zeros_like(sum_ref)

    parts = 2
    for part in range(parts):
        own = pl.ds(part * (rows // parts), rows // parts)
        pre = dot_nn(normed_ref[own, :], up_ref[...]) + bias_ref[...]
        square = pre * pre
        curve = jnp.tanh(pre * (GELU_C + GELU_C * 0.044715 * square))
        half = 0.5 + 0.5 * curve
        active = low(pre * half)
        active_ref[own, :] = active
        rise = pre * (GELU_C + 3.0 * GELU_C * 0.044715 * square)
        slope_ref[own, :] = low(half + rise * (half - half * half) * 2.0)
        sum_ref[own, :] += dot_nn(active, down_ref[...])

    @pl.when(step == pl.num_programs(0) - 1)
    def _():
        branch = sum_ref[...]
        result = resid_ref[...] + branch
        out_ref[...] = low(result)
        first, second = live_sums(length_ref[0], 0, (branch, result))
        stat_ref[0:1, :] = first
        stat_ref[1:2, :] = second


def feed_forward(length, resid, gain, shift, up, bias, down, tile=1024):
    rows, width = resid.shape
    hidden = up.shape[1]
    over = lambda j, *_: (0, j)
    return kernel_call(
        feed_forward_body,
        (hidden // tile,),
        [
            whole((rows, width)), whole((2, width)), whole((2, width)),
            pl.BlockSpec((width, tile), over), pl.BlockSpec((1, tile), over),
            pl.BlockSpec((tile, width), lambda j, *_: (j, 0)),
        ],
        [
            ((rows, width), BF16, whole((rows, width))),
            ((rows, hidden), BF16, pl.BlockSpec((rows, tile), over)),
            ((rows, hidden), BF16, pl.BlockSpec((rows, tile), over)),
            ((rows, width), BF16, whole((rows, width))),
            ((2, width), F32, whole((2, width))),
        ],
        [pltpu.VMEM((rows, width), F32)],
        32,
        4 * rows * width * hidden,
        4 * (rows * hidden + width * hidden) + 8 * rows * width,
        "feed_forward",
        rows * hidden,
    )(length, resid, gain, shift, up, bias, down)


def feed_backward_body(
    length_ref, grad_ref, resid_ref, gain_ref, slope_ref, up_ref, down_ref,
    pre_ref, bias_ref, out_ref, gain_out, shift_out, sum_ref,
):
    step = pl.program_id(0)
    rows = resid_ref.shape[0]

    @pl.when(step == 0)
    def _():
        sum_ref[...] = jnp.zeros_like(sum_ref)

    parts = 2
    total = None
    for part in range(parts):
        own = pl.ds(part * (rows // parts), rows // parts)
        grad_active = dot_nt(grad_ref[own, :], down_ref[...])
        grad_pre = low(slope_ref[own, :].astype(F32) * grad_active)
        pre_ref[own, :] = grad_pre
        here = jnp.sum(grad_pre.astype(F32), axis=0, keepdims=True)
        total = here if total is None else total + here
        sum_ref[own, :] += dot_nt(grad_pre, up_ref[...])

    bias_ref[...] = total

    @pl.when(step == pl.num_programs(0) - 1)
    def _():
        grad_input, grad_gain, grad_shift = norm_backward(resid_ref[...], gain_ref[1:2, :], sum_ref[...])
        out_ref[...] = grad_ref[...].astype(F32) + grad_input
        gain_out[...] = grad_gain
        shift_out[...] = grad_shift


def feed_backward(length, grad, doc, resid, gain, slope, up, down, tile=1024):
    rows, width = resid.shape
    hidden = up.shape[1]
    over = lambda j, *_: (0, j)
    return kernel_call(
        feed_backward_body,
        (hidden // tile,),
        [
            part_of((rows, width), doc, 0), whole((rows, width)), whole((2, width)),
            pl.BlockSpec((rows, tile), over), pl.BlockSpec((width, tile), over),
            pl.BlockSpec((tile, width), lambda j, *_: (j, 0)),
        ],
        [
            ((rows, hidden), BF16, pl.BlockSpec((rows, tile), over)),
            ((1, hidden), F32, pl.BlockSpec((1, tile), over)),
            ((rows, width), F32, whole((rows, width))),
            ((1, width), F32, whole((1, width))),
            ((1, width), F32, whole((1, width))),
        ],
        [pltpu.VMEM((rows, width), F32)],
        32,
        4 * rows * width * hidden,
        4 * (rows * hidden + width * hidden) + 10 * rows * width,
        "feed_backward",
    )(length, grad, resid, gain, slope, up, down)


def graph_windows(rows):
    span = QUERY_BLOCK + 2 * REACH
    return [
        (start, min(max(start - REACH, 0), rows - span), span)
        for start in range(0, rows, QUERY_BLOCK)
    ]


def graph_forward_body(
    length_ref, x_ref, near_ref_t, counts_ref, gain_ref, shift_ref, w_ref,
    left_ref, link_ref, sigma_ref, pull_ref, resid_ref, stat_ref,
):
    normed_ref, mean_ref, mixed_ref = (left_ref.at[i] for i in range(3))
    rows = x_ref.shape[0]
    normed_ref[...] = low(normalized(x_ref[...].astype(F32))[0] * gain_ref[0:1, :] + shift_ref[0:1, :])
    slots = near_ref_t.shape[0]
    slot = lax.broadcasted_iota(jnp.int32, (slots, QUERY_BLOCK), 0)
    for row, start, span in graph_windows(rows):
        own = pl.ds(row, QUERY_BLOCK)
        counts = counts_ref[:, own]
        index = jnp.where(slot < counts, near_ref_t[:, own], -1)
        place = start + lax.broadcasted_iota(jnp.int32, (span, QUERY_BLOCK), 0)
        links = jnp.zeros((span, QUERY_BLOCK), F32)
        for s in range(slots):
            links += jnp.where(index[s : s + 1, :] == place, 1.0, 0.0)
        link_ref[:, own] = low(links)
        total = dot_nn(low(links.T), normed_ref[pl.ds(start, span), :])
        mean_ref[own, :] = low(total / column(counts.astype(F32)))
    sums = None
    parts = 2
    for part in range(parts):
        own = pl.ds(part * (rows // parts), rows // parts)
        pre = dot_nn(normed_ref[own, :], w_ref[0]) + dot_nn(mean_ref[own, :], w_ref[1])
        sigma = jax.nn.sigmoid(dot_nn(mean_ref[own, :], w_ref[2]))
        mixed = pre * sigma
        sigma_ref[own, :] = low(sigma)
        pull_ref[own, :] = low(mixed - mixed * sigma)
        mixed_ref[own, :] = low(mixed)
        branch = dot_nn(low(mixed), w_ref[3])
        resid = x_ref[own, :].astype(F32) + branch
        resid_ref[own, :] = resid
        here = live_sums(length_ref[0], part * (rows // parts), (branch, resid))
        sums = here if sums is None else [a + b for a, b in zip(sums, here)]
    stat_ref[0:1, :] = sums[0]
    stat_ref[1:2, :] = sums[1]


def graph_forward(length, x, doc, rows, near_t, counts, gain, shift, weights):
    width = x.shape[1]
    slots = near_t.shape[0]
    span = QUERY_BLOCK + 2 * REACH
    full = whole((rows, width))
    return kernel_call(
        graph_forward_body,
        (1,),
        [
            part_of((rows, width), doc, 0), part_of((slots, rows), doc, 1), part_of((1, rows), doc, 1),
            whole((2, width)), whole((2, width)), whole(weights.shape),
        ],
        [
            ((3, rows, width), BF16, whole((3, rows, width))),
            ((span, rows), BF16, whole((span, rows))),
            ((rows, width), BF16, full),
            ((rows, width), BF16, full),
            ((rows, width), F32, full),
            ((2, width), F32, whole((2, width))),
        ],
        [],
        40,
        8 * rows * width * width + 2 * rows * span * width,
        16 * rows * width + 8 * width * width,
        "graph_forward",
    )(length, x, near_t, counts, gain, shift, weights)


def graph_backward_body(
    length_ref, grad_ref, x_ref, gain_ref, sigma_ref, pull_ref, link_ref, counts_ref, w_ref,
    right_ref, out_ref, gain_out, shift_out, mean_ref, sum_ref,
):
    rows = x_ref.shape[0]
    counts_column = column(counts_ref[...].astype(F32))
    parts = 2
    for part in range(parts):
        own = pl.ds(part * (rows // parts), rows // parts)
        grad_low = low(grad_ref[own, :])
        right_ref[2, own, :] = grad_low
        grad_mixed = dot_nt(grad_low, w_ref[3])
        grad_pre = low(sigma_ref[own, :].astype(F32) * grad_mixed)
        grad_gate = low(pull_ref[own, :].astype(F32) * grad_mixed)
        right_ref[0, own, :] = grad_pre
        right_ref[1, own, :] = grad_gate
        sum_ref[own, :] = dot_nt(grad_pre, w_ref[0])
        grad_mean = dot_nt(grad_pre, w_ref[1]) + dot_nt(grad_gate, w_ref[2])
        mean_ref[own, :] = low(grad_mean / counts_column[part * (rows // parts) : (part + 1) * (rows // parts), :])
    for row, start, span in graph_windows(rows):
        own = pl.ds(row, QUERY_BLOCK)
        sum_ref[pl.ds(start, span), :] += dot_nn(link_ref[:, own], mean_ref[own, :])
    grad_input, grad_gain, grad_shift = norm_backward(
        x_ref[...].astype(F32), gain_ref[0:1, :], sum_ref[...]
    )
    out_ref[...] = low(grad_ref[...] + grad_input)
    gain_out[...] = grad_gain
    shift_out[...] = grad_shift


def graph_backward(length, grad, x, doc, gain, sigma, pull, links, counts, weights):
    rows, width = grad.shape
    full = whole((rows, width))
    return kernel_call(
        graph_backward_body,
        (1,),
        [
            full, part_of((rows, width), doc, 0), whole((2, width)), full, full, whole(links.shape),
            part_of((1, rows), doc, 1), whole(weights.shape),
        ],
        [
            ((3, rows, width), BF16, whole((3, rows, width))),
            ((rows, width), BF16, full),
            ((1, width), F32, whole((1, width))),
            ((1, width), F32, whole((1, width))),
        ],
        [pltpu.VMEM((rows, width), BF16), pltpu.VMEM((rows, width), F32)],
        40,
        8 * rows * width * width + 2 * rows * links.shape[0] * width,
        18 * rows * width + 8 * width * width,
        "graph_backward",
    )(length, grad, x, gain, sigma, pull, links, counts, weights)


def attend_windows(rows):
    windows, offset = [], 0
    for row in range(0, rows, QUERY_BLOCK):
        start = max(row - RADIUS, 0)
        span = min(row + QUERY_BLOCK + RADIUS, rows) - start
        windows.append((row, start, span, offset))
        offset += span
    return windows, offset


def two_heads(block, lane):
    zero = jnp.zeros_like(block)
    return jnp.concatenate([jnp.where(lane, block, zero), jnp.where(lane, zero, block)], axis=0)


def attend_forward_body(
    length_ref, mid_ref, coords_ref, rich_ref, gain_ref, shift_ref, w_ref,
    left_ref, query_ref, key_ref, value_ref, probs_ref, terms_ref, resid_ref, stat_ref,
    turned_ref, turned_context, mask_ref,
):
    normed_ref, context_ref = left_ref.at[0], left_ref.at[1]
    rows, width = mid_ref.shape
    heads = rich_ref.shape[1]
    head_width = width // heads
    scale = head_width ** (-0.5)
    length = length_ref[0]
    windows, _ = attend_windows(rows)
    parts = 2
    for part in range(parts):
        own = pl.ds(part * (rows // parts), rows // parts)
        x = mid_ref[own, :].astype(F32)
        normed = low(normalized(x)[0] * gain_ref[0:1, :] + shift_ref[0:1, :])
        normed_ref[own, :] = normed
        query_ref[own, :] = low(dot_nn(normed, w_ref[0]))
        key_ref[own, :] = low(dot_nn(normed, w_ref[1]))
        value = dot_nn(normed, w_ref[2])
        value_ref[own, :] = low(value)
        turned_ref[:, own] = low(value.T)
    for row, start, span, offset in windows:
        i = row + lax.broadcasted_iota(jnp.int32, (span, QUERY_BLOCK), 1)
        j = start + lax.broadcasted_iota(jnp.int32, (span, QUERY_BLOCK), 0)
        allowed = (jnp.abs(i - j) <= RADIUS) & ((j < length) | (i == j))
        mask_ref[pl.ds(offset, span), :] = jnp.where(allowed, 0.0, NEG_FILL)
        across = coords_ref[:, pl.ds(row, QUERY_BLOCK)]
        along = [
            jnp.broadcast_to(coords_ref[:, pl.ds(at, QUERY_BLOCK)], (QUERY_BLOCK, QUERY_BLOCK)).T
            for at in range(start, start + span, QUERY_BLOCK)
        ]
        gap = across - jnp.concatenate(along, axis=0)
        terms_ref[0, pl.ds(offset, span), :] = jnp.log(1.0 + jnp.abs(gap))
        terms_ref[1, pl.ds(offset, span), :] = jnp.tanh(-gap)

    lane = lax.broadcasted_iota(jnp.int32, (QUERY_BLOCK, 2 * head_width), 1) < head_width

    def pair(index, carry):
        columns = pl.ds(pl.multiple_of(index * 2 * head_width, 2 * head_width), 2 * head_width)
        for row, start, span, offset in windows:
            queries = two_heads(query_ref[pl.ds(row, QUERY_BLOCK), columns], lane)
            raw = dot_nt(key_ref[pl.ds(start, span), columns], queries)
            spread = terms_ref[0, pl.ds(offset, span), :]
            order = terms_ref[1, pl.ds(offset, span), :]
            mask = mask_ref[pl.ds(offset, span), :]
            for side in range(2):
                head = 2 * index + side
                own = raw[:, side * QUERY_BLOCK : (side + 1) * QUERY_BLOCK]
                scores = own * scale + (spread * rich_ref[0, head] + order * rich_ref[1, head]) + mask
                weights = jnp.exp(scores - jnp.max(scores, axis=0, keepdims=True))
                probs = low(weights * (1.0 / jnp.sum(weights, axis=0, keepdims=True)))
                probs_ref[index, pl.ds(offset, span), pl.ds(side * QUERY_BLOCK, QUERY_BLOCK)] = probs
                place = pl.ds(pl.multiple_of(head * head_width, head_width), head_width)
                turned_context[place, pl.ds(row, QUERY_BLOCK)] = dot_nn(
                    turned_ref[place, pl.ds(start, span)], probs
                )
        return carry

    lax.fori_loop(0, heads // 2, pair, 0)
    sums = None
    for part in range(parts):
        own = pl.ds(part * (rows // parts), rows // parts)
        context = low(turned_context[:, own].T)
        context_ref[own, :] = context
        branch = dot_nn(context, w_ref[3])
        resid = mid_ref[own, :].astype(F32) + branch
        resid_ref[own, :] = resid
        here = live_sums(length, part * (rows // parts), (branch, resid))
        sums = here if sums is None else [a + b for a, b in zip(sums, here)]
    stat_ref[0:1, :] = sums[0]
    stat_ref[1:2, :] = sums[1]


def attend_forward(length, mid, doc, coords, rich, gain, shift, weights):
    rows, width = mid.shape
    heads = rich.shape[1]
    full = whole((rows, width))
    _, band = attend_windows(rows)
    return kernel_call(
        attend_forward_body,
        (1,),
        [
            full, part_of((1, rows), doc, 1), pl.BlockSpec(memory_space=pltpu.SMEM),
            whole((2, width)), whole((2, width)), whole(weights.shape),
        ],
        [
            ((2, rows, width), BF16, whole((2, rows, width))),
            ((rows, width), BF16, full),
            ((rows, width), BF16, full),
            ((rows, width), BF16, full),
            ((heads // 2, band, 2 * QUERY_BLOCK), BF16, whole((heads // 2, band, 2 * QUERY_BLOCK))),
            ((2, band, QUERY_BLOCK), F32, whole((2, band, QUERY_BLOCK))),
            ((rows, width), F32, full),
            ((2, width), F32, whole((2, width))),
        ],
        [
            pltpu.VMEM((width, rows), BF16),
            pltpu.VMEM((width, rows), F32),
            pltpu.VMEM((band, QUERY_BLOCK), F32),
        ],
        56,
        8 * rows * width * width + 4 * band * QUERY_BLOCK * width,
        14 * rows * width + 8 * width * width + 2 * heads * band * QUERY_BLOCK,
        "attend_forward",
        heads * band * QUERY_BLOCK,
    )(length, mid, coords, rich, gain, shift, weights)


def attend_backward_body(
    length_ref, grad_ref, mid_ref, gain_ref, query_ref, key_ref, value_ref, probs_ref, terms_ref, w_ref,
    right_ref, out_ref, rich_out, gain_out, shift_out,
    turned_key, turned_query, context_ref, key_sum, value_sum,
):
    rows, width = mid_ref.shape
    pairs = probs_ref.shape[0]
    head_width = width // (2 * pairs)
    scale = head_width ** (-0.5)
    windows, _ = attend_windows(rows)
    parts = 2
    for part in range(parts):
        own = pl.ds(part * (rows // parts), rows // parts)
        grad_low = low(grad_ref[own, :])
        right_ref[3, own, :] = grad_low
        context_ref[own, :] = low(dot_nt(grad_low, w_ref[3]))
        turned_key[:, own] = low(key_ref[own, :].astype(F32).T)
    key_sum[...] = jnp.zeros_like(key_sum)
    value_sum[...] = jnp.zeros_like(value_sum)
    lane = lax.broadcasted_iota(jnp.int32, (QUERY_BLOCK, 2 * head_width), 1) < head_width

    def pair(index, carry):
        columns = pl.ds(pl.multiple_of(index * 2 * head_width, 2 * head_width), 2 * head_width)
        rich = [[0.0, 0.0], [0.0, 0.0]]
        for row, start, span, offset in windows:
            keys = pl.ds(start, span)
            context = two_heads(context_ref[pl.ds(row, QUERY_BLOCK), columns], lane)
            queries = two_heads(query_ref[pl.ds(row, QUERY_BLOCK), columns], lane)
            grad_probs = dot_nt(value_ref[keys, columns], context)
            probs = probs_ref[index, pl.ds(offset, span), :]
            value_sum[keys, columns] += dot_nn(probs, context)
            spread = terms_ref[0, pl.ds(offset, span), :]
            order = terms_ref[1, pl.ds(offset, span), :]
            grads = []
            for side in range(2):
                lanes = slice(side * QUERY_BLOCK, (side + 1) * QUERY_BLOCK)
                own = probs[:, lanes].astype(F32)
                mixed = own * grad_probs[:, lanes]
                grad_scores = mixed - own * jnp.sum(mixed, axis=0, keepdims=True)
                rich[0][side] += jnp.sum(grad_scores * spread, axis=0, keepdims=True)
                rich[1][side] += jnp.sum(grad_scores * order, axis=0, keepdims=True)
                grad_raw = low(grad_scores * scale)
                grads.append(grad_raw)
                place = pl.ds(
                    pl.multiple_of((2 * index + side) * head_width, head_width), head_width
                )
                turned_query[place, pl.ds(row, QUERY_BLOCK)] = dot_nn(turned_key[place, keys], grad_raw)
            key_sum[keys, columns] += dot_nn(jnp.concatenate(grads, axis=1), queries)
        for which in range(2):
            for side in range(2):
                rich_out[which, pl.ds(2 * index + side, 1), :] = rich[which][side]
        return carry

    lax.fori_loop(0, pairs, pair, 0)
    gains, shifts = None, None
    for part in range(parts):
        own = pl.ds(part * (rows // parts), rows // parts)
        grad_query = low(turned_query[:, own].T)
        grad_key = low(key_sum[own, :])
        grad_value = low(value_sum[own, :])
        right_ref[0, own, :] = grad_query
        right_ref[1, own, :] = grad_key
        right_ref[2, own, :] = grad_value
        grad_normed = (
            dot_nt(grad_query, w_ref[0]) + dot_nt(grad_key, w_ref[1]) + dot_nt(grad_value, w_ref[2])
        )
        grad_input, grad_gain, grad_shift = norm_backward(
            mid_ref[own, :].astype(F32), gain_ref[0:1, :], grad_normed
        )
        out_ref[own, :] = low(grad_ref[own, :] + grad_input)
        gains = grad_gain if gains is None else gains + grad_gain
        shifts = grad_shift if shifts is None else shifts + grad_shift
    gain_out[...] = gains
    shift_out[...] = shifts


def attend_backward(length, grad, mid, gain, query, key, value, probs, terms, weights):
    rows, width = mid.shape
    pairs, band, _ = probs.shape
    full = whole((rows, width))
    return kernel_call(
        attend_backward_body,
        (1,),
        [
            full, full, whole((2, width)), full, full, full, whole(probs.shape), whole(terms.shape),
            whole(weights.shape),
        ],
        [
            ((4, rows, width), BF16, whole((4, rows, width))),
            ((rows, width), BF16, full),
            ((2, 2 * pairs, QUERY_BLOCK), F32, whole((2, 2 * pairs, QUERY_BLOCK))),
            ((1, width), F32, whole((1, width))),
            ((1, width), F32, whole((1, width))),
        ],
        [
            pltpu.VMEM((width, rows), BF16),
            pltpu.VMEM((width, rows), F32),
            pltpu.VMEM((rows, width), BF16),
            pltpu.VMEM((rows, width), F32),
            pltpu.VMEM((rows, width), F32),
        ],
        56,
        8 * rows * width * width + 8 * band * QUERY_BLOCK * width,
        18 * rows * width + 8 * width * width + 4 * pairs * band * QUERY_BLOCK,
        "attend_backward",
    )(length, grad, mid, gain, query, key, value, probs, terms, weights)


def weight_body(count, flag_ref, *refs):
    one, two, out_ref = refs[: 2 * count], refs[2 * count : 4 * count], refs[4 * count]

    def write(side):
        total = None
        for doc in range(count):
            left, right = side[2 * doc][...], side[2 * doc + 1][...]
            left, right = (v.reshape(v.shape[-2:]) for v in (left, right))
            here = dot_tn(left, right)
            total = here if total is None else total + here
        out_ref[...] = low(total)

    @pl.when(flag_ref[0] == 1)
    def _():
        write(one)

    @pl.when(flag_ref[0] == 0)
    def _():
        write(two)


def weight_product(flag, one, two, grid, block, name):
    count = len(one)
    specs, operands = [], []
    for pick, side in ((1, one), (0, two)):
        for left, left_block, left_map, right, right_block, right_map in side:
            for array, shape, place in ((left, left_block, left_map), (right, right_block, right_map)):
                operands.append(array)
                specs.append(
                    pl.BlockSpec(
                        shape,
                        functools.partial(
                            lambda place, pick, j, chosen: place(jnp.where(chosen[0] == pick, j, 0)),
                            place,
                            pick,
                        ),
                    )
                )
    tall, wide = block
    return kernel_call(
        functools.partial(weight_body, count),
        (grid,),
        specs,
        [((grid * tall, wide), BF16, pl.BlockSpec(block, lambda j, *_: (j, 0)))],
        [],
        32,
        2 * grid * tall * wide * count * one[0][0].shape[-2],
        2 * (grid * tall * wide + sum(v.size for v in operands) // 2),
        name,
    )(flag, *operands)[0]


def passed_along(block, axis, distance):
    devices = range(lax.axis_size(axis))
    route = [(i - distance, i) for i in devices if i - distance in devices]
    return lax.ppermute(block, axis, route)


def exchanged_sum(block, axis):
    size = lax.axis_size(axis)
    step = 1
    while step < size:
        route = [(i, i ^ step) for i in range(size)]
        block = block + lax.ppermute(block, axis, route)
        step *= 2
    return block


def summed_over_documents(block):
    core = lax.axis_index("core")
    swap = [(0, 1), (1, 0)]
    half = block.shape[0] // 2
    own = lax.dynamic_slice_in_dim(block, core * half, half, 0)
    other = lax.dynamic_slice_in_dim(block, (1 - core) * half, half, 0)
    part = own + lax.ppermute(other, "core", swap)
    part = lax.psum(part, "chip")
    other = lax.ppermute(part, "core", swap)
    return jnp.concatenate(
        [jnp.where(core == 0, part, other), jnp.where(core == 0, other, part)], axis=0
    )


def local(
    boundary,
    lengths,
    neighbours,
    counts,
    coords,
    square_weights,
    up_weight,
    down_weight,
    up_bias,
    norm_gain,
    norm_bias,
    rich_terms,
):
    first = lax.axis_index("section") == 0
    flag = first.astype(jnp.int32)[None]
    documents = lengths.shape[0]
    rows = boundary.shape[1] // documents
    width = boundary.shape[2]
    hidden = up_weight.shape[2]
    heads = rich_terms.shape[1]
    source = boundary[0]
    squares = square_weights[0]
    up, down, bias = up_weight[0], down_weight[0], up_bias
    gains, shifts = norm_gain[0], norm_bias[0]
    near_t = neighbours.T
    counts_row, coords_row = counts[None], coords[None]
    length = [lax.slice_in_dim(lengths, doc, doc + 1) for doc in range(documents)]

    graph_kept, ff_one, resid_one, arrived, stats_one = [], [], [], [], []
    sent = None
    for doc in range(documents):
        here = source
        if doc:
            here, _ = lax.optimization_barrier((source, sent))
        left, links, sigma, pull, resid, stat = graph_forward(
            length[doc], here, doc, rows, near_t, counts_row, gains, shifts, squares
        )
        normed, active, slope, sent, stat_f = feed_forward(
            length[doc], resid, gains, shifts, up, bias, down
        )
        graph_kept.append((left, links, sigma, pull))
        ff_one.append((normed, active, slope))
        resid_one.append(resid)
        stats_one.append((stat, stat_f))
        arrived.append(passed_along(sent, "section", 1))

    back, out_two, rich_two, stats_two, ff_two, rights_two, small_two = [], [], [], [], [], [], []
    for doc in range(documents):
        left, query, key, value, probs, terms, resid, stat = attend_forward(
            length[doc], arrived[doc], doc, coords_row, rich_terms, gains, shifts, squares
        )
        normed, active, slope, result, stat_f = feed_forward(
            length[doc], resid, gains, shifts, up, bias, down
        )
        grad_pre, grad_bias, grad_resid, gain_f, shift_f = feed_backward(
            length[doc], source, doc, resid, gains, slope, up, down
        )
        right, grad_mid, rich, gain_a, shift_a = attend_backward(
            length[doc], grad_resid, arrived[doc], gains, query, key, value, probs, terms, squares
        )
        out_two.append(result)
        ff_two.append((normed, active, grad_pre))
        rights_two.append((left, right))
        stats_two.append((stat, stat_f))
        rich_two.append(rich)
        small_two.append((grad_bias, gain_a, gain_f, shift_a, shift_f))
        back.append(passed_along(grad_mid, "section", -1))
        last_sent = grad_mid

    out_one, pre_one, rights_one, small_one = [], [], [], []
    for doc in range(documents):
        grad_mid = back[doc]
        if doc < documents - 1:
            grad_mid, _ = lax.optimization_barrier((grad_mid, last_sent))
        left, links, sigma, pull = graph_kept[doc]
        normed, active, slope = ff_one[doc]
        grad_pre, grad_bias, grad_resid, gain_f, shift_f = feed_backward(
            length[doc], grad_mid, 0, resid_one[doc], gains, slope, up, down
        )
        right, grad_x, gain_a, shift_a = graph_backward(
            length[doc], grad_resid, source, doc, gains, sigma, pull, links, counts_row, squares
        )
        out_one.append(grad_x)
        pre_one.append(grad_pre)
        rights_one.append((left, right))
        small_one.append((grad_bias, gain_a, gain_f, shift_a, shift_f))

    docs = range(documents)
    tile = 512
    grad_down = weight_product(
        flag,
        [
            (ff_one[d][1], (rows, tile), lambda j: (0, j), back[d], (rows, width), lambda j: (0, 0))
            for d in docs
        ],
        [
            (
                ff_two[d][1], (rows, tile), lambda j: (0, j),
                source, (rows, width), functools.partial(lambda d, j: (d, 0), d),
            )
            for d in docs
        ],
        hidden // tile,
        (tile, width),
        "down_gradient",
    )
    still, across = lambda j: (0, 0), lambda j: (0, j)
    grad_up = weight_product(
        flag,
        [(ff_one[d][0], (rows, width), still, pre_one[d], (rows, width), across) for d in docs],
        [(ff_two[d][0], (rows, width), still, ff_two[d][2], (rows, width), across) for d in docs],
        hidden // width,
        (width, width),
        "up_gradient",
    )
    stack = (1, rows, width)
    grad_squares = weight_product(
        flag,
        [
            (
                rights_one[d][0], stack, lambda j: ((j + 1) // 2, 0, 0),
                rights_one[d][1], stack, lambda j: (jnp.maximum(j - 1, 0), 0, 0),
            )
            for d in docs
        ],
        [
            (
                rights_two[d][0], stack, lambda j: (j // 3, 0, 0),
                rights_two[d][1], stack, lambda j: (j, 0, 0),
            )
            for d in docs
        ],
        4,
        (width, width),
        "square_gradients",
    )
    down_total = summed_over_documents(grad_down).astype(F32)
    up_total = summed_over_documents(grad_up).astype(F32)
    up_total = up_total.reshape(hidden // width, width, width).transpose(1, 0, 2)
    square_total = summed_over_documents(grad_squares).astype(F32)

    def small_of(parts):
        return jnp.concatenate([sum(p[i] for p in parts).reshape(-1) for i in range(5)])

    def stats_of(parts):
        return sum(jnp.concatenate(p, axis=0) for p in parts).sum(axis=1)

    small = jnp.where(first, small_of(small_one), small_of(small_two))
    count = jnp.sum(lengths).astype(F32)[None]
    shared = jnp.concatenate(
        [
            jnp.where(first, stats_of(stats_one), 0.0),
            jnp.where(first, 0.0, stats_of(stats_two)),
            jnp.where(first, 0.0, sum(rich_two).sum(axis=-1)).reshape(-1),
            jnp.where(first, 0.0, count),
        ]
    )
    packed = jnp.concatenate([small, shared])
    packed = jnp.pad(packed, (0, -packed.shape[0] % 1024))
    packed = exchanged_sum(exchanged_sum(packed, "core"), "chip")
    crossed = lax.ppermute(packed, "section", [(0, 1), (1, 0)])
    start = small.shape[0]
    shared = packed[start : start + shared.shape[0]] + crossed[start : start + shared.shape[0]]
    rms = jnp.sqrt(shared[:8].reshape(2, 4) / (shared[8 + 2 * heads] * width))
    rich_total = shared[8 : 8 + 2 * heads].reshape(2, heads)
    boundary_out = jnp.concatenate(
        [jnp.where(first, out_one[doc], out_two[doc]) for doc in range(documents)], axis=0
    )[None]
    return (
        boundary_out,
        square_total.reshape(1, 4, width, width),
        up_total.reshape(1, width, hidden),
        down_total[None],
        packed[:hidden][None],
        packed[hidden : hidden + 2 * width].reshape(1, 2, width),
        packed[hidden + 2 * width : hidden + 4 * width].reshape(1, 2, width),
        rich_total,
        rms,
    )


def solution(mesh):
    sections, dp = mesh.devices.shape
    split = Mesh(mesh.devices.reshape(sections, dp // 2, 2), ("section", "chip", "core"))
    data = ("chip", "core")
    in_specs = (
        P("section", data, None),
        P(data),
        P(data, None),
        P(data),
        P(data),
        P("section", None, None, None),
        P("section", None, None),
        P("section", None, None),
        P("section", None),
        P("section", None, None),
        P("section", None, None),
        P(),
    )
    out_specs = (
        P("section", data, None),
        P("section", None, None, None),
        P("section", None, None),
        P("section", None, None),
        P("section", None),
        P("section", None, None),
        P("section", None, None),
        P(),
        P(),
    )
    return jax.shard_map(local, mesh=split, in_specs=in_specs, out_specs=out_specs, check_vma=False)
```

time: 816 us -> 673 us (0.82)
  matrix products: 341 us -> 0 us
  Pallas kernels: 0 us -> 198 us
  other arithmetic: 145 us -> 35 us
  local copies, waits for them, and re-layouts: 57.9 us -> 136 us
  waiting for transfers between devices: 234 us -> 265 us
    dot_general x66 -> x0, matrix products: 302 us -> none  [the longest x22 94.1 us: product_right(): lax.dot_general(left, right, (((1,), (1,)), ((), ())), preferred_element_...]
    pallas_call x0 -> x19, Pallas kernels: none -> 198 us  [the longest x4 42.1 us: feed_forward(): kernel_call(feed_forward_body, (hidden // tile,), [whole((rows, width)),...]
    unnamed x382 -> x242, local copies, waits for them, and re-layouts: 18.8 us -> 98.7 us
    reduce_sum x16 -> x4, other arithmetic: 43.6 us -> 0.98 us  [the longest x1 0.63 us: local(): count = jnp.sum(lengths).astype(F32)[None]]
    sub x2 -> x0, matrix products: 39.1 us -> none  [attention_backward(): grad_scores = probs * (grad_probs - inner)]
    psum x1, waiting for transfers between devices: 205 us -> 237 us  [summed_over_documents(): part = lax.psum(part, 'chip')]
    sub x2 -> x0, other arithmetic: 30.5 us -> none  [attention_forward(): weights = jnp.exp(scores - jnp.max(scores, axis=-1, keepdims=True))]
    reshape x6 -> x2, local copies, waits for them, and re-layouts: 7.09 us -> 26 us  [local(): up_total.reshape(1, width, hidden)]
  transfers between devices with their start and end apart: 16 -> 16, of which waited for: 7 -> 7; matrix products, arithmetic and copies ran while one was open for 18% -> 9% of each run, Pallas kernels for 0% -> 12%
where the time goes in v2:
time: 673 us; the launch traced here: 666 us
  waiting for transfers between devices  265 us (39%)
  Pallas kernels  198 us (29%)
  local copies, waits for them, and re-layouts  136 us (20%)
  other arithmetic  35 us (5%)
  between operations  16.6 us (2%)
  starting transfers between devices  15 us (2%)
    psum x1, waiting for transfers between devices, summed_over_documents(): part = lax.psum(part, 'chip')  237 us
    unnamed x242, local copies, waits for them, and re-layouts  98.7 us
    pallas_call x4, Pallas kernels, feed_forward(): kernel_call(feed_forward_body, (hidden // tile,), [whole((rows, width)),...  42.1 us
    pallas_call x2, Pallas kernels, attend_backward(): kernel_call(attend_backward_body, (1,), [full, full, whole((2, width)), f...  38.8 us
    pallas_call x4, Pallas kernels, feed_backward(): kernel_call(feed_backward_body, (hidden // tile,), [part_of((rows, width)...  37.6 us
    pallas_call x2, Pallas kernels, attend_forward(): kernel_call(attend_forward_body, (1,), [full, part_of((1, rows), doc, 1),...  35.9 us
    reshape x2, local copies, waits for them, and re-layouts, local(): up_total.reshape(1, width, hidden)  26 us
    pallas_call x3, Pallas kernels, weight_product(): kernel_call(functools.partial(weight_body, count), (grid,), specs, [((gri...  21.8 us
  transfers between devices with their start and end apart: 16, of which 7 were waited for; matrix products, arithmetic and copies ran while one was open for 9% of the time, Pallas kernels for 12%

profile of v2, /device:TPU:0, one launch (start us, length us, event | category | flops | bytes accessed | tf_op | source)
XLA Modules:
  0.0 666.3 jit_solution(10542256582677941991)
XLA Ops:
  8.5 2.3 copy-done
  15.3 6.5 graph_forward.2
  24.9 2.9 copy-done.74
  27.8 11.2 %feed_forward.4 = (bf16[512,768]{1,0:T(8,128)(2,1)S(1)}, bf16[512,3072]{1,0:T(8,128)(2,1)S(1)}, bf16[512,3072]{1,0:T(8,128)(2,1)S(1)}, bf16[512,768]{1,0:T(8,128)(2,1)}, f32[2,768]{1,0:T(2,128)S(1)}) custom-call(s32[1]{0:T(128)} %get-tuple-element.196.length_ref, f32[512,768]{1,0:T(8,128)S(1)} %get-tuple-element.97.resid_ref, f32[2,768]{1,0:T(2,128)S(1)} %bitcast.52, ...), custom_call_target="tpu_custom_call" | custom-call | flops 4831838208 | bytes 18874368 | tf_op jit(solution)/shard_map/feed_forward/pallas_call | solution.py:130
  39.0 1.7 copy-done.5
  40.7 1.7 copy-done.87
  42.4 6.5 graph_forward.3
  55.3 10.2 %feed_forward.6 = (bf16[512,768]{1,0:T(8,128)(2,1)S(1)}, bf16[512,3072]{1,0:T(8,128)(2,1)S(1)}, bf16[512,3072]{1,0:T(8,128)(2,1)S(1)}, bf16[512,768]{1,0:T(8,128)(2,1)S(1)}, f32[2,768]{1,0:T(2,128)S(1)}) custom-call(s32[1]{0:T(128)} %get-tuple-element.197.length_ref, f32[512,768]{1,0:T(8,128)S(1)} %copy-done.98, f32[2,768]{1,0:T(2,128)S(1)} %bitcast.54, ...), custom_call_target="tpu_custom_call" | custom-call | flops 4831838208 | bytes 18874368 | tf_op jit(solution)/shard_map/feed_forward/pallas_call | solution.py:130
  68.8 4.9 collective-permute-start.2
  73.7 2.2 collective-permute-start
  75.9 15.7 %collective-permute-done.2.mid_ref = bf16[512,768]{1,0:T(8,128)(2,1)S(1)} collective-permute-done((bf16[512,768]{1,0:T(8,128)(2,1)S(1)}, bf16[512,768]{1,0:T(8,128)(2,1)S(1)}, u32[]{:S(2)}, u32[]{:S(2)}) %collective-permute-start.2) | collective-permute-done | bytes 786464 | tf_op jit(solution)/shard_map/ppermute | solution.py:630
  92.5 18.2 %attend_forward.3 = (bf16[2,512,768]{2,1,0:T(8,128)(2,1)}, bf16[512,768]{1,0:T(8,128)(2,1)}, bf16[512,768]{1,0:T(8,128)(2,1)}, bf16[512,768]{1,0:T(8,128)(2,1)},...) custom-call(s32[1]{0:T(128)} %get-tuple-element.197.length_ref, ...), custom_call_target="tpu_custom_call" | custom-call | flops 2919235584 | bytes 14155776 | tf_op jit(solution)/shard_map/attend_forward/pallas_call | solution.py:437
  110.7 2.3 copy-done.76
  114.4 10.2 %feed_forward.7 = (bf16[512,768]{1,0:T(8,128)(2,1)S(1)}, bf16[512,3072]{1,0:T(8,128)(2,1)S(1)}, bf16[512,3072]{1,0:T(8,128)(2,1)S(1)}, bf16[512,768]{1,0:T(8,128)(2,1)S(1)}, f32[2,768]{1,0:T(2,128)S(1)}) custom-call(s32[1]{0:T(128)} %get-tuple-element.197.length_ref, f32[512,768]{1,0:T(8,128)S(1)} %copy-done.91, f32[2,768]{1,0:T(2,128)S(1)} %bitcast.55, ...), custom_call_target="tpu_custom_call" | custom-call | flops 4831838208 | bytes 18874368 | tf_op jit(solution)/shard_map/feed_forward/pallas_call | solution.py:130
  128.0 1.7 copy-done.85
  129.7 17.7 %attend_forward.2 = (bf16[2,512,768]{2,1,0:T(8,128)(2,1)}, bf16[512,768]{1,0:T(8,128)(2,1)}, bf16[512,768]{1,0:T(8,128)(2,1)}, bf16[512,768]{1,0:T(8,128)(2,1)},...) custom-call(s32[1]{0:T(128)} %get-tuple-element.196.length_ref, ...), custom_call_target="tpu_custom_call" | custom-call | flops 2919235584 | bytes 14155776 | tf_op jit(solution)/shard_map/attend_forward/pallas_call | solution.py:437
  147.5 2.3 copy-done.77
  151.2 10.5 %feed_forward.5 = (bf16[512,768]{1,0:T(8,128)(2,1)S(1)}, bf16[512,3072]{1,0:T(8,128)(2,1)S(1)}, bf16[512,3072]{1,0:T(8,128)(2,1)S(1)}, bf16[512,768]{1,0:T(8,128)(2,1)S(1)}, f32[2,768]{1,0:T(2,128)S(1)}) custom-call(s32[1]{0:T(128)} %get-tuple-element.196.length_ref, f32[512,768]{1,0:T(8,128)S(1)} %copy-done.93, f32[2,768]{1,0:T(2,128)S(1)} %bitcast.56, ...), custom_call_target="tpu_custom_call" | custom-call | flops 4831838208 | bytes 18874368 | tf_op jit(solution)/shard_map/feed_forward/pallas_call | solution.py:130
  161.7 1.7 copy-done.12
  165.2 8.7 %feed_backward.4 = (bf16[512,3072]{1,0:T(8,128)(2,1)S(1)}, f32[1,3072]{1,0:T(1,128)S(1)}, f32[512,768]{1,0:T(8,128)S(1)}, f32[1,768]{1,0:T(1,128)S(1)}, f32[1,768]{1,0:T(1,128)S(1)}) custom-call(s32[1]{0:T(128)} %get-tuple-element.196.length_ref, bf16[1024,768]{1,0:T(8,128)(2,1)S(1)} %bitcast.41, f32[512,768]{1,0:T(8,128)S(1)} %copy-done.94, ...), custom_call_target="tpu_custom_call" | custom-call | flops 4831838208 | bytes 19660800 | tf_op jit(solution)/shard_map/feed_backward/pallas_call | solution.py:190
  173.9 1.7 copy-done.15
  176.8 19.4 %attend_backward.2 = (bf16[4,512,768]{2,1,0:T(8,128)(2,1)}, bf16[512,768]{1,0:T(8,128)(2,1)}, f32[2,12,128]{2,1,0:T(8,128)}, f32[1,768]{1,0:T(1,128)}, f32[1,768]{1,0:T(1,128)}) custom-call(s32[1]{0:T(128)} %get-tuple-element.196.length_ref, f32[512,768]{1,0:T(8,128)} %copy-done.37, bf16[512,768]{1,0:T(8,128)(2,1)} %collective-permute-done.mid_ref, ...), custom_call_target="tpu_custom_call" | custom-call | flops 3422552064 | bytes 15728640 | tf_op jit(solution)/shard_map/attend_backward/pallas_call | solution.py:547
  197.5 2.3 copy-done.78
  199.9 1.9 copy-done.86
  203.1 8.8 %feed_backward.5 = (bf16[512,3072]{1,0:T(8,128)(2,1)S(1)}, f32[1,3072]{1,0:T(1,128)S(1)}, f32[512,768]{1,0:T(8,128)S(1)}, f32[1,768]{1,0:T(1,128)S(1)}, f32[1,768]{1,0:T(1,128)S(1)}) custom-call(s32[1]{0:T(128)} %get-tuple-element.197.length_ref, bf16[1024,768]{1,0:T(8,128)(2,1)S(1)} %bitcast.42, f32[512,768]{1,0:T(8,128)S(1)} %copy-done.92, ...), custom_call_target="tpu_custom_call" | custom-call | flops 4831838208 | bytes 19660800 | tf_op jit(solution)/shard_map/feed_backward/pallas_call | solution.py:190
  214.7 19.4 %attend_backward.3 = (bf16[4,512,768]{2,1,0:T(8,128)(2,1)}, bf16[512,768]{1,0:T(8,128)(2,1)}, f32[2,12,128]{2,1,0:T(8,128)}, f32[1,768]{1,0:T(1,128)}, f32[1,768]{1,0:T(1,128)}) custom-call(s32[1]{0:T(128)} %get-tuple-element.197.length_ref, f32[512,768]{1,0:T(8,128)} %copy-done.38, bf16[512,768]{1,0:T(8,128)(2,1)} %copy-done.101, f32[2,768]{1,0:T(2,128)} %bitcast.50, ...), custom_call_target="tpu_custom_call" | custom-call | flops 3422552064 | bytes 15728640 | tf_op jit(solution)/shard_map/attend_backward/pallas_call | solution.py:547
  235.5 2.3 copy-done.73
  237.8 2.3 copy-done.79
  240.1 1.9 copy-done.88
  243.4 10.0 %feed_backward.6 = (bf16[512,3072]{1,0:T(8,128)(2,1)S(1)}, f32[1,3072]{1,0:T(1,128)S(1)}, f32[512,768]{1,0:T(8,128)S(1)}, f32[1,768]{1,0:T(1,128)S(1)}, f32[1,768]{1,0:T(1,128)S(1)}) custom-call(s32[1]{0:T(128)} %get-tuple-element.196.length_ref, bf16[512,768]{1,0:T(8,128)(2,1)} %collective-permute-done.1.grad_ref.refs_1_, f32[512,768]{1,0:T(8,128)S(1)} %copy-done.96, ...), custom_call_target="tpu_custom_call" | custom-call | flops 4831838208 | bytes 19660800 | tf_op jit(solution)/shard_map/feed_backward/pallas_call | solution.py:190
  257.7 10.1 %feed_backward.7 = (bf16[512,3072]{1,0:T(8,128)(2,1)S(1)}, f32[1,3072]{1,0:T(1,128)S(1)}, f32[512,768]{1,0:T(8,128)S(1)}, f32[1,768]{1,0:T(1,128)S(1)}, f32[1,768]{1,0:T(1,128)S(1)}) custom-call(s32[1]{0:T(128)} %get-tuple-element.197.length_ref, bf16[512,768]{1,0:T(8,128)(2,1)} %collective-permute-done.3.grad_ref.refs_3_, f32[512,768]{1,0:T(8,128)S(1)} %copy-done.99, ...), custom_call_target="tpu_custom_call" | custom-call | flops 4831838208 | bytes 19660800 | tf_op jit(solution)/shard_map/feed_backward/pallas_call | solution.py:190
  270.7 1.9 copy-done.18
  272.5 1.9 copy-done.20
  274.4 1.9 copy-done.22
  276.3 6.4 up_gradient.1
  284.4 1.9 copy-done.3
  286.3 2.1 copy-done.8
  288.4 1.9 copy-done.11
  290.3 1.9 copy-done.13
  292.2 8.4 %down_gradient.1 = bf16[3072,768]{1,0:T(8,128)(2,1)S(1)} custom-call(s32[1]{0:T(128)} %bitcast.10.flag_ref, bf16[512,3072]{1,0:T(8,128)(2,1)S(1)} %copy-done.6, bf16[512,768]{1,0:T(8,128)(2,1)} %collective-permute-done.1.grad_ref.refs_1_, bf16[512,3072]{1,0:T(8,128)(2,1)S(1)} %copy-done.8, bf16[512,768]{1,0:T(8,128)(2,1)} %collective-permute-done.3.grad_ref.refs_3_, ...), custom_call_target="tpu_custom_call" | custom-call | flops 4831838208 | bytes 13369344 | tf_op jit(solution)/shard_map/down_gradient/pallas_call | solution.py:614
  302.3 1.9 copy-done.4
  305.0 4.4 graph_backward.3
  315.4 4.5 graph_backward.2
  322.3 1.7 copy-done.26
  323.9 1.7 copy-done.28
  325.6 1.7 copy-done.30
  327.3 7.0 %square_gradients.1 = bf16[3072,768]{1,0:T(8,128)(2,1)} custom-call(s32[1]{0:T(128)} %bitcast.10.flag_ref, bf16[3,512,768]{2,1,0:T(8,128)(2,1)S(1)} %copy-done.24, bf16[3,512,768]{2,1,0:T(8,128)(2,1)S(1)} %copy-done.30, bf16[3,512,768]{2,1,0:T(8,128)(2,1)S(1)} %copy-done.26, bf16[3,512,768]{2,1,0:T(8,128)(2,1)S(1)} %copy-done.28, ...), custom_call_target="tpu_custom_call" | custom-call | flops 4831838208 | bytes 14155776 | tf_op jit(solution)/shard_map/square_gradients/pallas_call | solution.py:614
  334.3 3.3 constant_dynamic-slice_fusion.2
  337.6 4.6 dynamic-slice_add_fusion
  342.2 4.4 dynamic-slice_add_fusion.1
  346.6 2.0 dynamic-slice_add_fusion.2
  351.2 237.2 %all-reduce.4.cloned.1.call-done = (bf16[1536,768]{1,0:T(8,128)(2,1)}, bf16[1536,768]{1,0:T(8,128)(2,1)}, bf16[1536,768]{1,0:T(8,128)(2,1)}) async-done(((bf16[1536,768]{1,0:T(8,128)(2,1)}, bf16[1536,768]{1,0:T(8,128)(2,1)}, bf16[1536,768]{1,0:T(8,128)(2,1)}), (bf16[1536,768]{1,0:T(8,128)(2,1)}, bf16[1536,768]{1,0:T(8,128)(2,1)}, bf16[1536,768]{1,0:T(8,128)(2,1)})) %all-reduce.4.cloned.1.call-update) | async-done | bytes 7077904 | tf_op jit(solution)/shard_map/psum | solution.py:650
  589.1 3.4 collective-permute-done.10
  594.1 2.4 collective-permute-done.11
  596.7 3.6 collective-permute-done.12
  602.9 2.2 collective-permute-done.13
  611.6 2.7 broadcast_select_fusion.1
  614.6 4.6 convert_bitcast_fusion
  619.2 13.5 %copy.21 = f32[768,4,768]{2,1,0:T(4,128)} copy(f32[768,4,768]{2,0,1:T(8,128)} %convert_bitcast_fusion) | data formatting | bytes 18874368 | tf_op jit(solution)/shard_map/reshape | solution.py:829
  632.7 12.5 %reshape.141 = f32[1,768,3072]{2,1,0:T(8,128)} reshape(f32[768,4,768]{2,1,0:T(4,128)} %copy.21) | data formatting | bytes 18874368 | tf_op jit(solution)/shard_map/reshape | solution.py:829
  645.2 2.7 broadcast_select_fusion.3
  648.2 4.6 convert.5
  652.8 2.0 select_bitcast_fusion.1
  654.7 4.5 maximum_convert_fusion
  (284 shorter events, 69.6 us)
Async XLA Ops:
  7.2 581.2 %all-reduce.4.cloned.1.call-start = ((), (), s32[]{:S(2)}) async-start(), calls=%async_computation | async-start | bytes 14155776 | tf_op jit(solution)/shard_map/psum | solution.py:650
  15.3 9.6 %copy-start.72 = (bf16[1,768,3072]{2,1,0:T(8,128)(2,1)S(1)}, bf16[1,768,3072]{2,1,0:T(8,128)(2,1)}, u32[]{:S(2)}) copy-start(bf16[1,768,3072]{2,1,0:T(8,128)(2,1)} %param.18) | copy-start | bytes 14155780
  15.3 9.6 %copy-start.81 = (f32[1,3072]{1,0:T(1,128)S(1)}, f32[1,3072]{1,0:T(1,128)}, u32[]{:S(2)}) copy-start(f32[1,3072]{1,0:T(1,128)} %bias_ref.7) | copy-start | bytes 36868
  15.3 27.1 %slice-start = ((s8[4718592]{0:T(1024)(128)(4,1)}), s8[4194304]{0:T(1024)(128)(4,1)S(1)}, s32[]{:S(2)}) async-start(s8[4718592]{0:T(1024)(128)(4,1)} %bitcast.32), calls=%async_computation.1 | async-start | bytes 8388608
  24.9 14.1 %copy-start.95 = (f32[512,768]{1,0:T(8,128)}, f32[512,768]{1,0:T(8,128)S(1)}, u32[]{:S(2)}) copy-start(f32[512,768]{1,0:T(8,128)S(1)} %get-tuple-element.97.resid_ref) | copy-start | bytes 4718596
  24.9 2.9 copy-start.74
  27.8 14.6 %slice-start.1 = ((s8[4718592]{0:T(1024)(128)(4,1)}), s8[524288]{0:T(1024)(128)(4,1)S(1)}, s32[]{:S(2)}) async-start(s8[4718592]{0:T(1024)(128)(4,1)} %bitcast.32), calls=%async_computation.2 | async-start | bytes 1048576
  27.8 14.6 %copy-start.2 = (bf16[1,1024,768]{2,1,0:T(8,128)(2,1)S(1)}, bf16[1,1024,768]{2,1,0:T(8,128)(2,1)}, u32[]{:S(2)}) copy-start(bf16[1,1024,768]{2,1,0:T(8,128)(2,1)} %param.12) | copy-start | bytes 4718596
  42.4 11.5 %copy-start.75 = (bf16[1,3072,768]{2,1,0:T(8,128)(2,1)S(1)}, bf16[1,3072,768]{2,1,0:T(8,128)(2,1)}, u32[]{:S(2)}) copy-start(bf16[1,3072,768]{2,1,0:T(8,128)(2,1)} %param.19) | copy-start | bytes 14155780
  68.8 22.8 %collective-permute-start.2 = (bf16[512,768]{1,0:T(8,128)(2,1)S(1)}, bf16[512,768]{1,0:T(8,128)(2,1)S(1)}, u32[]{:S(2)}, u32[]{:S(2)}) collective-permute-start(bf16[512,768]{1,0:T(8,128)(2,1)S(1)} %get-tuple-element.110), channel_id=1, source_target_pairs={{0,16},{1,17},{2,18},{3,19},{4,20},{5,21},{6,22},{7,23},{8,24},{9,... | collective-permute-start | bytes 2359304 | tf_op jit(solution)/shard_map/ppermute | solution.py:630
  73.7 56.0 %collective-permute-start = (bf16[512,768]{1,0:T(8,128)(2,1)}, bf16[512,768]{1,0:T(8,128)(2,1)}, u32[]{:S(2)}, u32[]{:S(2)}) collective-permute-start(bf16[512,768]{1,0:T(8,128)(2,1)} %get-tuple-element.98), channel_id=1, source_target_pairs={{0,16},{1,17},{2,18},{3,19},{4,20},{5,21},{6,22},{7,23},{8,24},{9,... | collective-permute-start | bytes 2359304 | tf_op jit(solution)/shard_map/ppermute | solution.py:630
  92.5 18.2 %copy-start.62 = (f32[1,2,768]{2,1,0:T(2,128)S(1)}, f32[1,2,768]{2,1,0:T(2,128)}, u32[]{:S(2)}) copy-start(f32[1,2,768]{2,1,0:T(2,128)} %param.21) | copy-start | bytes 18436
  92.5 18.2 %copy-start.83 = (f32[1,2,768]{2,1,0:T(2,128)S(1)}, f32[1,2,768]{2,1,0:T(2,128)}, u32[]{:S(2)}) copy-start(f32[1,2,768]{2,1,0:T(2,128)} %param.22) | copy-start | bytes 18436
  129.7 17.7 %copy-start.63 = (f32[1,2,768]{2,1,0:T(2,128)S(1)}, f32[1,2,768]{2,1,0:T(2,128)}, u32[]{:S(2)}) copy-start(f32[1,2,768]{2,1,0:T(2,128)} %param.21) | copy-start | bytes 18436
  129.7 17.7 %copy-start.84 = (f32[1,2,768]{2,1,0:T(2,128)S(1)}, f32[1,2,768]{2,1,0:T(2,128)}, u32[]{:S(2)}) copy-start(f32[1,2,768]{2,1,0:T(2,128)} %param.22) | copy-start | bytes 18436
  151.2 14.0 %copy-start.94 = (f32[512,768]{1,0:T(8,128)S(1)}, f32[512,768]{1,0:T(8,128)}, u32[]{:S(2)}) copy-start(f32[512,768]{1,0:T(8,128)} %get-tuple-element.99.resid_ref) | copy-start | bytes 4718596
  176.8 20.7 %copy-start.64 = (f32[1,2,768]{2,1,0:T(2,128)S(1)}, f32[1,2,768]{2,1,0:T(2,128)}, u32[]{:S(2)}) copy-start(f32[1,2,768]{2,1,0:T(2,128)} %param.21) | copy-start | bytes 18436
  196.2 39.2 %collective-permute-start.1 = (bf16[512,768]{1,0:T(8,128)(2,1)}, bf16[512,768]{1,0:T(8,128)(2,1)}, u32[]{:S(2)}, u32[]{:S(2)}) collective-permute-start(bf16[512,768]{1,0:T(8,128)(2,1)} %get-tuple-element.107), channel_id=1, source_target_pairs={{16,0},{17,1},{18,2},{19,3},{20,4},{21,5},{22,6},{23,7},{24,8},{25... | collective-permute-start | bytes 2359304 | tf_op jit(solution)/shard_map/ppermute | solution.py:630
  214.7 20.7 %copy-start.65 = (f32[1,2,768]{2,1,0:T(2,128)S(1)}, f32[1,2,768]{2,1,0:T(2,128)}, u32[]{:S(2)}) copy-start(f32[1,2,768]{2,1,0:T(2,128)} %param.21) | copy-start | bytes 18436
  234.1 22.2 %collective-permute-start.3 = (bf16[512,768]{1,0:T(8,128)(2,1)}, bf16[512,768]{1,0:T(8,128)(2,1)}, u32[]{:S(2)}, u32[]{:S(2)}) collective-permute-start(bf16[512,768]{1,0:T(8,128)(2,1)} %get-tuple-element.119), channel_id=1, source_target_pairs={{16,0},{17,1},{18,2},{19,3},{20,4},{21,5},{22,6},{23,7},{24,8},{25... | collective-permute-start | bytes 2359304 | tf_op jit(solution)/shard_map/ppermute | solution.py:630
  243.4 12.9 %copy-start.90 = (bf16[512,3072]{1,0:T(8,128)(2,1)S(1)}, bf16[512,3072]{1,0:T(8,128)(2,1)}, u32[]{:S(2)}) copy-start(bf16[512,3072]{1,0:T(8,128)(2,1)} %copy-done.89) | copy-start | bytes 9437188
  257.7 12.9 %copy-start.16 = (bf16[512,3072]{1,0:T(8,128)(2,1)S(1)}, bf16[512,3072]{1,0:T(8,128)(2,1)}, u32[]{:S(2)}) copy-start(bf16[512,3072]{1,0:T(8,128)(2,1)} %copy-done.15) | copy-start | bytes 9437188
  257.7 12.9 %copy-start.40 = (bf16[512,768]{1,0:T(8,128)(2,1)S(1)}, bf16[512,768]{1,0:T(8,128)(2,1)}, u32[]{:S(2)}) copy-start(bf16[512,768]{1,0:T(8,128)(2,1)} %copy-done.39) | copy-start | bytes 2359300
  257.7 12.9 %copy-start.42 = (bf16[512,768]{1,0:T(8,128)(2,1)S(1)}, bf16[512,768]{1,0:T(8,128)(2,1)}, u32[]{:S(2)}) copy-start(bf16[512,768]{1,0:T(8,128)(2,1)} %copy-done.41) | copy-start | bytes 2359300
  276.3 10.0 %copy-start.6 = (bf16[512,3072]{1,0:T(8,128)(2,1)S(1)}, bf16[512,3072]{1,0:T(8,128)(2,1)}, u32[]{:S(2)}) copy-start(bf16[512,3072]{1,0:T(8,128)(2,1)} %copy-done.5) | copy-start | bytes 9437188
  282.7 3.5 copy-start.3
  282.8 21.9 %slice-start.2 = ((s8[4718592]{0:T(1024)(128)(4,1)}), s8[4194304]{0:T(1024)(128)(4,1)S(1)}, s32[]{:S(2)}) async-start(s8[4718592]{0:T(1024)(128)(4,1)} %bitcast.35), calls=%async_computation.3 | async-start | bytes 8388608
  292.2 12.4 %slice-start.3 = ((s8[4718592]{0:T(1024)(128)(4,1)}), s8[524288]{0:T(1024)(128)(4,1)S(1)}, s32[]{:S(2)}) async-start(s8[4718592]{0:T(1024)(128)(4,1)} %bitcast.35), calls=%async_computation.4 | async-start | bytes 1048576
  300.6 3.5 copy-start.4
  300.6 4.0 copy-start.36
  300.6 4.0 copy-start.56
  300.6 4.1 copy-start.58
  300.6 4.4 copy-start.60
  300.6 4.3 copy-start.67
  304.1 33.5 %collective-permute-start.8 = (bf16[1536,768]{1,0:T(8,128)(2,1)}, bf16[1536,768]{1,0:T(8,128)(2,1)}, u32[]{:S(2)}, u32[]{:S(2)}) collective-permute-start(bf16[1536,768]{1,0:T(8,128)(2,1)} %constant_dynamic-slice_fusion), channel_id=1, source_target_pairs={{0,1},{1,0},{2,3},{3,2},{4,5},{5,4},{6,7},{7,6},{8,9},{9,8},{10,11... | collective-permute-start | bytes 7077896 | tf_op jit(solution)/shard_map/ppermute | solution.py:649
  304.1 38.0 %collective-permute-start.6 = (bf16[1536,768]{1,0:T(8,128)(2,1)}, bf16[1536,768]{1,0:T(8,128)(2,1)}, u32[]{:S(2)}, u32[]{:S(2)}) collective-permute-start(bf16[1536,768]{1,0:T(8,128)(2,1)} %constant_dynamic-slice_fusion.1), channel_id=1, source_target_pairs={{0,1},{1,0},{2,3},{3,2},{4,5},{5,4},{6,7},{7,6},{8,9},{9,8},{10,11... | collective-permute-start | bytes 7077896 | tf_op jit(solution)/shard_map/ppermute | solution.py:649
  305.0 17.2 %copy-start.31 = (bf16[2,512,768]{2,1,0:T(8,128)(2,1)S(1)}, bf16[2,512,768]{2,1,0:T(8,128)(2,1)}, u32[]{:S(2)}) copy-start(bf16[2,512,768]{2,1,0:T(8,128)(2,1)} %get-tuple-element.141.refs_6_) | copy-start | bytes 4718596
  305.0 17.2 %copy-start.32 = (bf16[2,512,768]{2,1,0:T(8,128)(2,1)S(1)}, bf16[2,512,768]{2,1,0:T(8,128)(2,1)}, u32[]{:S(2)}) copy-start(bf16[2,512,768]{2,1,0:T(8,128)(2,1)} %get-tuple-element.139.refs_4_) | copy-start | bytes 4718596
  315.4 6.9 %copy-start.9 = (bf16[4,512,768]{2,1,0:T(8,128)(2,1)S(1)}, bf16[4,512,768]{2,1,0:T(8,128)(2,1)}, u32[]{:S(2)}) copy-start(bf16[4,512,768]{2,1,0:T(8,128)(2,1)} %get-tuple-element.140.refs_5_) | copy-start | bytes 9437188
  315.4 6.9 %copy-start.14 = (bf16[4,512,768]{2,1,0:T(8,128)(2,1)S(1)}, bf16[4,512,768]{2,1,0:T(8,128)(2,1)}, u32[]{:S(2)}) copy-start(bf16[4,512,768]{2,1,0:T(8,128)(2,1)} %get-tuple-element.142.refs_7_) | copy-start | bytes 9437188
  315.4 6.9 %copy-start.24 = (bf16[3,512,768]{2,1,0:T(8,128)(2,1)S(1)}, bf16[3,512,768]{2,1,0:T(8,128)(2,1)}, u32[]{:S(2)}) copy-start(bf16[3,512,768]{2,1,0:T(8,128)(2,1)} %copy-done.23) | copy-start | bytes 7077892
  322.2 12.1 %copy-start.68 = (f32[1,768]{1,0:T(1,128)}, f32[1,768]{1,0:T(1,128)S(1)}, u32[]{:S(2)}) copy-start(f32[1,768]{1,0:T(1,128)S(1)} %get-tuple-element.157) | copy-start | bytes 9220
  322.2 12.1 %copy-start.70 = (f32[1,768]{1,0:T(1,128)}, f32[1,768]{1,0:T(1,128)S(1)}, u32[]{:S(2)}) copy-start(f32[1,768]{1,0:T(1,128)S(1)} %get-tuple-element.161) | copy-start | bytes 9220
  334.3 12.2 %slice-start.4 = ((s8[4718592]{0:T(1024)(128)(4,1)}), s8[524288]{0:T(1024)(128)(4,1)S(1)}, s32[]{:S(2)}) async-start(s8[4718592]{0:T(1024)(128)(4,1)} %bitcast.93), calls=%async_computation.5 | async-start | bytes 1048576
  337.6 8.9 %collective-permute-start.4 = (bf16[1536,768]{1,0:T(8,128)(2,1)}, bf16[1536,768]{1,0:T(8,128)(2,1)S(1)}, u32[]{:S(2)}, u32[]{:S(2)}) collective-permute-start(bf16[1536,768]{1,0:T(8,128)(2,1)} %constant_dynamic-slice_fusion.2), channel_id=1, source_target_pairs={{0,1},{1,0},{2,3},{3,2},{4,5},{5,4},{6,7},{7,6},{8,9},{9,8},{10,11... | collective-permute-start | bytes 7077896 | tf_op jit(solution)/shard_map/ppermute | solution.py:649
  337.6 9.0 %slice-start.5 = ((s8[4718592]{0:T(1024)(128)(4,1)}), s8[4194304]{0:T(1024)(128)(4,1)S(1)}, s32[]{:S(2)}) async-start(s8[4718592]{0:T(1024)(128)(4,1)} %bitcast.93), calls=%async_computation.6 | async-start | bytes 8388608
  348.6 2.4 copy-start.106
  348.6 2.4 copy-start.107
  348.6 2.4 copy-start.108
  348.6 239.8 %copy-start.69 = (f32[1,768]{1,0:T(1,128)S(1)}, f32[1,768]{1,0:T(1,128)}, u32[]{:S(2)}) copy-start(f32[1,768]{1,0:T(1,128)} %copy-done.68) | copy-start | bytes 9220
  348.6 239.8 %copy-start.71 = (f32[1,768]{1,0:T(1,128)S(1)}, f32[1,768]{1,0:T(1,128)}, u32[]{:S(2)}) copy-start(f32[1,768]{1,0:T(1,128)} %copy-done.70) | copy-start | bytes 9220
  348.6 247.9 %copy-start.44 = (bf16[512,768]{1,0:T(8,128)(2,1)S(1)}, bf16[512,768]{1,0:T(8,128)(2,1)}, u32[]{:S(2)}) copy-start(bf16[512,768]{1,0:T(8,128)(2,1)} %copy-done.43) | copy-start | bytes 2359300
  348.6 247.9 %copy-start.46 = (bf16[512,768]{1,0:T(8,128)(2,1)S(1)}, bf16[512,768]{1,0:T(8,128)(2,1)}, u32[]{:S(2)}) copy-start(bf16[512,768]{1,0:T(8,128)(2,1)} %copy-done.45) | copy-start | bytes 2359300
  348.7 247.9 %copy-start.48 = (bf16[512,768]{1,0:T(8,128)(2,1)S(1)}, bf16[512,768]{1,0:T(8,128)(2,1)}, u32[]{:S(2)}) copy-start(bf16[512,768]{1,0:T(8,128)(2,1)} %copy-done.47) | copy-start | bytes 2359300
  348.7 247.9 %copy-start.50 = (bf16[512,768]{1,0:T(8,128)(2,1)S(1)}, bf16[512,768]{1,0:T(8,128)(2,1)}, u32[]{:S(2)}) copy-start(bf16[512,768]{1,0:T(8,128)(2,1)} %copy-done.49) | copy-start | bytes 2359300
  588.4 23.3 %collective-permute-start.7 = (bf16[1536,768]{1,0:T(8,128)(2,1)}, bf16[1536,768]{1,0:T(8,128)(2,1)}, u32[]{:S(2)}, u32[]{:S(2)}) collective-permute-start(bf16[1536,768]{1,0:T(8,128)(2,1)} %get-tuple-element.186), channel_id=1, source_target_pairs={{0,1},{1,0},{2,3},{3,2},{4,5},{5,4},{6,7},{7,6},{8,9},{9,8},{10,11... | collective-permute-start | bytes 7077896 | tf_op jit(solution)/shard_map/ppermute | solution.py:651
  588.6 4.0 collective-permute-start.10
  592.6 3.9 collective-permute-start.11
  596.5 3.9 collective-permute-start.12
  596.7 14.9 %copy-start.100 = (bf16[1536,768]{1,0:T(8,128)(2,1)S(1)}, bf16[1536,768]{1,0:T(8,128)(2,1)}, u32[]{:S(2)}) copy-start(bf16[1536,768]{1,0:T(8,128)(2,1)} %get-tuple-element.187) | copy-start | bytes 7077892
  600.4 4.8 collective-permute-start.13
  605.1 3.9 collective-permute-start.14
  606.6 38.6 %collective-permute-start.5 = (bf16[1536,768]{1,0:T(8,128)(2,1)}, bf16[1536,768]{1,0:T(8,128)(2,1)}, u32[]{:S(2)}, u32[]{:S(2)}) collective-permute-start(bf16[1536,768]{1,0:T(8,128)(2,1)} %get-tuple-element.185), channel_id=1, source_target_pairs={{0,1},{1,0},{2,3},{3,2},{4,5},{5,4},{6,7},{7,6},{8,9},{9,8},{10,11... | collective-permute-start | bytes 7077896 | tf_op jit(solution)/shard_map/ppermute | solution.py:651
  611.6 41.1 %collective-permute-start.9 = (bf16[1536,768]{1,0:T(8,128)(2,1)S(1)}, bf16[1536,768]{1,0:T(8,128)(2,1)}, u32[]{:S(2)}, u32[]{:S(2)}) collective-permute-start(bf16[1536,768]{1,0:T(8,128)(2,1)S(1)} %copy-done.100), channel_id=1, source_target_pairs={{0,1},{1,0},{2,3},{3,2},{4,5},{5,4},{6,7},{7,6},{8,9},{9,8},{10,11... | collective-permute-start | bytes 7077896 | tf_op jit(solution)/shard_map/ppermute | solution.py:651
  (69 other events, 103.0 us)
Sparse Core Ops, SparseCore 0:
  348.8 239.5 all-reduce.3

commit v3 on v2

v3 whole, which is shorter than its diff:
```python
import functools
import jax
import jax.numpy as jnp
from jax import lax
from jax.sharding import Mesh, PartitionSpec as P
from jax.experimental import pallas as pl
from jax.experimental.pallas import tpu as pltpu

RADIUS = 128
REACH = 64
QUERY_BLOCK = 128
EPSILON = 1e-05
NEG_FILL = -1e30
HIDDEN_TILE = 1024
GELU_C = 0.7978845608028654
F32, BF16 = jnp.float32, jnp.bfloat16
MIB = 1024 * 1024


def low(vector):
    return vector.astype(BF16)


def dot_nn(left, right):
    return jnp.dot(left, right, preferred_element_type=F32)


def dot_nt(left, right):
    return lax.dot_general(left, right, (((1,), (1,)), ((), ())), preferred_element_type=F32)


def dot_tn(left, right):
    return lax.dot_general(left, right, (((0,), (0,)), ((), ())), preferred_element_type=F32)


def normalized(vector):
    center = vector - jnp.mean(vector, axis=-1, keepdims=True)
    inverse = lax.rsqrt(jnp.mean(center * center, axis=-1, keepdims=True) + EPSILON)
    return center * inverse, inverse


def norm_backward(vector, gain_row, grad_normed):
    normed, inverse = normalized(vector)
    scaled = grad_normed * gain_row
    mean_scaled = jnp.mean(scaled, axis=-1, keepdims=True)
    mean_mixed = jnp.mean(scaled * normed, axis=-1, keepdims=True)
    grad_input = inverse * (scaled - mean_scaled - normed * mean_mixed)
    grad_gain = jnp.sum(grad_normed * normed, axis=0, keepdims=True)
    return grad_input, grad_gain, jnp.sum(grad_normed, axis=0, keepdims=True)


def live_sums(length, start, items):
    rows = items[0].shape[0]
    live = start + lax.broadcasted_iota(jnp.int32, (rows, 1), 0) < length
    return [jnp.sum(jnp.where(live, v * v, 0.0), axis=0, keepdims=True) for v in items]


def whole(shape):
    return pl.BlockSpec(shape, lambda *_: (0,) * len(shape))


def part_of(shape, doc, axis):
    place = tuple(doc if d == axis else 0 for d in range(len(shape)))
    return pl.BlockSpec(shape, lambda *_: place)


def column(row):
    return jnp.broadcast_to(row, (row.shape[1], row.shape[1])).T[:, 0:1]


def kernel_call(body, grid, in_specs, outs, scratch, flops, moved, name, aliases=None):
    return pl.pallas_call(
        body,
        out_shape=[jax.ShapeDtypeStruct(shape, kind) for shape, kind, _ in outs],
        grid_spec=pltpu.PrefetchScalarGridSpec(
            num_scalar_prefetch=1,
            grid=grid,
            in_specs=in_specs,
            out_specs=[spec for _, _, spec in outs],
            scratch_shapes=scratch,
        ),
        compiler_params=pltpu.CompilerParams(
            dimension_semantics=("arbitrary",) * len(grid), vmem_limit_bytes=60 * MIB
        ),
        cost_estimate=pl.CostEstimate(
            flops=int(flops) * 1, bytes_accessed=int(moved) * 1, transcendentals=0
        ),
        input_output_aliases=aliases or {},
        name=name,
    )


ANYWHERE = pl.BlockSpec(memory_space=pl.ANY)
PARTS = 2


def row_parts(rows):
    return [(at, pl.ds(at, rows // PARTS)) for at in range(0, rows, rows // PARTS)]


class Copies:
    def __init__(self, semaphores):
        self.semaphores, self.used, self.pending = semaphores, 0, []

    def start(self, source, target):
        copy = pltpu.make_async_copy(source, target, self.semaphores.at[self.used])
        self.used += 1
        copy.start()
        return copy

    def leave(self, source, target):
        self.pending.append(self.start(source, target))

    def finish(self):
        for copy in self.pending:
            copy.wait()


def add_rows(ref, rows, values):
    for at, value in zip(rows, values):
        ref[at : at + 1, :] += value


def feed_forward(resid_ref, gain, shift, up_ref, bias_ref, down_ref, normed_ref, active_ref, slope_ref, sum_ref):
    rows, hidden = active_ref.shape
    for _, own in row_parts(rows):
        normed_ref[own, :] = low(normalized(resid_ref[own, :])[0] * gain + shift)
    sum_ref[...] = jnp.zeros_like(sum_ref)

    def tile(index, carry):
        columns = pl.ds(pl.multiple_of(index * HIDDEN_TILE, HIDDEN_TILE), HIDDEN_TILE)
        for _, own in row_parts(rows):
            pre = dot_nn(normed_ref[own, :], up_ref[:, columns]) + bias_ref[:, columns]
            square = pre * pre
            curve = jnp.tanh(pre * (GELU_C + GELU_C * 0.044715 * square))
            half = 0.5 + 0.5 * curve
            active = low(pre * half)
            active_ref[own, columns] = active
            rise = pre * (GELU_C + 3.0 * GELU_C * 0.044715 * square)
            slope_ref[own, columns] = low(half + rise * (half - half * half) * 2.0)
            sum_ref[own, :] += dot_nn(active, down_ref[columns, :])
        return carry

    lax.fori_loop(0, hidden // HIDDEN_TILE, tile, 0)


def feed_backward_tile(columns, grad_ref, slope_ref, up_ref, down_ref, pre_ref, bias_ref, sum_ref):
    total = None
    for _, own in row_parts(grad_ref.shape[0]):
        grad_active = dot_nt(grad_ref[own, :], down_ref[columns, :])
        grad_pre = low(slope_ref[own, columns].astype(F32) * grad_active)
        pre_ref[own, columns] = grad_pre
        here = jnp.sum(grad_pre.astype(F32), axis=0, keepdims=True)
        total = here if total is None else total + here
        sum_ref[own, :] += dot_nt(grad_pre, up_ref[:, columns])
    bias_ref[:, columns] = total


def norm_back(out_ref, grad_ref, vector_ref, gain, sum_ref, gain_ref, shift_ref, at):
    gain_ref[at : at + 1, :] = jnp.zeros_like(gain)
    shift_ref[at : at + 1, :] = jnp.zeros_like(gain)
    for _, own in row_parts(out_ref.shape[0]):
        grad_input, grad_gain, grad_shift = norm_backward(vector_ref[own, :].astype(F32), gain, sum_ref[own, :])
        out_ref[own, :] = (grad_ref[own, :].astype(F32) + grad_input).astype(out_ref.dtype)
        gain_ref[at : at + 1, :] += grad_gain
        shift_ref[at : at + 1, :] += grad_shift


def graph_windows(rows):
    span = QUERY_BLOCK + 2 * REACH
    return [
        (start, min(max(start - REACH, 0), rows - span), span)
        for start in range(0, rows, QUERY_BLOCK)
    ]


def layer_one_forward_body(
    length_ref, x_ref, near_ref_t, counts_ref, gain_ref, shift_ref, bias_ref, w_any, up_any, down_any,
    mid_ref, stat_ref, link_ref, left_any, sigma_any, pull_any, resid_any, normed_any, active_any, slope_any,
    w_ref, up_ref, down_ref, left_ref, sigma_ref, pull_ref, resid_ref, normed_ref, active_ref, slope_ref, sum_ref,
    semaphores,
):
    rows, width = x_ref.shape
    length = length_ref[0]
    copies = Copies(semaphores)
    w_copies = [copies.start(w_any.at[i], w_ref.at[i]) for i in range(4)]
    up_copy, down_copy = copies.start(up_any, up_ref), copies.start(down_any, down_ref)
    graph_normed, mean_ref, mixed_ref = (left_ref.at[i] for i in range(3))
    stat_ref[...] = jnp.zeros_like(stat_ref)
    for _, own in row_parts(rows):
        graph_normed[own, :] = low(
            normalized(x_ref[own, :].astype(F32))[0] * gain_ref[0:1, :] + shift_ref[0:1, :]
        )
    slots = near_ref_t.shape[0]
    slot = lax.broadcasted_iota(jnp.int32, (slots, QUERY_BLOCK), 0)
    for row, start, span in graph_windows(rows):
        own = pl.ds(row, QUERY_BLOCK)
        counts = counts_ref[:, own]
        index = jnp.where(slot < counts, near_ref_t[:, own], -1)
        place = start + lax.broadcasted_iota(jnp.int32, (span, QUERY_BLOCK), 0)
        links = jnp.zeros((span, QUERY_BLOCK), F32)
        for s in range(slots):
            links += jnp.where(index[s : s + 1, :] == place, 1.0, 0.0)
        link_ref[:, own] = low(links)
        total = dot_nn(low(links.T), graph_normed[pl.ds(start, span), :])
        mean_ref[own, :] = low(total / column(counts.astype(F32)))
    for copy in w_copies:
        copy.wait()
    for at, own in row_parts(rows):
        pre = dot_nn(graph_normed[own, :], w_ref[0]) + dot_nn(mean_ref[own, :], w_ref[1])
        sigma = jax.nn.sigmoid(dot_nn(mean_ref[own, :], w_ref[2]))
        mixed = pre * sigma
        sigma_ref[own, :] = low(sigma)
        pull_ref[own, :] = low(mixed - mixed * sigma)
        mixed_ref[own, :] = low(mixed)
        branch = dot_nn(low(mixed), w_ref[3])
        resid = x_ref[own, :].astype(F32) + branch
        resid_ref[own, :] = resid
        add_rows(stat_ref, (0, 1), live_sums(length, at, (branch, resid)))
    copies.leave(left_ref, left_any)
    copies.leave(sigma_ref, sigma_any)
    copies.leave(pull_ref, pull_any)
    copies.leave(resid_ref, resid_any)
    up_copy.wait()
    down_copy.wait()
    feed_forward(
        resid_ref, gain_ref[1:2, :], shift_ref[1:2, :], up_ref, bias_ref, down_ref,
        normed_ref, active_ref, slope_ref, sum_ref,
    )
    copies.leave(normed_ref, normed_any)
    copies.leave(active_ref, active_any)
    copies.leave(slope_ref, slope_any)
    for at, own in row_parts(rows):
        branch = sum_ref[own, :]
        result = resid_ref[own, :] + branch
        mid_ref[own, :] = low(result)
        add_rows(stat_ref, (2, 3), live_sums(length, at, (branch, result)))
    copies.finish()


def layer_one_forward(length, x, doc, rows, near_t, counts, gain, shift, bias, weights, up, down):
    width, hidden = up.shape
    slots = near_t.shape[0]
    span = QUERY_BLOCK + 2 * REACH
    flat, wide = ((rows, width), BF16), ((rows, hidden), BF16)
    kept = [((3, rows, width), BF16), flat, flat, ((rows, width), F32), flat, wide, wide]
    return kernel_call(
        layer_one_forward_body,
        (1,),
        [
            part_of((rows, width), doc, 0), part_of((slots, rows), doc, 1), part_of((1, rows), doc, 1),
            whole((2, width)), whole((2, width)), whole((1, hidden)), ANYWHERE, ANYWHERE, ANYWHERE,
        ],
        [
            ((rows, width), BF16, whole((rows, width))),
            ((4, width), F32, whole((4, width))),
            ((span, rows), BF16, whole((span, rows))),
        ]
        + [(*what, ANYWHERE) for what in kept],
        [pltpu.VMEM(v.shape, BF16) for v in (weights, up, down)]
        + [pltpu.VMEM(*what) for what in kept]
        + [pltpu.VMEM((rows, width), F32), pltpu.SemaphoreType.DMA((13,))],
        8 * rows * width * width + 4 * rows * width * hidden,
        16 * rows * width + 8 * width * width + 4 * (rows + width) * hidden,
        "layer_one_forward",
    )(length, x, near_t, counts, gain, shift, bias, weights, up, down)


def layer_one_backward_body(
    length_ref, grad_ref, x_ref, gain_ref, counts_ref, link_ref,
    resid_any, slope_any, sigma_any, pull_any, w_any, up_any, down_any,
    out_ref, bias_out, gain_out, shift_out, pre_any, right_any,
    resid_ref, slope_ref, sigma_ref, pull_ref, w_ref, up_ref, down_ref,
    pre_ref, right_ref, grad_resid, mean_ref, sum_ref,
    semaphores,
):
    rows, width = x_ref.shape
    hidden = slope_ref.shape[1]
    copies = Copies(semaphores)
    tiles = [pl.ds(at, HIDDEN_TILE) for at in range(0, hidden, HIDDEN_TILE)]
    arriving = [
        [
            copies.start(down_any.at[columns, :], down_ref.at[columns, :]),
            copies.start(slope_any.at[:, columns], slope_ref.at[:, columns]),
            copies.start(up_any.at[:, columns], up_ref.at[:, columns]),
        ]
        for columns in tiles
    ]
    resid_copy = copies.start(resid_any, resid_ref)
    w_copies = [copies.start(w_any.at[i], w_ref.at[i]) for i in range(4)]
    gate_copies = [copies.start(sigma_any, sigma_ref), copies.start(pull_any, pull_ref)]
    counts_column = column(counts_ref[...].astype(F32))
    sum_ref[...] = jnp.zeros_like(sum_ref)
    for columns, parts in zip(tiles, arriving):
        for copy in parts:
            copy.wait()
        feed_backward_tile(columns, grad_ref, slope_ref, up_ref, down_ref, pre_ref, bias_out, sum_ref)
    copies.leave(pre_ref, pre_any)
    resid_copy.wait()
    norm_back(grad_resid, grad_ref, resid_ref, gain_ref[1:2, :], sum_ref, gain_out, shift_out, 1)
    for copy in w_copies + gate_copies:
        copy.wait()
    for at, own in row_parts(rows):
        grad_low = low(grad_resid[own, :])
        right_ref[2, own, :] = grad_low
        grad_mixed = dot_nt(grad_low, w_ref[3])
        grad_pre = low(sigma_ref[own, :].astype(F32) * grad_mixed)
        grad_gate = low(pull_ref[own, :].astype(F32) * grad_mixed)
        right_ref[0, own, :] = grad_pre
        right_ref[1, own, :] = grad_gate
        sum_ref[own, :] = dot_nt(grad_pre, w_ref[0])
        grad_mean = dot_nt(grad_pre, w_ref[1]) + dot_nt(grad_gate, w_ref[2])
        mean_ref[own, :] = low(grad_mean / counts_column[at : at + rows // PARTS, :])
    copies.leave(right_ref, right_any)
    for row, start, span in graph_windows(rows):
        own = pl.ds(row, QUERY_BLOCK)
        sum_ref[pl.ds(start, span), :] += dot_nn(link_ref[:, own], mean_ref[own, :])
    norm_back(out_ref, grad_resid, x_ref, gain_ref[0:1, :], sum_ref, gain_out, shift_out, 0)
    copies.finish()


def layer_one_backward(length, grad, x, doc, gain, counts, links, resid, slope, sigma, pull, weights, up, down):
    rows, width = grad.shape
    hidden = slope.shape[1]
    full = whole((rows, width))
    sent = [((rows, hidden), BF16), ((3, rows, width), BF16)]
    return kernel_call(
        layer_one_backward_body,
        (1,),
        [
            full, part_of((rows, width), doc, 0), whole((2, width)), part_of((1, rows), doc, 1), whole(links.shape),
        ]
        + [ANYWHERE] * 7,
        [
            ((rows, width), BF16, full),
            ((1, hidden), F32, whole((1, hidden))),
            ((2, width), F32, whole((2, width))),
            ((2, width), F32, whole((2, width))),
        ]
        + [(*what, ANYWHERE) for what in sent],
        [pltpu.VMEM(v.shape, v.dtype) for v in (resid, slope, sigma, pull, weights, up, down)]
        + [pltpu.VMEM(*what) for what in sent]
        + [
            pltpu.VMEM((rows, width), F32),
            pltpu.VMEM((rows, width), BF16),
            pltpu.VMEM((rows, width), F32),
            pltpu.SemaphoreType.DMA((3 * (hidden // HIDDEN_TILE) + 9,)),
        ],
        8 * rows * width * width + 4 * rows * width * hidden,
        18 * rows * width + 8 * width * width + 4 * (rows + width) * hidden,
        "layer_one_backward",
    )(length, grad, x, gain, counts, links, resid, slope, sigma, pull, weights, up, down)


def attend_windows(rows):
    windows, offset = [], 0
    for row in range(0, rows, QUERY_BLOCK):
        start = max(row - RADIUS, 0)
        span = min(row + QUERY_BLOCK + RADIUS, rows) - start
        windows.append((row, start, span, offset))
        offset += span
    return windows, offset


def two_heads(block, lane):
    zero = jnp.zeros_like(block)
    return jnp.concatenate([jnp.where(lane, block, zero), jnp.where(lane, zero, block)], axis=0)


def layer_two_body(
    length_ref, mid_ref, cotangent_ref, coords_ref, rich_ref, gain_ref, shift_ref, bias_ref, w_any, up_any, down_any,
    out_ref, result_ref, stat_ref, bias_out, gain_out, shift_out, rich_out,
    left_any, right_any, normed_any, active_any, pre_any,
    left_ref, right_ref, normed_ref, active_ref, pre_ref,
    w_ref, up_ref, down_ref, query_ref, key_ref, value_ref, probs_ref, terms_ref, mask_ref, slope_ref, resid_ref,
    grad_ref, sum_ref, key_sum, value_sum, turned_ref, turned_sum, semaphores,
):
    rows, width = mid_ref.shape
    hidden = active_ref.shape[1]
    heads = rich_ref.shape[1]
    head_width = width // heads
    scale = head_width ** (-0.5)
    length = length_ref[0]
    windows, _ = attend_windows(rows)
    copies = Copies(semaphores)
    w_copies = [copies.start(w_any.at[i], w_ref.at[i]) for i in range(4)]
    up_copy, down_copy = copies.start(up_any, up_ref), copies.start(down_any, down_ref)
    attend_normed, context_ref = left_ref.at[0], left_ref.at[1]
    stat_ref[...] = jnp.zeros_like(stat_ref)

    for row, start, span, offset in windows:
        i = row + lax.broadcasted_iota(jnp.int32, (span, QUERY_BLOCK), 1)
        j = start + lax.broadcasted_iota(jnp.int32, (span, QUERY_BLOCK), 0)
        allowed = (jnp.abs(i - j) <= RADIUS) & ((j < length) | (i == j))
        mask_ref[pl.ds(offset, span), :] = jnp.where(allowed, 0.0, NEG_FILL)
        across = coords_ref[:, pl.ds(row, QUERY_BLOCK)]
        along = [
            jnp.broadcast_to(coords_ref[:, pl.ds(at, QUERY_BLOCK)], (QUERY_BLOCK, QUERY_BLOCK)).T
            for at in range(start, start + span, QUERY_BLOCK)
        ]
        gap = across - jnp.concatenate(along, axis=0)
        terms_ref[0, pl.ds(offset, span), :] = jnp.log(1.0 + jnp.abs(gap))
        terms_ref[1, pl.ds(offset, span), :] = jnp.tanh(-gap)
    for copy in w_copies:
        copy.wait()
    for _, own in row_parts(rows):
        normed = low(normalized(mid_ref[own, :].astype(F32))[0] * gain_ref[0:1, :] + shift_ref[0:1, :])
        attend_normed[own, :] = normed
        query_ref[own, :] = low(dot_nn(normed, w_ref[0]))
        key_ref[own, :] = low(dot_nn(normed, w_ref[1]))
        value = dot_nn(normed, w_ref[2])
        value_ref[own, :] = low(value)
        turned_ref[:, own] = low(value.T)
    lane = lax.broadcasted_iota(jnp.int32, (QUERY_BLOCK, 2 * head_width), 1) < head_width

    def pair_of(index):
        return pl.ds(pl.multiple_of(index * 2 * head_width, 2 * head_width), 2 * head_width)

    def head_of(index, side):
        return pl.ds(pl.multiple_of((2 * index + side) * head_width, head_width), head_width)

    def attend(index, carry):
        columns = pair_of(index)
        for row, start, span, offset in windows:
            queries = two_heads(query_ref[pl.ds(row, QUERY_BLOCK), columns], lane)
            raw = dot_nt(key_ref[pl.ds(start, span), columns], queries)
            spread = terms_ref[0, pl.ds(offset, span), :]
            order = terms_ref[1, pl.ds(offset, span), :]
            mask = mask_ref[pl.ds(offset, span), :]
            for side in range(2):
                head = 2 * index + side
                own = raw[:, side * QUERY_BLOCK : (side + 1) * QUERY_BLOCK]
                scores = own * scale + (spread * rich_ref[0, head] + order * rich_ref[1, head]) + mask
                weights = jnp.exp(scores - jnp.max(scores, axis=0, keepdims=True))
                probs = low(weights * (1.0 / jnp.sum(weights, axis=0, keepdims=True)))
                probs_ref[index, pl.ds(offset, span), pl.ds(side * QUERY_BLOCK, QUERY_BLOCK)] = probs
                place = head_of(index, side)
                turned_sum[place, pl.ds(row, QUERY_BLOCK)] = dot_nn(
                    turned_ref[place, pl.ds(start, span)], probs
                )
        return carry

    lax.fori_loop(0, heads // 2, attend, 0)
    for at, own in row_parts(rows):
        context = low(turned_sum[:, own].T)
        context_ref[own, :] = context
        branch = dot_nn(context, w_ref[3])
        resid = mid_ref[own, :].astype(F32) + branch
        resid_ref[own, :] = resid
        add_rows(stat_ref, (0, 1), live_sums(length, at, (branch, resid)))
    copies.leave(left_ref, left_any)

    up_copy.wait()
    down_copy.wait()
    feed_forward(
        resid_ref, gain_ref[1:2, :], shift_ref[1:2, :], up_ref, bias_ref, down_ref,
        normed_ref, active_ref, slope_ref, sum_ref,
    )
    copies.leave(normed_ref, normed_any)
    copies.leave(active_ref, active_any)
    for at, own in row_parts(rows):
        branch = sum_ref[own, :]
        result = resid_ref[own, :] + branch
        result_ref[own, :] = low(result)
        add_rows(stat_ref, (2, 3), live_sums(length, at, (branch, result)))
    sum_ref[...] = jnp.zeros_like(sum_ref)

    def tile(index, carry):
        columns = pl.ds(pl.multiple_of(index * HIDDEN_TILE, HIDDEN_TILE), HIDDEN_TILE)
        feed_backward_tile(columns, cotangent_ref, slope_ref, up_ref, down_ref, pre_ref, bias_out, sum_ref)
        return carry

    lax.fori_loop(0, hidden // HIDDEN_TILE, tile, 0)
    copies.leave(pre_ref, pre_any)
    norm_back(grad_ref, cotangent_ref, resid_ref, gain_ref[1:2, :], sum_ref, gain_out, shift_out, 1)

    grad_context = right_ref.at[0]
    for _, own in row_parts(rows):
        grad_low = low(grad_ref[own, :])
        right_ref[3, own, :] = grad_low
        grad_context[own, :] = low(dot_nt(grad_low, w_ref[3]))
        turned_ref[:, own] = low(key_ref[own, :].astype(F32).T)
    key_sum[...] = jnp.zeros_like(key_sum)
    value_sum[...] = jnp.zeros_like(value_sum)

    def attend_back(index, carry):
        columns = pair_of(index)
        rich = [[0.0, 0.0], [0.0, 0.0]]
        for row, start, span, offset in windows:
            keys = pl.ds(start, span)
            context = two_heads(grad_context[pl.ds(row, QUERY_BLOCK), columns], lane)
            queries = two_heads(query_ref[pl.ds(row, QUERY_BLOCK), columns], lane)
            grad_probs = dot_nt(value_ref[keys, columns], context)
            probs = probs_ref[index, pl.ds(offset, span), :]
            value_sum[keys, columns] += dot_nn(probs, context)
            spread = terms_ref[0, pl.ds(offset, span), :]
            order = terms_ref[1, pl.ds(offset, span), :]
            grads = []
            for side in range(2):
                lanes = slice(side * QUERY_BLOCK, (side + 1) * QUERY_BLOCK)
                own = probs[:, lanes].astype(F32)
                mixed = own * grad_probs[:, lanes]
                grad_scores = mixed - own * jnp.sum(mixed, axis=0, keepdims=True)
                rich[0][side] += jnp.sum(grad_scores * spread, axis=0, keepdims=True)
                rich[1][side] += jnp.sum(grad_scores * order, axis=0, keepdims=True)
                grad_raw = low(grad_scores * scale)
                grads.append(grad_raw)
                place = head_of(index, side)
                turned_sum[place, pl.ds(row, QUERY_BLOCK)] = dot_nn(turned_ref[place, keys], grad_raw)
            key_sum[keys, columns] += dot_nn(jnp.concatenate(grads, axis=1), queries)
        for which in range(2):
            for side in range(2):
                rich_out[which, pl.ds(2 * index + side, 1), :] = rich[which][side]
        return carry

    lax.fori_loop(0, heads // 2, attend_back, 0)
    for _, own in row_parts(rows):
        grad_query = low(turned_sum[:, own].T)
        grad_key = low(key_sum[own, :])
        grad_value = low(value_sum[own, :])
        right_ref[0, own, :] = grad_query
        right_ref[1, own, :] = grad_key
        right_ref[2, own, :] = grad_value
        sum_ref[own, :] = (
            dot_nt(grad_query, w_ref[0]) + dot_nt(grad_key, w_ref[1]) + dot_nt(grad_value, w_ref[2])
        )
    copies.leave(right_ref, right_any)
    norm_back(out_ref, grad_ref, mid_ref, gain_ref[0:1, :], sum_ref, gain_out, shift_out, 0)
    copies.finish()


def layer_two(length, mid, cotangent, doc, coords, rich, gain, shift, bias, weights, up, down):
    rows, width = mid.shape
    hidden = up.shape[1]
    heads = rich.shape[1]
    full = whole((rows, width))
    _, band = attend_windows(rows)
    flat, wide = ((rows, width), BF16), ((rows, hidden), BF16)
    sent = [((2, rows, width), BF16), ((4, rows, width), BF16), flat, wide, wide]
    exact = ((rows, width), F32)
    held = [
        flat, flat, flat, ((heads // 2, band, 2 * QUERY_BLOCK), BF16), ((2, band, QUERY_BLOCK), F32),
        ((band, QUERY_BLOCK), F32), wide, exact, exact, exact, exact, exact, ((width, rows), BF16), ((width, rows), F32),
    ]
    return kernel_call(
        layer_two_body,
        (1,),
        [
            full, part_of((rows, width), doc, 0), part_of((1, rows), doc, 1), pl.BlockSpec(memory_space=pltpu.SMEM),
            whole((2, width)), whole((2, width)), whole((1, hidden)), ANYWHERE, ANYWHERE, ANYWHERE,
        ],
        [
            (*flat, full),
            (*flat, full),
            ((4, width), F32, whole((4, width))),
            ((1, hidden), F32, whole((1, hidden))),
            ((2, width), F32, whole((2, width))),
            ((2, width), F32, whole((2, width))),
            ((2, heads, QUERY_BLOCK), F32, whole((2, heads, QUERY_BLOCK))),
        ]
        + [(*what, ANYWHERE) for what in sent],
        [pltpu.VMEM(*what) for what in sent]
        + [pltpu.VMEM(v.shape, BF16) for v in (weights, up, down)]
        + [pltpu.VMEM(*what) for what in held]
        + [pltpu.SemaphoreType.DMA((11,))],
        16 * rows * width * width + 8 * rows * width * hidden + 12 * band * QUERY_BLOCK * width,
        20 * rows * width + 8 * width * width + 4 * (rows + width) * hidden,
        "layer_two",
    )(length, mid, cotangent, coords, rich, gain, shift, bias, weights, up, down)


def weight_body(count, picks_ref, *refs):
    one, two, outs = refs[: 2 * count], refs[2 * count : 4 * count], refs[4 * count :]
    step = pl.program_id(0)

    def write(side):
        total = None
        for doc in range(count):
            left, right = (v[...].reshape(v.shape[-2:]) for v in side[2 * doc : 2 * doc + 2])
            here = dot_tn(left, right)
            total = here if total is None else total + here
        for at in range(2):

            @pl.when(step == at)
            def _():
                outs[at][...] = low(total)

    for which, side in ((1, one), (0, two)):

        @pl.when(picks_ref[0] == which)
        def _():
            write(side)


def weight_quarters(picks, one, two, name):
    count = len(one)
    specs, operands = [], []
    for which, side in ((1, one), (0, two)):
        for left, left_block, left_map, right, right_block, right_map in side:
            for array, shape, place in ((left, left_block, left_map), (right, right_block, right_map)):

                def index(j, chosen, place=place, which=which):
                    return place(jnp.where(chosen[0] == which, chosen[1 + j], 0))

                operands.append(array)
                specs.append(pl.BlockSpec(shape, index))
    width, rows = one[0][4][-1], one[0][1][-2]
    quarter = whole((width, width))
    return kernel_call(
        functools.partial(weight_body, count),
        (2,),
        specs,
        [((width, width), BF16, quarter)] * 2,
        [],
        4 * width * width * count * rows,
        8 * width * width + 8 * count * rows * width,
        name,
    )(picks, *operands)


def place_body(count, places_ref, *refs):
    out_ref = refs[-1]
    for at, piece in enumerate(refs[:count]):

        @pl.when(pl.program_id(0) == at)
        def _():
            out_ref[...] = piece[...].astype(F32)


def placed(places, pieces, shape, columns, into, name):
    width = pieces[0].shape[0]
    if columns:
        spec = pl.BlockSpec((width, width), lambda i, where: (0, where[i]))
    else:
        spec = pl.BlockSpec((width, width), lambda i, where: (where[i], 0))
    more = [] if into is None else [into]
    return kernel_call(
        functools.partial(place_body, len(pieces)),
        (len(pieces),),
        [whole((width, width))] * len(pieces) + [ANYWHERE] * len(more),
        [(shape, F32, spec)],
        [],
        0,
        6 * len(pieces) * width * width,
        name,
        {1 + len(pieces): 0} if more else {},
    )(places, *pieces, *more)[0]


def pack_body(docs, flag_ref, lengths_ref, *refs):
    sides = {1: refs[: 4 * docs], 0: refs[4 * docs : 8 * docs]}
    rich_refs, out_ref = refs[8 * docs : 9 * docs], refs[9 * docs]
    width = out_ref.shape[1]

    def spread(values, base):
        sums = jnp.sum(values, axis=1, keepdims=True)
        shape = (values.shape[0], width)
        lane = lax.broadcasted_iota(jnp.int32, shape, 1)
        row = lax.broadcasted_iota(jnp.int32, shape, 0)
        return jnp.sum(jnp.where(lane == base + row, sums, 0.0), axis=0, keepdims=True)

    for which, side in sides.items():

        @pl.when(flag_ref[0] == which)
        def _():
            bias, gain, shift, stat = (sum(side[4 * d + i][...] for d in range(docs)) for i in range(4))
            for at in range(0, bias.shape[1], width):
                out_ref[at // width : at // width + 1, :] = bias[:, at : at + width]
            base = bias.shape[1] // width
            out_ref[base : base + 2, :] = gain
            out_ref[base + 2 : base + 4, :] = shift
            scalars = spread(stat, 0 if which else stat.shape[0])
            if not which:
                heads = rich_refs[0].shape[1]
                for term in range(2):
                    total = sum(ref[term] for ref in rich_refs)
                    scalars += spread(total, 2 * stat.shape[0] + term * heads)
                count = lengths_ref[0]
                for d in range(1, docs):
                    count += lengths_ref[d]
                lane = lax.broadcasted_iota(jnp.int32, (1, width), 1)
                scalars += jnp.where(lane == 2 * (stat.shape[0] + heads), count.astype(F32), 0.0)
            out_ref[base + 4 : base + 5, :] = scalars


def packed_row(flag, lengths, one, two, rich):
    docs = len(one)
    width = one[0][1].shape[1]
    operands = [v for side in (one, two) for parts in side for v in parts] + list(rich)
    rows = one[0][0].shape[1] // width + 5
    return kernel_call(
        functools.partial(pack_body, docs),
        (1,),
        [pl.BlockSpec(memory_space=pltpu.SMEM)] + [whole(v.shape) for v in operands],
        [((rows, width), F32, whole((rows, width)))],
        [],
        0,
        4 * sum(v.size for v in operands),
        "packed_row",
    )(flag, lengths, *operands)[0]


def passed_along(block, axis, distance):
    devices = range(lax.axis_size(axis))
    route = [(i - distance, i) for i in devices if i - distance in devices]
    return lax.ppermute(block, axis, route)


def after(value, token):
    return lax.optimization_barrier((value, token))[0]


def core_swap(block):
    return lax.ppermute(block, "core", [(0, 1), (1, 0)])


class Ordered:
    def __init__(self):
        self.token = None

    def read(self, *values):
        if self.token is None:
            return values if len(values) > 1 else values[0]
        values = lax.optimization_barrier((*values, self.token))[:-1]
        return values if len(values) > 1 else values[0]

    def gave(self, value):
        self.token = value
        return value


def rounded_sum(*blocks):
    return low(sum(block.astype(F32) for block in blocks))


def quarters_sum(order, sent, kept):
    swap = [(0, 1), (1, 0)]
    inward, outward, across = [(0, 1), (3, 2)], [(1, 0), (2, 3)], [(1, 2), (2, 1)]
    z = lax.axis_index("z")
    arrived = lax.ppermute(sent, "x", swap)
    yield
    total = order.gave(rounded_sum(*kept, order.read(arrived)))
    arrived = lax.ppermute(total, "z", inward)
    yield
    total = order.gave(rounded_sum(total, order.read(arrived)))
    arrived = lax.ppermute(total, "z", across)
    yield
    total = order.gave(rounded_sum(total, order.read(arrived)))
    arrived = lax.ppermute(total, "z", outward)
    yield
    total = order.gave(jnp.where((z == 1) | (z == 2), total, order.read(arrived)))
    arrived, near = lax.ppermute(total, "x", swap), core_swap(total)
    yield
    arrived = order.gave(order.read(arrived))
    yield total, near, arrived, core_swap(arrived)


def small_sum(order, block):
    for axis in ("core", "x", "z"):
        step = 1
        while step < lax.axis_size(axis):
            route = [(i, i ^ step) for i in range(lax.axis_size(axis))]
            arrived = lax.ppermute(block, axis, route)
            yield
            block = order.gave(block + order.read(arrived))
            step *= 2
    arrived = lax.ppermute(block, "section", [(0, 1), (1, 0)])
    yield
    arrived = order.read(arrived)
    yield block, arrived


def local(
    boundary,
    lengths,
    neighbours,
    counts,
    coords,
    square_weights,
    up_weight,
    down_weight,
    up_bias,
    norm_gain,
    norm_bias,
    rich_terms,
):
    first = lax.axis_index("section") == 0
    core, across_x = lax.axis_index("core"), lax.axis_index("x")
    if lax.axis_size("z") != 4 or lax.axis_size("x") != 2:
        across_x = across_x * 0
    use_one = first.astype(jnp.int32)
    give = jnp.stack([use_one, 2 * (1 - core) + 1 - across_x, 2 * (1 - core) + across_x])
    keep = jnp.stack([use_one, 2 * core + 1 - across_x, 2 * core + across_x])
    places = jnp.stack([keep[2], give[2], keep[1], give[1]])
    documents = lengths.shape[0]
    docs = range(documents)
    rows = boundary.shape[1] // documents
    width = boundary.shape[2]
    hidden = up_weight.shape[2]
    heads = rich_terms.shape[1]
    source = boundary[0]
    squares = square_weights[0]
    up, down, bias = up_weight[0], down_weight[0], up_bias
    gains, shifts = norm_gain[0], norm_bias[0]
    near_t = neighbours.T
    counts_row, coords_row = counts[None], coords[None]
    length = [lax.slice_in_dim(lengths, doc, doc + 1) for doc in range(documents)]

    kept_one, arrived, stats_one = [], [], []
    sent = None
    for doc in docs:
        here = source if sent is None else after(source, sent)
        sent, stat, links, left, sigma, pull, resid, normed, active, slope = layer_one_forward(
            length[doc], here, doc, rows, near_t, counts_row, gains, shifts, bias, squares, up, down
        )
        kept_one.append((links, resid, slope, sigma, pull, left, normed, active))
        stats_one.append(stat)
        arrived.append(passed_along(sent, "section", 1))

    back, out_two, rich_two, kept_two, small_two = [], [], [], [], []
    for doc in docs:
        grad_mid, result, stat, bias_grad, gain_grad, shift_grad, rich, left, right, normed, active, pre = layer_two(
            length[doc], arrived[doc], source, doc, coords_row, rich_terms, gains, shifts, bias, squares, up, down
        )
        out_two.append(result)
        kept_two.append((left, right, normed, active, pre))
        small_two.append((bias_grad, gain_grad, shift_grad, stat))
        rich_two.append(rich)
        back.append(passed_along(grad_mid, "section", -1))
        last_sent = grad_mid

    out_one, pre_one, right_one, small_one = [], [], [], []

    def first_back(doc, grad_mid):
        links, resid, slope, sigma, pull = kept_one[doc][:5]
        grad_x, bias_grad, gain_grad, shift_grad, pre, right = layer_one_backward(
            length[doc], grad_mid, source, doc, gains, counts_row, links, resid, slope, sigma, pull, squares, up, down
        )
        out_one.append(grad_x)
        pre_one.append(pre)
        right_one.append(right)
        small_one.append((bias_grad, gain_grad, shift_grad, stats_one[doc]))
        return grad_x

    token = last_sent
    for doc in range(documents - 1):
        token = first_back(doc, after(back[doc], token))
    if documents > 1:
        back[-1] = after(back[-1], token)

    quarter, stack = (rows, width), (1, rows, width)
    still, across = lambda q: (0, 0), lambda q: (0, q)
    own_rows = [functools.partial(lambda d, q: (d, 0), d) for d in docs]
    down_pairs = (
        [(kept_one[d][7], quarter, across, back[d], quarter, still) for d in docs],
        [(kept_two[d][3], quarter, across, source, quarter, own_rows[d]) for d in docs],
    )

    def up_pairs():
        return (
            [(kept_one[d][6], quarter, still, pre_one[d], quarter, across) for d in docs],
            [(kept_two[d][2], quarter, still, kept_two[d][4], quarter, across) for d in docs],
        )

    def square_pairs():
        left_one, right_of_one = lambda q: ((q + 1) // 2, 0, 0), lambda q: (jnp.maximum(q - 1, 0), 0, 0)
        left_two, right_of_two = lambda q: (q // 3, 0, 0), lambda q: (q, 0, 0)
        return (
            [(kept_one[d][5], stack, left_one, right_one[d], stack, right_of_one) for d in docs],
            [(kept_two[d][0], stack, left_two, kept_two[d][1], stack, right_of_two) for d in docs],
        )

    order = Ordered()
    custom = lax.axis_size("z") == 4 and lax.axis_size("x") == 2

    def products(pairs, name):
        given = weight_quarters(order.read(give), *pairs, name + "_give")
        order.gave(given[1])
        given = [core_swap(v) for v in given]
        kept = weight_quarters(order.read(keep), *pairs, name + "_keep")
        order.gave(kept[1])
        yield
        sent = order.gave(rounded_sum(kept[0], order.read(given[0])))
        if custom:
            yield from quarters_sum(order, sent, (kept[1], given[1]))
        else:
            near = lax.psum(rounded_sum(kept[1], given[1]), ("z", "x"))
            far = lax.psum(sent, ("z", "x"))
            yield from [None] * 5 + [(near, core_swap(near), far, core_swap(far))]

    totals = {}

    def place(name, pieces):
        shape = (width, hidden) if name == "up" else (hidden, width)
        near, near_swapped, far, far_swapped = pieces
        out = placed(
            places[:2], order.read(near, near_swapped), shape, name == "up", None, name + "_near"
        )
        order.gave(out)
        out = placed(places[2:], order.read(far, far_swapped), shape, name == "up", out, name + "_far")
        totals[name] = order.gave(out)

    down_sum = products(down_pairs, "down")
    next(down_sum)
    next(down_sum)
    order.gave(first_back(documents - 1, order.read(back[-1])))
    up_sum = products(up_pairs(), "up")
    next(up_sum)
    next(down_sum)
    next(up_sum)
    square_sum = products(square_pairs(), "square")
    next(square_sum)
    next(down_sum)
    next(square_sum)
    rows_out = [jnp.where(first, *order.read(out_one[doc], out_two[doc])) for doc in docs]
    boundary_out = order.gave(jnp.concatenate(rows_out, axis=0))[None]
    small = packed_row(use_one[None], order.read(lengths), small_one, small_two, rich_two)
    row_sum = small_sum(order, order.gave(small))
    next(row_sum)
    for steps in (up_sum, row_sum, down_sum, square_sum, up_sum, row_sum, down_sum, square_sum, up_sum, row_sum):
        next(steps)
    down_pieces = next(down_sum)
    next(square_sum)
    next(up_sum)
    for _ in range(lax.axis_size("z").bit_length() - 3):
        next(row_sum)
    next(row_sum)
    place("down", down_pieces)
    next(square_sum)
    up_pieces = next(up_sum)
    packed, crossed = next(row_sum)
    place("up", up_pieces)
    place("square", next(square_sum))
    down_total, up_total, square_total = totals["down"], totals["up"], totals["square"]

    at = hidden // width
    size = 9 + 2 * heads
    shared = packed[at + 4, :size] + crossed[at + 4, :size]
    rms = jnp.sqrt(shared[:8].reshape(2, 4) / (shared[8 + 2 * heads] * width))
    rich_total = shared[8 : 8 + 2 * heads].reshape(2, heads)
    return (
        boundary_out,
        square_total.reshape(1, 4, width, width),
        up_total.reshape(1, width, hidden),
        down_total[None],
        packed[:at].reshape(1, hidden),
        packed[at : at + 2][None],
        packed[at + 2 : at + 4][None],
        rich_total,
        rms,
    )


def solution(mesh):
    sections, dp = mesh.devices.shape
    split = Mesh(mesh.devices.reshape(sections, dp // 4, 2, 2), ("section", "z", "x", "core"))
    data = ("z", "x", "core")
    in_specs = (
        P("section", data, None),
        P(data),
        P(data, None),
        P(data),
        P(data),
        P("section", None, None, None),
        P("section", None, None),
        P("section", None, None),
        P("section", None),
        P("section", None, None),
        P("section", None, None),
        P(),
    )
    out_specs = (
        P("section", data, None),
        P("section", None, None, None),
        P("section", None, None),
        P("section", None, None),
        P("section", None),
        P("section", None, None),
        P("section", None, None),
        P(),
        P(),
    )
    return jax.shard_map(local, mesh=split, in_specs=in_specs, out_specs=out_specs, check_vma=False)
```

time: 673 us -> 445 us (0.66)
  waiting for transfers between devices: 265 us -> 115 us
  local copies, waits for them, and re-layouts: 136 us -> 9.23 us
  Pallas kernels: 198 us -> 245 us
  starting transfers between devices: 15 us -> 40.3 us
  between operations: 16.6 us -> 1.97 us
  other arithmetic: 35 us -> 25.2 us
    psum x1 -> x0, waiting for transfers between devices: 237 us -> none  [summed_over_documents(): part = lax.psum(part, 'chip')]
    ppermute x11 -> x32, waiting for transfers between devices: 12.3 us -> 114 us  [the longest x4 32.7 us: small_sum(): arrived = lax.ppermute(block, axis, route)]
    unnamed x242 -> x32, local copies, waits for them, and re-layouts: 98.7 us -> 5.35 us
    pallas_call x19, Pallas kernels: 198 us -> 245 us  [the longest x2 91.9 us: layer_two(): kernel_call(layer_two_body, (1,), [full, part_of((rows, width), doc, 0),...]
    reshape x4 -> x0, local copies, waits for them, and re-layouts: 27.2 us -> none  [the longest x2 26 us: local(): up_total.reshape(1, width, hidden)]
    ppermute x11 -> x32, starting transfers between devices: 5.37 us -> 31.2 us  [the longest x4 9.32 us: small_sum(): arrived = lax.ppermute(block, axis, route)]
    ppermute x4, waiting for transfers between devices: 15.7 us -> 0.47 us  [passed_along(): return lax.ppermute(block, axis, route)]
    add x14 -> x5, other arithmetic: 11.1 us -> 1.47 us  [the longest x4 1.47 us: small_sum(): block = order.gave(block + order.read(arrived))]
  transfers between devices with their start and end apart: 16 -> 36, of which waited for: 7 -> 13; matrix products, arithmetic and copies ran while one was open for 9% -> 7% of each run, Pallas kernels for 12% -> 49%
where the time goes in v3:
time: 445 us; the launch traced here: 437 us
  Pallas kernels  245 us (55%)
  waiting for transfers between devices  115 us (26%)
  starting transfers between devices  40.3 us (9%)
  other arithmetic  25.2 us (6%)
  local copies, waits for them, and re-layouts  9.23 us (2%)
    pallas_call x2, Pallas kernels, layer_two(): kernel_call(layer_two_body, (1,), [full, part_of((rows, width), doc, 0),...  91.9 us
    pallas_call x6, Pallas kernels, weight_quarters(): kernel_call(functools.partial(weight_body, count), (2,), specs, [((width,...  49.8 us
    pallas_call x2, Pallas kernels, layer_one_forward(): kernel_call(layer_one_forward_body, (1,), [part_of((rows, width), doc, 0)...  38.3 us
    pallas_call x2, Pallas kernels, layer_one_backward(): kernel_call(layer_one_backward_body, (1,), [full, part_of((rows, width),...  35.8 us
    ppermute x4, waiting for transfers between devices, small_sum(): arrived = lax.ppermute(block, axis, route)  32.7 us
    pallas_call x6, Pallas kernels, placed(): kernel_call(functools.partial(place_body, len(pieces)), (len(pieces),), [...  27.9 us
    ppermute x3, waiting for transfers between devices, quarters_sum(): arrived = lax.ppermute(sent, 'x', swap)  26.9 us
    ppermute x3, waiting for transfers between devices, quarters_sum(): arrived = lax.ppermute(total, 'z', outward)  22.6 us
  transfers between devices with their start and end apart: 36, of which 13 were waited for; matrix products, arithmetic and copies ran while one was open for 7% of the time, Pallas kernels for 49%

profile of v3, /device:TPU:0, one launch (start us, length us, event | category | flops | bytes accessed | tf_op | source)
XLA Modules:
  0.0 436.7 jit_solution(5834645523832744317)
XLA Ops:
  0.6 1.3 fusion.1
  2.0 19.1 %layer_one_forward.2 = (bf16[512,768]{1,0:T(8,128)(2,1)}, f32[4,768]{1,0:T(4,128)}, bf16[256,512]{1,0:T(8,128)(2,1)}, bf16[3,512,768]{2,1,0:T(8,128)(2,1)}, bf16...) custom-call(s32[1]{0:T(128)} %get-tuple-element.245.length_ref, ...), custom_call_target="tpu_custom_call" | custom-call | flops 7247757312 | bytes 26738688 | tf_op jit(solution)/shard_map/layer_one_forward/pallas_call | solution.py:247
  21.1 5.1 %collective-permute-start = (bf16[512,768]{1,0:T(8,128)(2,1)}, bf16[512,768]{1,0:T(8,128)(2,1)S(1)}, u32[]{:S(2)}, u32[]{:S(2)}) collective-permute-start(bf16[512,768]{1,0:T(8,128)(2,1)} %get-tuple-element.126), channel_id=1, source_target_pairs={{0,16},{1,17},{2,18},{3,19},{4,20},{5,21},{6,22},{7,23},{8,24},{9,... | collective-permute-start | bytes 2359304 | tf_op jit(solution)/shard_map/ppermute | solution.py:706
  26.2 19.1 %layer_one_forward.3 = (bf16[512,768]{1,0:T(8,128)(2,1)}, f32[4,768]{1,0:T(4,128)}, bf16[256,512]{1,0:T(8,128)(2,1)}, bf16[3,512,768]{2,1,0:T(8,128)(2,1)}, bf16...) custom-call(s32[1]{0:T(128)} %get-tuple-element.246.length_ref, ...), custom_call_target="tpu_custom_call" | custom-call | flops 7247757312 | bytes 26738688 | tf_op jit(solution)/shard_map/layer_one_forward/pallas_call | solution.py:247
  45.3 1.3 collective-permute-start.2
  46.7 0.9 copy-done.14
  47.6 46.0 %layer_two.2 = (bf16[512,768]{1,0:T(8,128)(2,1)}, bf16[512,768]{1,0:T(8,128)(2,1)}, f32[4,768]{1,0:T(4,128)}, f32[1,3072]{1,0:T(1,128)}, f32[2,768]{1,0:T(2,128)...) custom-call(s32[1]{0:T(128)} %get-tuple-element.245.length_ref, ...), custom_call_target="tpu_custom_call" | custom-call | flops 16005464064 | bytes 28311552 | tf_op jit(solution)/shard_map/layer_two/pallas_call | solution.py:545
  93.6 1.3 collective-permute-start.1
  95.8 45.9 %layer_two.3 = (bf16[512,768]{1,0:T(8,128)(2,1)}, bf16[512,768]{1,0:T(8,128)(2,1)}, f32[4,768]{1,0:T(4,128)}, f32[1,3072]{1,0:T(1,128)}, f32[2,768]{1,0:T(2,128)...) custom-call(s32[1]{0:T(128)} %get-tuple-element.246.length_ref, ...), custom_call_target="tpu_custom_call" | custom-call | flops 16005464064 | bytes 28311552 | tf_op jit(solution)/shard_map/layer_two/pallas_call | solution.py:545
  141.7 1.3 collective-permute-start.3
  143.7 0.9 copy-done.4
  144.6 17.8 %layer_one_backward.2 = (bf16[512,768]{1,0:T(8,128)(2,1)}, f32[1,3072]{1,0:T(1,128)}, f32[2,768]{1,0:T(2,128)}, f32[2,768]{1,0:T(2,128)}, bf16[512,3072]{1,0:T(8,128)(2,1)}, /*index=5*/bf16[3,512,768]{2,1,0:T(8,128)(2,1)}) custom-call(s32[1]{0:T(128)} %get-tuple-element.245.length_ref, bf16[512,768]{1,0:T(8,128)(2,1)} %copy-done.4, ...), custom_call_target="tpu_custom_call" | custom-call | flops 7247757312 | bytes 27525120 | tf_op jit(solution)/shard_map/layer_one_backward/pallas_call | solution.py:327
  162.9 0.9 copy-done.3
  163.8 8.2 %down_give.1 = (bf16[768,768]{1,0:T(8,128)(2,1)}, bf16[768,768]{1,0:T(8,128)(2,1)}) custom-call(s32[3]{0:T(128)} %pad_add_fusion.1.picks_ref, bf16[512,3072]{1,0:T(8,128)(2,1)} %get-tuple-element.140.refs_0_, bf16[512,768]{1,0:T(8,128)(2,1)} %copy-done.4, bf16[512,3072]{1,0:T(8,128)(2,1)} %get-tuple-element.141.refs_2_, bf16[512,768]{1,0:T(8,128)(2,1)} %copy-done.3, ...), custom_call_target="tpu_custom_call" | custom-call | flops 2415919104 | bytes 11010048 | tf_op jit(solution)/shard_map/down_give/pallas_call | solution.py:609
  173.1 8.0 %down_keep.1 = (bf16[768,768]{1,0:T(8,128)(2,1)}, bf16[768,768]{1,0:T(8,128)(2,1)}) custom-call(s32[3]{0:T(128)} %pad_add_fusion.picks_ref, bf16[512,3072]{1,0:T(8,128)(2,1)} %get-tuple-element.140.refs_0_, bf16[512,768]{1,0:T(8,128)(2,1)} %copy-done.4, bf16[512,3072]{1,0:T(8,128)(2,1)} %get-tuple-element.141.refs_2_, bf16[512,768]{1,0:T(8,128)(2,1)} %copy-done.3, ...), custom_call_target="tpu_custom_call" | custom-call | flops 2415919104 | bytes 11010048 | tf_op jit(solution)/shard_map/down_keep/pallas_call | solution.py:609
  181.2 1.6 add_convert_fusion.11
  182.7 1.6 collective-permute-start.7
  184.3 18.0 %layer_one_backward.3 = (bf16[512,768]{1,0:T(8,128)(2,1)}, f32[1,3072]{1,0:T(1,128)}, f32[2,768]{1,0:T(2,128)}, f32[2,768]{1,0:T(2,128)}, bf16[512,3072]{1,0:T(8,128)(2,1)}, /*index=5*/bf16[3,512,768]{2,1,0:T(8,128)(2,1)}) custom-call(s32[1]{0:T(128)} %get-tuple-element.246.length_ref, bf16[512,768]{1,0:T(8,128)(2,1)} %copy-done.3, ...), custom_call_target="tpu_custom_call" | custom-call | flops 7247757312 | bytes 27525120 | tf_op jit(solution)/shard_map/layer_one_backward/pallas_call | solution.py:327
  202.3 8.5 %up_give.1 = (bf16[768,768]{1,0:T(8,128)(2,1)}, bf16[768,768]{1,0:T(8,128)(2,1)}) custom-call(s32[3]{0:T(128)} %pad_add_fusion.1.picks_ref, bf16[512,768]{1,0:T(8,128)(2,1)} %get-tuple-element.158.refs_0_, bf16[512,3072]{1,0:T(8,128)(2,1)} %get-tuple-element.159.refs_1_, bf16[512,768]{1,0:T(8,128)(2,1)} %get-tuple-element.160.refs_2_, ...), custom_call_target="tpu_custom_call" | custom-call | flops 2415919104 | bytes 11010048 | tf_op jit(solution)/shard_map/up_give/pallas_call | solution.py:609
  210.8 8.3 %up_keep.1 = (bf16[768,768]{1,0:T(8,128)(2,1)}, bf16[768,768]{1,0:T(8,128)(2,1)}) custom-call(s32[3]{0:T(128)} %pad_add_fusion.picks_ref, bf16[512,768]{1,0:T(8,128)(2,1)} %get-tuple-element.158.refs_0_, bf16[512,3072]{1,0:T(8,128)(2,1)} %get-tuple-element.159.refs_1_, bf16[512,768]{1,0:T(8,128)(2,1)} %get-tuple-element.160.refs_2_, ...), custom_call_target="tpu_custom_call" | custom-call | flops 2415919104 | bytes 11010048 | tf_op jit(solution)/shard_map/up_keep/pallas_call | solution.py:609
  219.2 1.8 add_convert_fusion.10
  221.0 3.6 collective-permute-start.9
  224.6 1.6 add_convert_fusion.9
  226.2 8.2 %square_give.1 = (bf16[768,768]{1,0:T(8,128)(2,1)}, bf16[768,768]{1,0:T(8,128)(2,1)}) custom-call(s32[3]{0:T(128)} %pad_add_fusion.1.picks_ref, bf16[3,512,768]{2,1,0:T(8,128)(2,1)} %get-tuple-element.174.refs_0_, bf16[3,512,768]{2,1,0:T(8,128)(2,1)} %get-tuple-element.175.refs_1_, bf16[3,512,768]{2,1,0:T(8,128)(2,1)} %get-tuple-element.176.refs_2_, ...), custom_call_target="tpu_custom_call" | custom-call | flops 2415919104 | bytes 11010048 | tf_op jit(solution)/shard_map/square_give/pallas_call | solution.py:609
  235.0 1.6 packed_row.1
  237.1 8.4 %square_keep.1 = (bf16[768,768]{1,0:T(8,128)(2,1)}, bf16[768,768]{1,0:T(8,128)(2,1)}) custom-call(s32[3]{0:T(128)} %pad_add_fusion.picks_ref, bf16[3,512,768]{2,1,0:T(8,128)(2,1)} %get-tuple-element.174.refs_0_, bf16[3,512,768]{2,1,0:T(8,128)(2,1)} %get-tuple-element.175.refs_1_, bf16[3,512,768]{2,1,0:T(8,128)(2,1)} %get-tuple-element.176.refs_2_, ...), custom_call_target="tpu_custom_call" | custom-call | flops 2415919104 | bytes 11010048 | tf_op jit(solution)/shard_map/square_keep/pallas_call | solution.py:609
  245.6 4.7 %collective-permute-done.9 = bf16[768,768]{1,0:T(8,128)(2,1)S(1)} collective-permute-done((bf16[768,768]{1,0:T(8,128)(2,1)S(1)}, bf16[768,768]{1,0:T(8,128)(2,1)S(1)}, u32[]{:S(2)}, u32[]{:S(2)}) %collective-permute-start.9) | collective-permute-done | bytes 1179680 | tf_op jit(solution)/shard_map/ppermute | solution.py:743
  250.5 0.9 collective-permute-start.12
  251.5 1.7 add_convert_fusion.7
  253.8 9.6 %collective-permute-done.15 = bf16[768,768]{1,0:T(8,128)(2,1)} collective-permute-done((bf16[768,768]{1,0:T(8,128)(2,1)S(1)}, bf16[768,768]{1,0:T(8,128)(2,1)}, u32[]{:S(2)}, u32[]{:S(2)}) %collective-permute-start.15) | collective-permute-done | bytes 1179680 | tf_op jit(solution)/shard_map/ppermute | solution.py:740
  263.4 2.1 add_convert_fusion.6
  265.5 1.6 collective-permute-start.19
  267.2 1.2 collective-permute-done.13
  269.4 1.4 collective-permute-start.17
  270.8 17.3 %collective-permute-done.11 = bf16[768,768]{1,0:T(8,128)(2,1)S(1)} collective-permute-done((bf16[768,768]{1,0:T(8,128)(2,1)S(1)}, bf16[768,768]{1,0:T(8,128)(2,1)S(1)}, u32[]{:S(2)}, u32[]{:S(2)}) %collective-permute-start.11) | collective-permute-done | bytes 1179680 | tf_op jit(solution)/shard_map/ppermute | solution.py:740
  288.1 2.8 add_convert_fusion.4
  290.9 2.3 collective-permute-start.16
  293.6 1.7 collective-permute-start.23
  295.6 4.1 collective-permute-done.18
  300.5 8.6 %collective-permute-done.17 = bf16[768,768]{1,0:T(8,128)(2,1)S(1)} collective-permute-done((bf16[768,768]{1,0:T(8,128)(2,1)S(1)}, bf16[768,768]{1,0:T(8,128)(2,1)S(1)}, u32[]{:S(2)}, u32[]{:S(2)}) %collective-permute-start.17) | collective-permute-done | bytes 1179680 | tf_op jit(solution)/shard_map/ppermute | solution.py:749
  309.2 0.9 collective-permute-start.21
  310.1 7.7 %collective-permute-done.16 = bf16[768,768]{1,0:T(8,128)(2,1)} collective-permute-done((bf16[768,768]{1,0:T(8,128)(2,1)}, bf16[768,768]{1,0:T(8,128)(2,1)}, u32[]{:S(2)}, u32[]{:S(2)}) %collective-permute-start.16) | collective-permute-done | bytes 1179680 | tf_op jit(solution)/shard_map/ppermute | solution.py:743
  317.8 1.9 add_convert_fusion.2
  320.5 1.6 add_convert_fusion.1
  322.0 1.3 collective-permute-start.28
  323.3 5.4 %collective-permute-start.22 = (f32[9,768]{1,0:T(8,128)S(1)}, f32[9,768]{1,0:T(8,128)S(1)}, u32[]{:S(2)}, u32[]{:S(2)}) collective-permute-start(f32[9,768]{1,0:T(8,128)S(1)} %add.90), channel_id=1, source_target_pairs={{0,4},{4,0},{8,12},{12,8},{1,5},{5,1},{9,13},{13,9},{2,6},{6,2},{1... | collective-permute-start | bytes 82952 | tf_op jit(solution)/shard_map/ppermute | solution.py:763
  328.7 25.8 %collective-permute-done.22 = f32[9,768]{1,0:T(8,128)S(1)} collective-permute-done((f32[9,768]{1,0:T(8,128)S(1)}, f32[9,768]{1,0:T(8,128)S(1)}, u32[]{:S(2)}, u32[]{:S(2)}) %collective-permute-start.22) | collective-permute-done | bytes 27680 | tf_op jit(solution)/shard_map/ppermute | solution.py:763
  354.9 1.3 collective-permute-start.24
  357.3 3.5 collective-permute-start.27
  361.5 1.6 collective-permute-done.27
  363.0 4.7 %down_near.1.refs_2_ = f32[3072,768]{1,0:T(8,128)} custom-call(s32[2]{0:T(128)} %pad_add_fusion.3.places_ref, bf16[768,768]{1,0:T(8,128)(2,1)} %copy-done, bf16[768,768]{1,0:T(8,128)(2,1)} %collective-permute-done.26.refs_1_), custom_call_target="tpu_custom_call" | custom-call | bytes 7077888 | tf_op jit(solution)/shard_map/down_near/pallas_call | solution.py:637
  367.7 4.7 %down_far.1 = f32[3072,768]{1,0:T(8,128)} custom-call(s32[2]{0:T(128)} %pad_add_fusion.2.places_ref, bf16[768,768]{1,0:T(8,128)(2,1)} %collective-permute-done.21.refs_0_, bf16[768,768]{1,0:T(8,128)(2,1)} %collective-permute-done.25.refs_1_, f32[3072,768]{1,0:T(8,128)} %down_near.1.refs_2_), custom_call_target="tpu_custom_call", output_to_operand_aliasing={{}: (3, {})} | custom-call | bytes 7077888 | tf_op jit(solution)/shard_map/down_far/pallas_call | solution.py:637
  372.4 14.0 %collective-permute-done.24 = bf16[768,768]{1,0:T(8,128)(2,1)} collective-permute-done((bf16[768,768]{1,0:T(8,128)(2,1)S(1)}, bf16[768,768]{1,0:T(8,128)(2,1)}, u32[]{:S(2)}, u32[]{:S(2)}) %collective-permute-start.24) | collective-permute-done | bytes 1179680 | tf_op jit(solution)/shard_map/ppermute | solution.py:749
  386.4 1.4 broadcast_select_fusion.refs_0_
  388.4 4.7 %up_near.1.refs_2_ = f32[768,3072]{1,0:T(8,128)} custom-call(s32[2]{0:T(128)} %pad_add_fusion.3.places_ref, bf16[768,768]{1,0:T(8,128)(2,1)} %copy-done.2, bf16[768,768]{1,0:T(8,128)(2,1)} %collective-permute-done.32.refs_1_), custom_call_target="tpu_custom_call" | custom-call | bytes 7077888 | tf_op jit(solution)/shard_map/up_near/pallas_call | solution.py:637
  393.0 4.7 %up_far.1 = f32[768,3072]{1,0:T(8,128)} custom-call(s32[2]{0:T(128)} %pad_add_fusion.2.places_ref, bf16[768,768]{1,0:T(8,128)(2,1)} %collective-permute-done.30.refs_0_, bf16[768,768]{1,0:T(8,128)(2,1)} %collective-permute-done.31.refs_1_, f32[768,3072]{1,0:T(8,128)} %up_near.1.refs_2_), custom_call_target="tpu_custom_call", output_to_operand_aliasing={{}: (3, {})} | custom-call | bytes 7077888 | tf_op jit(solution)/shard_map/up_far/pallas_call | solution.py:637
  397.7 18.6 %collective-permute-done.29.refs_0_ = bf16[768,768]{1,0:T(8,128)(2,1)S(1)} collective-permute-done((bf16[768,768]{1,0:T(8,128)(2,1)S(1)}, bf16[768,768]{1,0:T(8,128)(2,1)S(1)}, u32[]{:S(2)}, u32[]{:S(2)}) %collective-permute-start.29) | collective-permute-done | bytes 1179680 | tf_op jit(solution)/shard_map/ppermute | solution.py:752
  416.2 2.0 broadcast_select_fusion.3
  418.2 1.2 fusion
  419.5 1.8 collective-permute-start.35
  422.4 1.1 collective-permute-done.35
  426.2 4.7 %square_near.1.refs_2_ = f32[3072,768]{1,0:T(8,128)} custom-call(s32[2]{0:T(128)} %pad_add_fusion.3.places_ref, bf16[768,768]{1,0:T(8,128)(2,1)} %copy-done.1, bf16[768,768]{1,0:T(8,128)(2,1)} %collective-permute-done.34.refs_1_), custom_call_target="tpu_custom_call" | custom-call | bytes 7077888 | tf_op jit(solution)/shard_map/square_near/pallas_call | solution.py:637
  430.9 1.0 copy-done.6
  431.9 4.7 %square_far.1 = f32[3072,768]{1,0:T(8,128)} custom-call(s32[2]{0:T(128)} %pad_add_fusion.2.places_ref, bf16[768,768]{1,0:T(8,128)(2,1)} %copy-done.5, bf16[768,768]{1,0:T(8,128)(2,1)} %copy-done.6, f32[3072,768]{1,0:T(8,128)} %square_near.1.refs_2_), custom_call_target="tpu_custom_call", output_to_operand_aliasing={{}: (3, {})} | custom-call | bytes 7077888 | tf_op jit(solution)/shard_map/square_far/pallas_call | solution.py:637
  (92 shorter events, 14.3 us)
Async XLA Ops:
  21.1 25.6 %collective-permute-start = (bf16[512,768]{1,0:T(8,128)(2,1)}, bf16[512,768]{1,0:T(8,128)(2,1)S(1)}, u32[]{:S(2)}, u32[]{:S(2)}) collective-permute-start(bf16[512,768]{1,0:T(8,128)(2,1)} %get-tuple-element.126), channel_id=1, source_target_pairs={{0,16},{1,17},{2,18},{3,19},{4,20},{5,21},{6,22},{7,23},{8,24},{9,... | collective-permute-start | bytes 2359304 | tf_op jit(solution)/shard_map/ppermute | solution.py:706
  45.3 49.6 %collective-permute-start.2 = (bf16[512,768]{1,0:T(8,128)(2,1)}, bf16[512,768]{1,0:T(8,128)(2,1)S(1)}, u32[]{:S(2)}, u32[]{:S(2)}) collective-permute-start(bf16[512,768]{1,0:T(8,128)(2,1)} %get-tuple-element.129), channel_id=1, source_target_pairs={{0,16},{1,17},{2,18},{3,19},{4,20},{5,21},{6,22},{7,23},{8,24},{9,... | collective-permute-start | bytes 2359304 | tf_op jit(solution)/shard_map/ppermute | solution.py:706
  46.7 0.9 copy-start.14
  93.6 50.0 %collective-permute-start.1 = (bf16[512,768]{1,0:T(8,128)(2,1)}, bf16[512,768]{1,0:T(8,128)(2,1)S(1)}, u32[]{:S(2)}, u32[]{:S(2)}) collective-permute-start(bf16[512,768]{1,0:T(8,128)(2,1)} %get-tuple-element.127), channel_id=1, source_target_pairs={{16,0},{17,1},{18,2},{19,3},{20,4},{21,5},{22,6},{23,7},{24,8},{25... | collective-permute-start | bytes 2359304 | tf_op jit(solution)/shard_map/ppermute | solution.py:706
  94.9 0.9 copy-start.13
  141.7 21.2 %collective-permute-start.3 = (bf16[512,768]{1,0:T(8,128)(2,1)}, bf16[512,768]{1,0:T(8,128)(2,1)S(1)}, u32[]{:S(2)}, u32[]{:S(2)}) collective-permute-start(bf16[512,768]{1,0:T(8,128)(2,1)} %get-tuple-element.130), channel_id=1, source_target_pairs={{16,0},{17,1},{18,2},{19,3},{20,4},{21,5},{22,6},{23,7},{24,8},{25... | collective-permute-start | bytes 2359304 | tf_op jit(solution)/shard_map/ppermute | solution.py:706
  143.7 0.9 copy-start.4
  162.9 0.9 copy-start.3
  172.0 9.2 %collective-permute-start.4 = (bf16[768,768]{1,0:T(8,128)(2,1)}, bf16[768,768]{1,0:T(8,128)(2,1)S(1)}, u32[]{:S(2)}, u32[]{:S(2)}) collective-permute-start(bf16[768,768]{1,0:T(8,128)(2,1)} %get-tuple-element.147), channel_id=1, source_target_pairs={{0,1},{1,0},{2,3},{3,2},{4,5},{5,4},{6,7},{7,6},{8,9},{9,8},{10,11... | collective-permute-start | bytes 3538952 | tf_op jit(solution)/shard_map/ppermute | solution.py:714
  172.6 46.6 %collective-permute-start.6 = (bf16[768,768]{1,0:T(8,128)(2,1)}, bf16[768,768]{1,0:T(8,128)(2,1)S(1)}, u32[]{:S(2)}, u32[]{:S(2)}) collective-permute-start(bf16[768,768]{1,0:T(8,128)(2,1)} %get-tuple-element.144), channel_id=1, source_target_pairs={{0,1},{1,0},{2,3},{3,2},{4,5},{5,4},{6,7},{7,6},{8,9},{9,8},{10,11... | collective-permute-start | bytes 3538952 | tf_op jit(solution)/shard_map/ppermute | solution.py:714
  182.7 36.5 %collective-permute-start.7 = (bf16[768,768]{1,0:T(8,128)(2,1)S(1)}, bf16[768,768]{1,0:T(8,128)(2,1)}, u32[]{:S(2)}, u32[]{:S(2)}) collective-permute-start(bf16[768,768]{1,0:T(8,128)(2,1)S(1)} %add_convert_fusion.11), channel_id=1, source_target_pairs={{0,2},{2,0},{1,3},{3,1},{4,6},{6,4},{5,7},{7,5},{8,10},{10,8},{9,1... | collective-permute-start | bytes 3538952 | tf_op jit(solution)/shard_map/ppermute | solution.py:740
  210.8 13.8 %collective-permute-start.5 = (bf16[768,768]{1,0:T(8,128)(2,1)}, bf16[768,768]{1,0:T(8,128)(2,1)}, u32[]{:S(2)}, u32[]{:S(2)}) collective-permute-start(bf16[768,768]{1,0:T(8,128)(2,1)} %get-tuple-element.169), channel_id=1, source_target_pairs={{0,1},{1,0},{2,3},{3,2},{4,5},{5,4},{6,7},{7,6},{8,9},{9,8},{10,11... | collective-permute-start | bytes 3538952 | tf_op jit(solution)/shard_map/ppermute | solution.py:714
  210.8 8.4 %copy-start.11 = (bf16[768,768]{1,0:T(8,128)(2,1)S(1)}, bf16[768,768]{1,0:T(8,128)(2,1)}, u32[]{:S(2)}) copy-start(bf16[768,768]{1,0:T(8,128)(2,1)} %get-tuple-element.148) | copy-start | bytes 3538948
  219.2 5.4 %copy-start.7 = (bf16[768,768]{1,0:T(8,128)(2,1)S(1)}, bf16[768,768]{1,0:T(8,128)(2,1)}, u32[]{:S(2)}) copy-start(bf16[768,768]{1,0:T(8,128)(2,1)} %get-tuple-element.168) | copy-start | bytes 3538948
  221.0 29.2 %collective-permute-start.9 = (bf16[768,768]{1,0:T(8,128)(2,1)S(1)}, bf16[768,768]{1,0:T(8,128)(2,1)S(1)}, u32[]{:S(2)}, u32[]{:S(2)}) collective-permute-start(bf16[768,768]{1,0:T(8,128)(2,1)S(1)} %add_convert_fusion.10), channel_id=1, source_target_pairs={{0,4},{12,8},{1,5},{13,9},{2,6},{14,10},{3,7},{15,11},{16,20},{28,... | collective-permute-start | bytes 3538952 | tf_op jit(solution)/shard_map/ppermute | solution.py:743
  234.5 17.0 %collective-permute-start.8 = (bf16[768,768]{1,0:T(8,128)(2,1)}, bf16[768,768]{1,0:T(8,128)(2,1)}, u32[]{:S(2)}, u32[]{:S(2)}) collective-permute-start(bf16[768,768]{1,0:T(8,128)(2,1)} %get-tuple-element.185), channel_id=1, source_target_pairs={{0,1},{1,0},{2,3},{3,2},{4,5},{5,4},{6,7},{7,6},{8,9},{9,8},{10,11... | collective-permute-start | bytes 3538952 | tf_op jit(solution)/shard_map/ppermute | solution.py:714
  234.5 28.9 %collective-permute-start.15 = (bf16[768,768]{1,0:T(8,128)(2,1)S(1)}, bf16[768,768]{1,0:T(8,128)(2,1)}, u32[]{:S(2)}, u32[]{:S(2)}) collective-permute-start(bf16[768,768]{1,0:T(8,128)(2,1)S(1)} %add_convert_fusion.9), channel_id=1, source_target_pairs={{0,2},{2,0},{1,3},{3,1},{4,6},{6,4},{5,7},{7,5},{8,10},{10,8},{9,1... | collective-permute-start | bytes 3538952 | tf_op jit(solution)/shard_map/ppermute | solution.py:740
  235.0 28.4 %collective-permute-start.14 = (bf16[768,768]{1,0:T(8,128)(2,1)}, bf16[768,768]{1,0:T(8,128)(2,1)}, u32[]{:S(2)}, u32[]{:S(2)}) collective-permute-start(bf16[768,768]{1,0:T(8,128)(2,1)} %get-tuple-element.166), channel_id=1, source_target_pairs={{0,1},{1,0},{2,3},{3,2},{4,5},{5,4},{6,7},{7,6},{8,9},{9,8},{10,11... | collective-permute-start | bytes 3538952 | tf_op jit(solution)/shard_map/ppermute | solution.py:714
  236.7 51.5 %collective-permute-start.10 = (bf16[768,768]{1,0:T(8,128)(2,1)}, bf16[768,768]{1,0:T(8,128)(2,1)}, u32[]{:S(2)}, u32[]{:S(2)}) collective-permute-start(bf16[768,768]{1,0:T(8,128)(2,1)} %get-tuple-element.182), channel_id=1, source_target_pairs={{0,1},{1,0},{2,3},{3,2},{4,5},{5,4},{6,7},{7,6},{8,9},{9,8},{10,11... | collective-permute-start | bytes 3538952 | tf_op jit(solution)/shard_map/ppermute | solution.py:714
  250.3 1.3 copy-start.8
  250.5 18.6 %collective-permute-start.12 = (bf16[768,768]{1,0:T(8,128)(2,1)S(1)}, bf16[768,768]{1,0:T(8,128)(2,1)S(1)}, u32[]{:S(2)}, u32[]{:S(2)}) collective-permute-start(bf16[768,768]{1,0:T(8,128)(2,1)S(1)} %add_convert_fusion.8), channel_id=1, source_target_pairs={{4,8},{8,4},{5,9},{9,5},{6,10},{10,6},{7,11},{11,7},{20,24},{24,20... | collective-permute-start | bytes 3538952 | tf_op jit(solution)/shard_map/ppermute | solution.py:746
  251.5 11.9 %copy-start.9 = (bf16[768,768]{1,0:T(8,128)(2,1)S(1)}, bf16[768,768]{1,0:T(8,128)(2,1)}, u32[]{:S(2)}) copy-start(bf16[768,768]{1,0:T(8,128)(2,1)} %get-tuple-element.170) | copy-start | bytes 3538948
  253.2 13.9 %copy-start.12 = (f32[9,768]{1,0:T(8,128)S(1)}, f32[9,768]{1,0:T(8,128)}, u32[]{:S(2)}) copy-start(f32[9,768]{1,0:T(8,128)} %packed_row.1) | copy-start | bytes 82948
  253.2 34.9 %collective-permute-start.11 = (bf16[768,768]{1,0:T(8,128)(2,1)S(1)}, bf16[768,768]{1,0:T(8,128)(2,1)S(1)}, u32[]{:S(2)}, u32[]{:S(2)}) collective-permute-start(bf16[768,768]{1,0:T(8,128)(2,1)S(1)} %add_convert_fusion.7), channel_id=1, source_target_pairs={{0,2},{2,0},{1,3},{3,1},{4,6},{6,4},{5,7},{7,5},{8,10},{10,8},{9,1... | collective-permute-start | bytes 3538952 | tf_op jit(solution)/shard_map/ppermute | solution.py:740
  265.5 27.7 %collective-permute-start.19 = (bf16[768,768]{1,0:T(8,128)(2,1)S(1)}, bf16[768,768]{1,0:T(8,128)(2,1)S(1)}, u32[]{:S(2)}, u32[]{:S(2)}) collective-permute-start(bf16[768,768]{1,0:T(8,128)(2,1)S(1)} %add_convert_fusion.6), channel_id=1, source_target_pairs={{0,4},{12,8},{1,5},{13,9},{2,6},{14,10},{3,7},{15,11},{16,20},{28,... | collective-permute-start | bytes 3538952 | tf_op jit(solution)/shard_map/ppermute | solution.py:743
  267.2 1.3 collective-permute-start.13
  269.1 19.0 %copy-start.10 = (bf16[768,768]{1,0:T(8,128)(2,1)S(1)}, bf16[768,768]{1,0:T(8,128)(2,1)}, u32[]{:S(2)}) copy-start(bf16[768,768]{1,0:T(8,128)(2,1)} %get-tuple-element.186) | copy-start | bytes 3538948
  269.4 39.7 %collective-permute-start.17 = (bf16[768,768]{1,0:T(8,128)(2,1)S(1)}, bf16[768,768]{1,0:T(8,128)(2,1)S(1)}, u32[]{:S(2)}, u32[]{:S(2)}) collective-permute-start(bf16[768,768]{1,0:T(8,128)(2,1)S(1)} %add_convert_fusion.5), channel_id=1, source_target_pairs={{4,0},{8,12},{5,1},{9,13},{6,2},{10,14},{7,3},{11,15},{20,16},{24,... | collective-permute-start | bytes 3538952 | tf_op jit(solution)/shard_map/ppermute | solution.py:749
  290.9 26.9 %collective-permute-start.16 = (bf16[768,768]{1,0:T(8,128)(2,1)}, bf16[768,768]{1,0:T(8,128)(2,1)}, u32[]{:S(2)}, u32[]{:S(2)}) collective-permute-start(bf16[768,768]{1,0:T(8,128)(2,1)} %add_convert_fusion.4), channel_id=1, source_target_pairs={{0,4},{12,8},{1,5},{13,9},{2,6},{14,10},{3,7},{15,11},{16,20},{28,... | collective-permute-start | bytes 3538952 | tf_op jit(solution)/shard_map/ppermute | solution.py:743
  293.6 26.9 %collective-permute-start.23 = (bf16[768,768]{1,0:T(8,128)(2,1)S(1)}, bf16[768,768]{1,0:T(8,128)(2,1)}, u32[]{:S(2)}, u32[]{:S(2)}) collective-permute-start(bf16[768,768]{1,0:T(8,128)(2,1)S(1)} %add_convert_fusion.3), channel_id=1, source_target_pairs={{4,8},{8,4},{5,9},{9,5},{6,10},{10,6},{7,11},{11,7},{20,24},{24,20... | collective-permute-start | bytes 3538952 | tf_op jit(solution)/shard_map/ppermute | solution.py:746
  295.3 4.4 %collective-permute-start.18 = (f32[9,768]{1,0:T(8,128)}, f32[9,768]{1,0:T(8,128)}, u32[]{:S(2)}, u32[]{:S(2)}) collective-permute-start(f32[9,768]{1,0:T(8,128)} %add.86), channel_id=1, source_target_pairs={{0,2},{2,0},{1,3},{3,1},{4,6},{6,4},{5,7},{7,5},{8,10},{10,8},{9,1... | collective-permute-start | bytes 82952 | tf_op jit(solution)/shard_map/ppermute | solution.py:763
  309.2 19.5 %copy-start = (bf16[768,768]{1,0:T(8,128)(2,1)}, bf16[768,768]{1,0:T(8,128)(2,1)S(1)}, u32[]{:S(2)}) copy-start(bf16[768,768]{1,0:T(8,128)(2,1)S(1)} %broadcast_select_fusion.2.refs_0_) | copy-start | bytes 3538948
  309.2 45.3 %collective-permute-start.21 = (bf16[768,768]{1,0:T(8,128)(2,1)S(1)}, bf16[768,768]{1,0:T(8,128)(2,1)}, u32[]{:S(2)}, u32[]{:S(2)}) collective-permute-start(bf16[768,768]{1,0:T(8,128)(2,1)S(1)} %broadcast_select_fusion.2.refs_0_), channel_id=1, source_target_pairs={{0,2},{2,0},{1,3},{3,1},{4,6},{6,4},{5,7},{7,5},{8,10},{10,8},{9,1... | collective-permute-start | bytes 3538952 | tf_op jit(solution)/shard_map/ppermute | solution.py:752
  319.7 34.9 %collective-permute-start.20 = (bf16[768,768]{1,0:T(8,128)(2,1)S(1)}, bf16[768,768]{1,0:T(8,128)(2,1)S(1)}, u32[]{:S(2)}, u32[]{:S(2)}) collective-permute-start(bf16[768,768]{1,0:T(8,128)(2,1)S(1)} %add_convert_fusion.2), channel_id=1, source_target_pairs={{4,8},{8,4},{5,9},{9,5},{6,10},{10,6},{7,11},{11,7},{20,24},{24,20... | collective-permute-start | bytes 3538952 | tf_op jit(solution)/shard_map/ppermute | solution.py:746
  322.0 34.2 %collective-permute-start.28 = (bf16[768,768]{1,0:T(8,128)(2,1)S(1)}, bf16[768,768]{1,0:T(8,128)(2,1)S(1)}, u32[]{:S(2)}, u32[]{:S(2)}) collective-permute-start(bf16[768,768]{1,0:T(8,128)(2,1)S(1)} %add_convert_fusion.1), channel_id=1, source_target_pairs={{4,0},{8,12},{5,1},{9,13},{6,2},{10,14},{7,3},{11,15},{20,16},{24,... | collective-permute-start | bytes 3538952 | tf_op jit(solution)/shard_map/ppermute | solution.py:749
  323.3 31.2 %collective-permute-start.22 = (f32[9,768]{1,0:T(8,128)S(1)}, f32[9,768]{1,0:T(8,128)S(1)}, u32[]{:S(2)}, u32[]{:S(2)}) collective-permute-start(f32[9,768]{1,0:T(8,128)S(1)} %add.90), channel_id=1, source_target_pairs={{0,4},{4,0},{8,12},{12,8},{1,5},{5,1},{9,13},{13,9},{2,6},{6,2},{1... | collective-permute-start | bytes 82952 | tf_op jit(solution)/shard_map/ppermute | solution.py:763
  328.7 34.3 %collective-permute-start.26 = (bf16[768,768]{1,0:T(8,128)(2,1)S(1)}, bf16[768,768]{1,0:T(8,128)(2,1)}, u32[]{:S(2)}, u32[]{:S(2)}) collective-permute-start(bf16[768,768]{1,0:T(8,128)(2,1)S(1)} %broadcast_select_fusion.2.refs_0_), channel_id=1, source_target_pairs={{0,1},{1,0},{2,3},{3,2},{4,5},{5,4},{6,7},{7,6},{8,9},{9,8},{10,11... | collective-permute-start | bytes 3538952 | tf_op jit(solution)/shard_map/ppermute | solution.py:714
  354.5 13.2 %collective-permute-start.25 = (bf16[768,768]{1,0:T(8,128)(2,1)}, bf16[768,768]{1,0:T(8,128)(2,1)}, u32[]{:S(2)}, u32[]{:S(2)}) collective-permute-start(bf16[768,768]{1,0:T(8,128)(2,1)} %collective-permute-done.21.refs_0_), channel_id=1, source_target_pairs={{0,1},{1,0},{2,3},{3,2},{4,5},{5,4},{6,7},{7,6},{8,9},{9,8},{10,11... | collective-permute-start | bytes 3538952 | tf_op jit(solution)/shard_map/ppermute | solution.py:714
  354.9 31.4 %collective-permute-start.24 = (bf16[768,768]{1,0:T(8,128)(2,1)S(1)}, bf16[768,768]{1,0:T(8,128)(2,1)}, u32[]{:S(2)}, u32[]{:S(2)}) collective-permute-start(bf16[768,768]{1,0:T(8,128)(2,1)S(1)} %add_convert_fusion), channel_id=1, source_target_pairs={{4,0},{8,12},{5,1},{9,13},{6,2},{10,14},{7,3},{11,15},{20,16},{24,... | collective-permute-start | bytes 3538952 | tf_op jit(solution)/shard_map/ppermute | solution.py:749
  356.4 11.3 %copy-start.2 = (bf16[768,768]{1,0:T(8,128)(2,1)}, bf16[768,768]{1,0:T(8,128)(2,1)S(1)}, u32[]{:S(2)}) copy-start(bf16[768,768]{1,0:T(8,128)(2,1)S(1)} %broadcast_select_fusion.1.refs_0_) | copy-start | bytes 3538948
  356.4 31.4 %collective-permute-start.30 = (bf16[768,768]{1,0:T(8,128)(2,1)S(1)}, bf16[768,768]{1,0:T(8,128)(2,1)}, u32[]{:S(2)}, u32[]{:S(2)}) collective-permute-start(bf16[768,768]{1,0:T(8,128)(2,1)S(1)} %broadcast_select_fusion.1.refs_0_), channel_id=1, source_target_pairs={{0,2},{2,0},{1,3},{3,1},{4,6},{6,4},{5,7},{7,5},{8,10},{10,8},{9,1... | collective-permute-start | bytes 3538952 | tf_op jit(solution)/shard_map/ppermute | solution.py:752
  357.3 5.8 %collective-permute-start.27 = (f32[9,768]{1,0:T(8,128)S(1)}, f32[9,768]{1,0:T(8,128)S(1)}, u32[]{:S(2)}, u32[]{:S(2)}) collective-permute-start(f32[9,768]{1,0:T(8,128)S(1)} %add.93), channel_id=1, source_target_pairs={{0,8},{4,12},{8,0},{12,4},{1,9},{5,13},{9,1},{13,5},{2,10},{6,14},... | collective-permute-start | bytes 82952 | tf_op jit(solution)/shard_map/ppermute | solution.py:763
  363.0 25.3 %collective-permute-start.32 = (bf16[768,768]{1,0:T(8,128)(2,1)S(1)}, bf16[768,768]{1,0:T(8,128)(2,1)}, u32[]{:S(2)}, u32[]{:S(2)}) collective-permute-start(bf16[768,768]{1,0:T(8,128)(2,1)S(1)} %broadcast_select_fusion.1.refs_0_), channel_id=1, source_target_pairs={{0,1},{1,0},{2,3},{3,2},{4,5},{5,4},{6,7},{7,6},{8,9},{9,8},{10,11... | collective-permute-start | bytes 3538952 | tf_op jit(solution)/shard_map/ppermute | solution.py:714
  387.8 5.3 %copy-start.1 = (bf16[768,768]{1,0:T(8,128)(2,1)}, bf16[768,768]{1,0:T(8,128)(2,1)S(1)}, u32[]{:S(2)}) copy-start(bf16[768,768]{1,0:T(8,128)(2,1)S(1)} %broadcast_select_fusion.refs_0_) | copy-start | bytes 3538948
  387.8 5.2 %collective-permute-start.31 = (bf16[768,768]{1,0:T(8,128)(2,1)}, bf16[768,768]{1,0:T(8,128)(2,1)}, u32[]{:S(2)}, u32[]{:S(2)}) collective-permute-start(bf16[768,768]{1,0:T(8,128)(2,1)} %collective-permute-done.30.refs_0_), channel_id=1, source_target_pairs={{0,1},{1,0},{2,3},{3,2},{4,5},{5,4},{6,7},{7,6},{8,9},{9,8},{10,11... | collective-permute-start | bytes 3538952 | tf_op jit(solution)/shard_map/ppermute | solution.py:714
  387.9 28.4 %collective-permute-start.29 = (bf16[768,768]{1,0:T(8,128)(2,1)S(1)}, bf16[768,768]{1,0:T(8,128)(2,1)S(1)}, u32[]{:S(2)}, u32[]{:S(2)}) collective-permute-start(bf16[768,768]{1,0:T(8,128)(2,1)S(1)} %broadcast_select_fusion.refs_0_), channel_id=1, source_target_pairs={{0,2},{2,0},{1,3},{3,1},{4,6},{6,4},{5,7},{7,5},{8,10},{10,8},{9,1... | collective-permute-start | bytes 3538952 | tf_op jit(solution)/shard_map/ppermute | solution.py:752
  387.9 38.3 %collective-permute-start.34 = (bf16[768,768]{1,0:T(8,128)(2,1)S(1)}, bf16[768,768]{1,0:T(8,128)(2,1)}, u32[]{:S(2)}, u32[]{:S(2)}) collective-permute-start(bf16[768,768]{1,0:T(8,128)(2,1)S(1)} %broadcast_select_fusion.refs_0_), channel_id=1, source_target_pairs={{0,1},{1,0},{2,3},{3,2},{4,5},{5,4},{6,7},{7,6},{8,9},{9,8},{10,11... | collective-permute-start | bytes 3538952 | tf_op jit(solution)/shard_map/ppermute | solution.py:714
  416.2 2.0 copy-start.5
  416.2 14.6 %collective-permute-start.33 = (bf16[768,768]{1,0:T(8,128)(2,1)S(1)}, bf16[768,768]{1,0:T(8,128)(2,1)S(1)}, u32[]{:S(2)}, u32[]{:S(2)}) collective-permute-start(bf16[768,768]{1,0:T(8,128)(2,1)S(1)} %collective-permute-done.29.refs_0_), channel_id=1, source_target_pairs={{0,1},{1,0},{2,3},{3,2},{4,5},{5,4},{6,7},{7,6},{8,9},{9,8},{10,11... | collective-permute-start | bytes 3538952 | tf_op jit(solution)/shard_map/ppermute | solution.py:714
  419.5 4.1 collective-permute-start.35
  430.9 1.0 copy-start.6

commit v4 on v3

v4 whole, which is shorter than its diff:
```python
import functools
import jax
import jax.numpy as jnp
from jax import lax
from jax.sharding import Mesh, PartitionSpec as P
from jax.experimental import pallas as pl
from jax.experimental.pallas import tpu as pltpu

RADIUS = 128
REACH = 64
QUERY_BLOCK = 128
EPSILON = 1e-05
NEG_FILL = -1e30
HIDDEN_TILE = 1024
SCALE = 1
GELU_C = 0.7978845608028654
F32, BF16 = jnp.float32, jnp.bfloat16
MIB = 1024 * 1024


def low(vector):
    return vector.astype(BF16)


def dot_nn(left, right):
    return jnp.dot(left, right, preferred_element_type=F32)


def dot_nt(left, right):
    return lax.dot_general(left, right, (((1,), (1,)), ((), ())), preferred_element_type=F32)


def dot_tn(left, right):
    return lax.dot_general(left, right, (((0,), (0,)), ((), ())), preferred_element_type=F32)


def normalized(vector):
    center = vector - jnp.mean(vector, axis=-1, keepdims=True)
    inverse = lax.rsqrt(jnp.mean(center * center, axis=-1, keepdims=True) + EPSILON)
    return center * inverse, inverse


def norm_backward(vector, gain_row, grad_normed):
    normed, inverse = normalized(vector)
    scaled = grad_normed * gain_row
    mean_scaled = jnp.mean(scaled, axis=-1, keepdims=True)
    mean_mixed = jnp.mean(scaled * normed, axis=-1, keepdims=True)
    grad_input = inverse * (scaled - mean_scaled - normed * mean_mixed)
    grad_gain = jnp.sum(grad_normed * normed, axis=0, keepdims=True)
    return grad_input, grad_gain, jnp.sum(grad_normed, axis=0, keepdims=True)


def live_sums(length, start, items):
    rows = items[0].shape[0]
    live = start + lax.broadcasted_iota(jnp.int32, (rows, 1), 0) < length
    return [jnp.sum(jnp.where(live, v * v, 0.0), axis=0, keepdims=True) for v in items]


def whole(shape):
    return pl.BlockSpec(shape, lambda *_: (0,) * len(shape))


def part_of(shape, doc, axis):
    place = tuple(doc if d == axis else 0 for d in range(len(shape)))
    return pl.BlockSpec(shape, lambda *_: place)


def column(row):
    return jnp.broadcast_to(row, (row.shape[1], row.shape[1])).T[:, 0:1]


def kernel_call(body, grid, in_specs, outs, scratch, flops, moved, name, aliases=None, token=None):
    taken, given = 1 + len(in_specs), len(outs)

    def with_token(*refs):
        rest = refs[taken + 1 :]
        body(*refs[:taken], *rest[:given], *rest[given + 1 :])

    if token is not None:
        in_specs = [*in_specs, pl.BlockSpec(memory_space=pl.ANY)]
        outs = [*outs, (token.shape, token.dtype, pl.BlockSpec(memory_space=pl.ANY))]
    call = pl.pallas_call(
        body if token is None else with_token,
        out_shape=[jax.ShapeDtypeStruct(shape, kind) for shape, kind, _ in outs],
        grid_spec=pltpu.PrefetchScalarGridSpec(
            num_scalar_prefetch=1,
            grid=grid,
            in_specs=in_specs,
            out_specs=[spec for _, _, spec in outs],
            scratch_shapes=scratch,
        ),
        compiler_params=pltpu.CompilerParams(
            dimension_semantics=("arbitrary",) * len(grid), vmem_limit_bytes=60 * MIB
        ),
        cost_estimate=pl.CostEstimate(flops=SCALE * int(flops), bytes_accessed=SCALE * int(moved), transcendentals=0),
        input_output_aliases=aliases or {},
        name=name,
    )
    return call if token is None else lambda *operands: call(*operands, token)


ANYWHERE = pl.BlockSpec(memory_space=pl.ANY)
PARTS = 2


def row_parts(rows):
    return [(at, pl.ds(at, rows // PARTS)) for at in range(0, rows, rows // PARTS)]


class Copies:
    def __init__(self, semaphores):
        self.semaphores, self.used, self.pending = semaphores, 0, []

    def start(self, source, target):
        copy = pltpu.make_async_copy(source, target, self.semaphores.at[self.used])
        self.used += 1
        copy.start()
        return copy

    def leave(self, source, target):
        self.pending.append(self.start(source, target))

    def finish(self):
        for copy in self.pending:
            copy.wait()


def add_rows(ref, rows, values):
    for at, value in zip(rows, values):
        ref[at : at + 1, :] += value


def feed_forward(resid_ref, gain, shift, up_ref, bias_ref, down_ref, normed_ref, active_ref, slope_ref, sum_ref):
    rows, hidden = active_ref.shape
    for _, own in row_parts(rows):
        normed_ref[own, :] = low(normalized(resid_ref[own, :])[0] * gain + shift)
    sum_ref[...] = jnp.zeros_like(sum_ref)

    def tile(index, carry):
        columns = pl.ds(pl.multiple_of(index * HIDDEN_TILE, HIDDEN_TILE), HIDDEN_TILE)
        parts = [own for _, own in row_parts(rows)]
        pres = [dot_nn(normed_ref[own, :], up_ref[:, columns]) + bias_ref[:, columns] for own in parts]
        for own, pre in zip(parts, pres):
            square = pre * pre
            curve = jnp.tanh(pre * (GELU_C + GELU_C * 0.044715 * square))
            half = 0.5 + 0.5 * curve
            active = low(pre * half)
            active_ref[own, columns] = active
            rise = pre * (GELU_C + 3.0 * GELU_C * 0.044715 * square)
            slope_ref[own, columns] = low(half + rise * (half - half * half) * 2.0)
            sum_ref[own, :] += dot_nn(active, down_ref[columns, :])
        return carry

    lax.fori_loop(0, hidden // HIDDEN_TILE, tile, 0)


def feed_backward_tile(columns, grad_ref, slope_ref, up_ref, down_ref, pre_ref, bias_ref, sum_ref):
    total = None
    for _, own in row_parts(grad_ref.shape[0]):
        grad_active = dot_nt(grad_ref[own, :], down_ref[columns, :])
        grad_pre = low(slope_ref[own, columns].astype(F32) * grad_active)
        pre_ref[own, columns] = grad_pre
        here = jnp.sum(grad_pre.astype(F32), axis=0, keepdims=True)
        total = here if total is None else total + here
        sum_ref[own, :] += dot_nt(grad_pre, up_ref[:, columns])
    bias_ref[:, columns] = total


def norm_back(out_ref, grad_ref, vector_ref, gain, sum_ref, gain_ref, shift_ref, at):
    gain_ref[at : at + 1, :] = jnp.zeros_like(gain)
    shift_ref[at : at + 1, :] = jnp.zeros_like(gain)
    for _, own in row_parts(out_ref.shape[0]):
        grad_input, grad_gain, grad_shift = norm_backward(vector_ref[own, :].astype(F32), gain, sum_ref[own, :])
        out_ref[own, :] = (grad_ref[own, :].astype(F32) + grad_input).astype(out_ref.dtype)
        gain_ref[at : at + 1, :] += grad_gain
        shift_ref[at : at + 1, :] += grad_shift


def graph_windows(rows):
    span = QUERY_BLOCK + 2 * REACH
    return [
        (start, min(max(start - REACH, 0), rows - span), span)
        for start in range(0, rows, QUERY_BLOCK)
    ]


def layer_one_forward_body(
    length_ref, x_ref, near_ref_t, counts_ref, gain_ref, shift_ref, bias_ref, w_any, up_any, down_any,
    mid_ref, stat_ref, link_ref, left_any, sigma_any, pull_any, resid_any, normed_any, active_any, slope_any,
    w_ref, up_ref, down_ref, left_ref, sigma_ref, pull_ref, resid_ref, normed_ref, active_ref, slope_ref, sum_ref,
    semaphores,
):
    @pl.when(length_ref[1] == 1)
    def _():
        rows, width = x_ref.shape
        length = length_ref[0]
        copies = Copies(semaphores)
        w_copies = [copies.start(w_any.at[i], w_ref.at[i]) for i in range(4)]
        up_copy, down_copy = copies.start(up_any, up_ref), copies.start(down_any, down_ref)
        graph_normed, mean_ref, mixed_ref = (left_ref.at[i] for i in range(3))
        stat_ref[...] = jnp.zeros_like(stat_ref)
        for _, own in row_parts(rows):
            graph_normed[own, :] = low(
                normalized(x_ref[own, :].astype(F32))[0] * gain_ref[0:1, :] + shift_ref[0:1, :]
            )
        slots = near_ref_t.shape[0]
        slot = lax.broadcasted_iota(jnp.int32, (slots, QUERY_BLOCK), 0)
        for row, start, span in graph_windows(rows):
            own = pl.ds(row, QUERY_BLOCK)
            counts = counts_ref[:, own]
            index = jnp.where(slot < counts, near_ref_t[:, own], -1)
            place = start + lax.broadcasted_iota(jnp.int32, (span, QUERY_BLOCK), 0)
            links = jnp.zeros((span, QUERY_BLOCK), F32)
            for s in range(slots):
                links += jnp.where(index[s : s + 1, :] == place, 1.0, 0.0)
            link_ref[:, own] = low(links)
            total = dot_nn(low(links.T), graph_normed[pl.ds(start, span), :])
            mean_ref[own, :] = low(total / column(counts.astype(F32)))
        for copy in w_copies:
            copy.wait()
        for at, own in row_parts(rows):
            pre = dot_nn(graph_normed[own, :], w_ref[0]) + dot_nn(mean_ref[own, :], w_ref[1])
            sigma = jax.nn.sigmoid(dot_nn(mean_ref[own, :], w_ref[2]))
            mixed = pre * sigma
            sigma_ref[own, :] = low(sigma)
            pull_ref[own, :] = low(mixed - mixed * sigma)
            mixed_ref[own, :] = low(mixed)
            branch = dot_nn(low(mixed), w_ref[3])
            resid = x_ref[own, :].astype(F32) + branch
            resid_ref[own, :] = resid
            add_rows(stat_ref, (0, 1), live_sums(length, at, (branch, resid)))
        copies.leave(left_ref, left_any)
        copies.leave(sigma_ref, sigma_any)
        copies.leave(pull_ref, pull_any)
        copies.leave(resid_ref, resid_any)
        up_copy.wait()
        down_copy.wait()
        feed_forward(
            resid_ref, gain_ref[1:2, :], shift_ref[1:2, :], up_ref, bias_ref, down_ref,
            normed_ref, active_ref, slope_ref, sum_ref,
        )
        copies.leave(normed_ref, normed_any)
        copies.leave(active_ref, active_any)
        copies.leave(slope_ref, slope_any)
        for at, own in row_parts(rows):
            branch = sum_ref[own, :]
            result = resid_ref[own, :] + branch
            mid_ref[own, :] = low(result)
            add_rows(stat_ref, (2, 3), live_sums(length, at, (branch, result)))
        copies.finish()


def layer_one_forward(length, x, doc, rows, near_t, counts, gain, shift, bias, weights, up, down):
    width, hidden = up.shape
    slots = near_t.shape[0]
    span = QUERY_BLOCK + 2 * REACH
    flat, wide = ((rows, width), BF16), ((rows, hidden), BF16)
    kept = [((3, rows, width), BF16), flat, flat, ((rows, width), F32), flat, wide, wide]
    return kernel_call(
        layer_one_forward_body,
        (1,),
        [
            part_of((rows, width), doc, 0), part_of((slots, rows), doc, 1), part_of((1, rows), doc, 1),
            whole((2, width)), whole((2, width)), whole((1, hidden)), ANYWHERE, ANYWHERE, ANYWHERE,
        ],
        [
            ((rows, width), BF16, whole((rows, width))),
            ((4, width), F32, whole((4, width))),
            ((span, rows), BF16, whole((span, rows))),
        ]
        + [(*what, ANYWHERE) for what in kept],
        [pltpu.VMEM(v.shape, BF16) for v in (weights, up, down)]
        + [pltpu.VMEM(*what) for what in kept]
        + [pltpu.VMEM((rows, width), F32), pltpu.SemaphoreType.DMA((13,))],
        8 * rows * width * width + 4 * rows * width * hidden,
        16 * rows * width + 8 * width * width + 4 * (rows + width) * hidden,
        "layer_one_forward",
    )(length, x, near_t, counts, gain, shift, bias, weights, up, down)


def layer_one_backward_body(
    length_ref, grad_ref, x_ref, gain_ref, counts_ref, link_ref,
    resid_any, slope_any, sigma_any, pull_any, w_any, up_any, down_any, pre_given, right_given,
    out_ref, bias_out, gain_out, shift_out, pre_any, right_any,
    resid_ref, slope_ref, sigma_ref, pull_ref, w_ref, up_ref, down_ref,
    pre_ref, right_ref, grad_resid, mean_ref, sum_ref,
    semaphores,
):
    @pl.when(length_ref[1] == 1)
    def _():
        rows, width = x_ref.shape
        hidden = slope_ref.shape[1]
        copies = Copies(semaphores)
        tiles = [pl.ds(at, HIDDEN_TILE) for at in range(0, hidden, HIDDEN_TILE)]
        arriving = [
            [
                copies.start(down_any.at[columns, :], down_ref.at[columns, :]),
                copies.start(slope_any.at[:, columns], slope_ref.at[:, columns]),
                copies.start(up_any.at[:, columns], up_ref.at[:, columns]),
            ]
            for columns in tiles
        ]
        resid_copy = copies.start(resid_any, resid_ref)
        w_copies = [copies.start(w_any.at[i], w_ref.at[i]) for i in range(4)]
        gate_copies = [copies.start(sigma_any, sigma_ref), copies.start(pull_any, pull_ref)]
        counts_column = column(counts_ref[...].astype(F32))
        sum_ref[...] = jnp.zeros_like(sum_ref)
        for columns, parts in zip(tiles, arriving):
            for copy in parts:
                copy.wait()
            feed_backward_tile(columns, grad_ref, slope_ref, up_ref, down_ref, pre_ref, bias_out, sum_ref)
        copies.leave(pre_ref, pre_any)
        resid_copy.wait()
        norm_back(grad_resid, grad_ref, resid_ref, gain_ref[1:2, :], sum_ref, gain_out, shift_out, 1)
        for copy in w_copies + gate_copies:
            copy.wait()
        for at, own in row_parts(rows):
            grad_low = low(grad_resid[own, :])
            right_ref[2, own, :] = grad_low
            grad_mixed = dot_nt(grad_low, w_ref[3])
            grad_pre = low(sigma_ref[own, :].astype(F32) * grad_mixed)
            grad_gate = low(pull_ref[own, :].astype(F32) * grad_mixed)
            right_ref[0, own, :] = grad_pre
            right_ref[1, own, :] = grad_gate
            sum_ref[own, :] = dot_nt(grad_pre, w_ref[0])
            grad_mean = dot_nt(grad_pre, w_ref[1]) + dot_nt(grad_gate, w_ref[2])
            mean_ref[own, :] = low(grad_mean / counts_column[at : at + rows // PARTS, :])
        copies.leave(right_ref, right_any.at[0:3])
        for row, start, span in graph_windows(rows):
            own = pl.ds(row, QUERY_BLOCK)
            sum_ref[pl.ds(start, span), :] += dot_nn(link_ref[:, own], mean_ref[own, :])
        norm_back(out_ref, grad_resid, x_ref, gain_ref[0:1, :], sum_ref, gain_out, shift_out, 0)
        copies.finish()


def layer_one_backward(length, grad, x, doc, gain, counts, links, resid, slope, sigma, pull, weights, up, down, pre, right, token=None):
    rows, width = grad.shape
    hidden = slope.shape[1]
    full = whole((rows, width))
    sent = [((rows, hidden), BF16), ((3, rows, width), BF16)]
    return kernel_call(
        layer_one_backward_body,
        (1,),
        [
            full, part_of((rows, width), doc, 0), whole((2, width)), part_of((1, rows), doc, 1), whole(links.shape),
        ]
        + [ANYWHERE] * 9,
        [
            ((rows, width), BF16, full),
            ((1, hidden), F32, whole((1, hidden))),
            ((2, width), F32, whole((2, width))),
            ((2, width), F32, whole((2, width))),
        ]
        + [(pre.shape, BF16, ANYWHERE), (right.shape, BF16, ANYWHERE)],
        [pltpu.VMEM(v.shape, v.dtype) for v in (resid, slope, sigma, pull, weights, up, down)]
        + [pltpu.VMEM(*what) for what in sent]
        + [
            pltpu.VMEM((rows, width), F32),
            pltpu.VMEM((rows, width), BF16),
            pltpu.VMEM((rows, width), F32),
            pltpu.SemaphoreType.DMA((3 * (hidden // HIDDEN_TILE) + 9,)),
        ],
        8 * rows * width * width + 4 * rows * width * hidden,
        18 * rows * width + 8 * width * width + 4 * (rows + width) * hidden,
        "layer_one_backward",
        {13: 4, 14: 5},
        token,
    )(length, grad, x, gain, counts, links, resid, slope, sigma, pull, weights, up, down, pre, right)


def attend_windows(rows):
    windows, offset = [], 0
    for row in range(0, rows, QUERY_BLOCK):
        start = max(row - RADIUS, 0)
        span = min(row + QUERY_BLOCK + RADIUS, rows) - start
        windows.append((row, start, span, offset))
        offset += span
    return windows, offset


def two_heads(block, lane):
    zero = jnp.zeros_like(block)
    return jnp.concatenate([jnp.where(lane, block, zero), jnp.where(lane, zero, block)], axis=0)


def layer_two_body(
    length_ref, mid_ref, cotangent_ref, coords_ref, rich_ref, gain_ref, shift_ref, bias_ref, w_any, up_any, down_any,
    left_given, normed_given, active_given,
    out_ref, result_ref, stat_ref, bias_out, gain_out, shift_out, rich_out,
    left_any, right_any, normed_any, active_any, pre_any,
    left_ref, right_ref, normed_ref, active_ref, pre_ref,
    w_ref, up_ref, down_ref, query_ref, key_ref, value_ref, probs_ref, terms_ref, mask_ref, slope_ref, resid_ref,
    grad_ref, sum_ref, key_sum, value_sum, turned_ref, turned_sum, semaphores,
):
    @pl.when(length_ref[1] == 0)
    def _():
        rows, width = mid_ref.shape
        hidden = active_ref.shape[1]
        heads = rich_ref.shape[1]
        head_width = width // heads
        scale = head_width ** (-0.5)
        length = length_ref[0]
        windows, _ = attend_windows(rows)
        copies = Copies(semaphores)
        w_copies = [copies.start(w_any.at[i], w_ref.at[i]) for i in range(4)]
        attend_normed, context_ref = left_ref.at[0], left_ref.at[1]
        stat_ref[...] = jnp.zeros_like(stat_ref)

        for row, start, span, offset in windows:
            i = row + lax.broadcasted_iota(jnp.int32, (span, QUERY_BLOCK), 1)
            j = start + lax.broadcasted_iota(jnp.int32, (span, QUERY_BLOCK), 0)
            allowed = (jnp.abs(i - j) <= RADIUS) & ((j < length) | (i == j))
            mask_ref[pl.ds(offset, span), :] = jnp.where(allowed, 0.0, NEG_FILL)
            across = coords_ref[:, pl.ds(row, QUERY_BLOCK)]
            along = [
                jnp.broadcast_to(coords_ref[:, pl.ds(at, QUERY_BLOCK)], (QUERY_BLOCK, QUERY_BLOCK)).T
                for at in range(start, start + span, QUERY_BLOCK)
            ]
            gap = across - jnp.concatenate(along, axis=0)
            terms_ref[0, pl.ds(offset, span), :] = jnp.log(1.0 + jnp.abs(gap))
            terms_ref[1, pl.ds(offset, span), :] = jnp.tanh(-gap)
        for copy in w_copies:
            copy.wait()
        up_copy, down_copy = copies.start(up_any, up_ref), copies.start(down_any, down_ref)
        for _, own in row_parts(rows):
            normed = low(normalized(mid_ref[own, :].astype(F32))[0] * gain_ref[0:1, :] + shift_ref[0:1, :])
            attend_normed[own, :] = normed
            query_ref[own, :] = low(dot_nn(normed, w_ref[0]))
            key_ref[own, :] = low(dot_nn(normed, w_ref[1]))
            value = dot_nn(normed, w_ref[2])
            value_ref[own, :] = low(value)
            turned_ref[:, own] = low(value.T)
        lane = lax.broadcasted_iota(jnp.int32, (QUERY_BLOCK, 2 * head_width), 1) < head_width

        def pair_of(index):
            return pl.ds(pl.multiple_of(index * 2 * head_width, 2 * head_width), 2 * head_width)

        def head_of(index, side):
            return pl.ds(pl.multiple_of((2 * index + side) * head_width, head_width), head_width)

        def attend(index, carry):
            columns = pair_of(index)
            for row, start, span, offset in windows:
                queries = two_heads(query_ref[pl.ds(row, QUERY_BLOCK), columns], lane)
                raw = dot_nt(key_ref[pl.ds(start, span), columns], queries)
                spread = terms_ref[0, pl.ds(offset, span), :]
                order = terms_ref[1, pl.ds(offset, span), :]
                mask = mask_ref[pl.ds(offset, span), :]
                for side in range(2):
                    head = 2 * index + side
                    own = raw[:, side * QUERY_BLOCK : (side + 1) * QUERY_BLOCK]
                    scores = own * scale + (spread * rich_ref[0, head] + order * rich_ref[1, head]) + mask
                    weights = jnp.exp(scores - jnp.max(scores, axis=0, keepdims=True))
                    probs = low(weights * (1.0 / jnp.sum(weights, axis=0, keepdims=True)))
                    probs_ref[index, pl.ds(offset, span), pl.ds(side * QUERY_BLOCK, QUERY_BLOCK)] = probs
                    place = head_of(index, side)
                    turned_sum[place, pl.ds(row, QUERY_BLOCK)] = dot_nn(
                        turned_ref[place, pl.ds(start, span)], probs
                    )
            return carry

        lax.fori_loop(0, heads // 2, attend, 0, unroll=2)
        for at, own in row_parts(rows):
            context = low(turned_sum[:, own].T)
            context_ref[own, :] = context
            branch = dot_nn(context, w_ref[3])
            resid = mid_ref[own, :].astype(F32) + branch
            resid_ref[own, :] = resid
            add_rows(stat_ref, (0, 1), live_sums(length, at, (branch, resid)))
        copies.leave(left_ref, left_any.at[0:2])

        up_copy.wait()
        down_copy.wait()
        feed_forward(
            resid_ref, gain_ref[1:2, :], shift_ref[1:2, :], up_ref, bias_ref, down_ref,
            normed_ref, active_ref, slope_ref, sum_ref,
        )
        copies.leave(normed_ref, normed_any)
        copies.leave(active_ref, active_any)
        for at, own in row_parts(rows):
            branch = sum_ref[own, :]
            result = resid_ref[own, :] + branch
            result_ref[own, :] = low(result)
            add_rows(stat_ref, (2, 3), live_sums(length, at, (branch, result)))
        sum_ref[...] = jnp.zeros_like(sum_ref)

        def tile(index, carry):
            columns = pl.ds(pl.multiple_of(index * HIDDEN_TILE, HIDDEN_TILE), HIDDEN_TILE)
            feed_backward_tile(columns, cotangent_ref, slope_ref, up_ref, down_ref, pre_ref, bias_out, sum_ref)
            return carry

        lax.fori_loop(0, hidden // HIDDEN_TILE, tile, 0)
        copies.leave(pre_ref, pre_any)
        norm_back(grad_ref, cotangent_ref, resid_ref, gain_ref[1:2, :], sum_ref, gain_out, shift_out, 1)

        grad_context = right_ref.at[0]
        for _, own in row_parts(rows):
            grad_low = low(grad_ref[own, :])
            right_ref[3, own, :] = grad_low
            grad_context[own, :] = low(dot_nt(grad_low, w_ref[3]))
            turned_ref[:, own] = low(key_ref[own, :].astype(F32).T)
        key_sum[...] = jnp.zeros_like(key_sum)
        value_sum[...] = jnp.zeros_like(value_sum)

        def attend_back(index, carry):
            columns = pair_of(index)
            rich = [[0.0, 0.0], [0.0, 0.0]]
            for row, start, span, offset in windows:
                keys = pl.ds(start, span)
                context = two_heads(grad_context[pl.ds(row, QUERY_BLOCK), columns], lane)
                queries = two_heads(query_ref[pl.ds(row, QUERY_BLOCK), columns], lane)
                grad_probs = dot_nt(value_ref[keys, columns], context)
                probs = probs_ref[index, pl.ds(offset, span), :]
                value_sum[keys, columns] += dot_nn(probs, context)
                spread = terms_ref[0, pl.ds(offset, span), :]
                order = terms_ref[1, pl.ds(offset, span), :]
                grads = []
                for side in range(2):
                    lanes = slice(side * QUERY_BLOCK, (side + 1) * QUERY_BLOCK)
                    own = probs[:, lanes].astype(F32)
                    mixed = own * grad_probs[:, lanes]
                    grad_scores = mixed - own * jnp.sum(mixed, axis=0, keepdims=True)
                    rich[0][side] += jnp.sum(grad_scores * spread, axis=0, keepdims=True)
                    rich[1][side] += jnp.sum(grad_scores * order, axis=0, keepdims=True)
                    grad_raw = low(grad_scores * scale)
                    grads.append(grad_raw)
                    place = head_of(index, side)
                    turned_sum[place, pl.ds(row, QUERY_BLOCK)] = dot_nn(turned_ref[place, keys], grad_raw)
                key_sum[keys, columns] += dot_nn(jnp.concatenate(grads, axis=1), queries)
            for which in range(2):
                for side in range(2):
                    rich_out[which, pl.ds(2 * index + side, 1), :] = rich[which][side]
            return carry

        lax.fori_loop(0, heads // 2, attend_back, 0)
        for _, own in row_parts(rows):
            grad_query = low(turned_sum[:, own].T)
            grad_key = low(key_sum[own, :])
            grad_value = low(value_sum[own, :])
            right_ref[0, own, :] = grad_query
            right_ref[1, own, :] = grad_key
            right_ref[2, own, :] = grad_value
            sum_ref[own, :] = (
                dot_nt(grad_query, w_ref[0]) + dot_nt(grad_key, w_ref[1]) + dot_nt(grad_value, w_ref[2])
            )
        copies.leave(right_ref, right_any)
        norm_back(out_ref, grad_ref, mid_ref, gain_ref[0:1, :], sum_ref, gain_out, shift_out, 0)
        copies.finish()


def layer_two(length, mid, cotangent, doc, coords, rich, gain, shift, bias, weights, up, down, left, normed, active):
    rows, width = mid.shape
    hidden = up.shape[1]
    heads = rich.shape[1]
    full = whole((rows, width))
    _, band = attend_windows(rows)
    flat, wide = ((rows, width), BF16), ((rows, hidden), BF16)
    sent = [((2, rows, width), BF16), ((4, rows, width), BF16), flat, wide, wide]
    exact = ((rows, width), F32)
    held = [
        flat, flat, flat, ((heads // 2, band, 2 * QUERY_BLOCK), BF16), ((2, band, QUERY_BLOCK), F32),
        ((band, QUERY_BLOCK), F32), wide, exact, exact, exact, exact, exact, ((width, rows), BF16), ((width, rows), F32),
    ]
    return kernel_call(
        layer_two_body,
        (1,),
        [
            full, part_of((rows, width), doc, 0), part_of((1, rows), doc, 1), pl.BlockSpec(memory_space=pltpu.SMEM),
            whole((2, width)), whole((2, width)), whole((1, hidden)),
        ]
        + [ANYWHERE] * 6,
        [
            (*flat, full),
            (*flat, full),
            ((4, width), F32, whole((4, width))),
            ((1, hidden), F32, whole((1, hidden))),
            ((2, width), F32, whole((2, width))),
            ((2, width), F32, whole((2, width))),
            ((2, heads, QUERY_BLOCK), F32, whole((2, heads, QUERY_BLOCK))),
        ]
        + [(left.shape, BF16, ANYWHERE)]
        + [(*what, ANYWHERE) for what in sent[1:]],
        [pltpu.VMEM(*what) for what in sent]
        + [pltpu.VMEM(v.shape, BF16) for v in (weights, up, down)]
        + [pltpu.VMEM(*what) for what in held]
        + [pltpu.SemaphoreType.DMA((11,))],
        16 * rows * width * width + 8 * rows * width * hidden + 12 * band * QUERY_BLOCK * width,
        20 * rows * width + 8 * width * width + 4 * (rows + width) * hidden,
        "layer_two",
        {11: 7, 12: 9, 13: 10},
    )(length, mid, cotangent, coords, rich, gain, shift, bias, weights, up, down, left, normed, active)


def weight_body(count, adds, picks_ref, *refs):
    lefts, rights, outs = refs[:count], refs[count : -2 - adds], refs[-2:]
    step = pl.program_id(0)

    def write(right_refs):
        total = None
        for left_ref, right_ref in zip(lefts, right_refs):
            left, right = (v[...].reshape(v.shape[-2:]) for v in (left_ref, right_ref))
            here = dot_tn(left, right)
            total = here if total is None else total + here
        for at in range(2):

            @pl.when(step == at)
            def _():
                outs[at][...] = low(total + refs[-3][...].astype(F32) if adds and at == 0 else total)

    if len(rights) == count:
        write(rights)
        return
    for which in range(2):

        @pl.when(picks_ref[0] == which)
        def _():
            write(rights[which * count : (which + 1) * count])


def weight_quarters(picks, lefts, rights, rights_one, arrived, name, token=None):
    count = len(lefts)
    specs, operands = [], []
    for array, shape, place in lefts + rights + (rights_one or []):
        operands.append(array)
        specs.append(pl.BlockSpec(shape, lambda j, chosen, place=place: place(chosen[0], chosen[1 + j])))
    width, rows = rights[0][1][-1], lefts[0][1][-2]
    quarter = (width, width)
    if arrived is not None:
        operands.append(arrived)
        specs.append(whole(quarter))
    return kernel_call(
        functools.partial(weight_body, count, int(arrived is not None)),
        (2,),
        specs,
        [(quarter, BF16, whole(quarter))] * 2,
        [],
        4 * width * width * count * rows,
        8 * width * width + 8 * count * rows * width,
        name,
        None,
        token,
    )(picks, *operands)


def place_body(count, places_ref, *refs):
    out_ref, copy_ref = refs[-2:]
    for at, piece in enumerate(refs[:count]):

        @pl.when(pl.program_id(0) == at)
        def _():
            out_ref[...] = piece[...].astype(F32)

    @pl.when(pl.program_id(0) == 0)
    def _():
        copy_ref[...] = refs[0][...]


def placed(places, first, pieces, shape, columns, into, name, token):
    width = pieces[0].shape[0]

    def index(i, where):
        return (0, where[first + i]) if columns else (where[first + i], 0)

    more = [] if into is None else [into]
    quarter = whole((width, width))
    return kernel_call(
        functools.partial(place_body, len(pieces)),
        (len(pieces),),
        [quarter] * len(pieces) + [ANYWHERE] * len(more),
        [(shape, F32, pl.BlockSpec((width, width), index)), ((width, width), BF16, quarter)],
        [],
        0,
        6 * len(pieces) * width * width,
        name,
        {1 + len(pieces): 0} if more else {},
        token,
    )(places, *pieces, *more)


def pack_body(docs, flag_ref, lengths_ref, *refs):
    sides = {1: refs[: 4 * docs], 0: refs[4 * docs : 8 * docs]}
    rich_refs, out_ref = refs[8 * docs : 9 * docs], refs[9 * docs]
    width = out_ref.shape[1]

    def spread(values, base):
        sums = jnp.sum(values, axis=1, keepdims=True)
        shape = (values.shape[0], width)
        lane = lax.broadcasted_iota(jnp.int32, shape, 1)
        row = lax.broadcasted_iota(jnp.int32, shape, 0)
        return jnp.sum(jnp.where(lane == base + row, sums, 0.0), axis=0, keepdims=True)

    for which, side in sides.items():

        @pl.when(flag_ref[0] == which)
        def _():
            bias, gain, shift, stat = (sum(side[4 * d + i][...] for d in range(docs)) for i in range(4))
            for at in range(0, bias.shape[1], width):
                out_ref[at // width : at // width + 1, :] = bias[:, at : at + width]
            base = bias.shape[1] // width
            out_ref[base : base + 2, :] = gain
            out_ref[base + 2 : base + 4, :] = shift
            scalars = spread(stat, 0 if which else stat.shape[0])
            if not which:
                heads = rich_refs[0].shape[1]
                for term in range(2):
                    total = sum(ref[term] for ref in rich_refs)
                    scalars += spread(total, 2 * stat.shape[0] + term * heads)
                count = lengths_ref[0]
                for d in range(1, docs):
                    count += lengths_ref[d]
                lane = lax.broadcasted_iota(jnp.int32, (1, width), 1)
                scalars += jnp.where(lane == 2 * (stat.shape[0] + heads), count.astype(F32), 0.0)
            out_ref[base + 4 : base + 5, :] = scalars
            out_ref[base + 5 :, :] = jnp.zeros((out_ref.shape[0] - base - 5, width), F32)


def packed_row(flag, lengths, one, two, rich, token=None):
    docs = len(one)
    width = one[0][1].shape[1]
    operands = [v for side in (one, two) for parts in side for v in parts] + list(rich)
    rows = -(-(one[0][0].shape[1] // width + 5) // 8) * 8
    return kernel_call(
        functools.partial(pack_body, docs),
        (1,),
        [pl.BlockSpec(memory_space=pltpu.SMEM)] + [whole(v.shape) for v in operands],
        [((rows, width), F32, whole((rows, width)))],
        [],
        0,
        4 * sum(v.size for v in operands),
        "packed_row",
        None,
        token,
    )(flag, lengths, *operands)


def rows_body(docs, flag_ref, *refs):
    out_ref = refs[2 * docs]
    for doc in range(docs):
        for which in range(2):

            @pl.when((flag_ref[0] == which) & (pl.program_id(0) == doc))
            def _():
                out_ref[...] = refs[(1 - which) * docs + doc][...]


def section_rows(flag, one, two):
    docs = len(one)
    rows, width = one[0].shape
    return kernel_call(
        functools.partial(rows_body, docs),
        (docs,),
        [whole((rows, width))] * (2 * docs),
        [((docs * rows, width), one[0].dtype, pl.BlockSpec((rows, width), lambda i, *_: (i, 0)))],
        [],
        0,
        4 * docs * rows * width,
        "section_rows",
    )(flag, *one, *two)


def sum_body(flag_ref, left_ref, right_ref, out_ref):
    out_ref[...] = left_ref[...] + right_ref[...]


def summed(flag, left, right, token):
    return kernel_call(
        sum_body,
        (1,),
        [whole(left.shape)] * 2,
        [(left.shape, left.dtype, whole(left.shape))],
        [],
        0,
        12 * left.size,
        "small_sum",
        None,
        token,
    )(flag, left, right)


STEPS = (
    "d", "d", "D", "back", "pack", "u", "q", "D", "u", "U", "s", "D",
    "s", "S", "U", "D", "U", "D", "S", "rows", "S", "U", "S", "U",
    "S", "q", "ad", "q", "bu", "q", "ns", "fs", "ou", "os",
)


def passed_along(block, axis, distance):
    devices = range(lax.axis_size(axis))
    route = [(i - distance, i) for i in devices if i - distance in devices]
    return lax.ppermute(block, axis, route)


def after(value, token):
    return lax.optimization_barrier((value, token))[0]


def core_swap(block):
    return lax.ppermute(block, "core", [(0, 1), (1, 0)])


class Ordered:
    def __init__(self):
        self.token = None

    def read(self, *values):
        if self.token is None:
            return values if len(values) > 1 else values[0]
        values = lax.optimization_barrier((*values, self.token))[:-1]
        return values if len(values) > 1 else values[0]

    def gave(self, value):
        self.token = value
        return value


def rounded_sum(*blocks):
    return low(sum(block.astype(F32) for block in blocks))


def chips_sum(order, sent, kept):
    across_x = [(0, 1), (1, 0)]
    neighbours = [(0, 1), (1, 0), (2, 3), (3, 2)]
    partners = [(1, 2), (2, 1), (0, 3), (3, 0)]
    z = lax.axis_index("z")
    middle = (z == 1) | (z == 2)
    half = sent.shape[0] // 2
    arrived = lax.ppermute(sent, "x", across_x)
    yield
    parts = (*kept, order.read(arrived))

    def half_of(start):
        return rounded_sum(*(lax.dynamic_slice_in_dim(part, start, half, 0) for part in parts))

    other = half_of(jnp.where(middle, half, 0))
    arrived = lax.ppermute(other, "z", neighbours)
    mine = order.gave(half_of(jnp.where(middle, 0, half)))
    yield
    mine = order.gave(rounded_sum(mine, order.read(arrived)))
    arrived = lax.ppermute(mine, "z", partners)
    yield
    mine = order.gave(rounded_sum(mine, order.read(arrived)))
    arrived = lax.ppermute(mine, "z", neighbours)
    yield
    other = order.read(arrived)
    total = jnp.concatenate([jnp.where(middle, mine, other), jnp.where(middle, other, mine)], axis=0)
    order.gave(total)
    yield total, core_swap(total), lax.ppermute(total, "x", across_x)


def small_sum(flag, block, totals, axes):
    for axis in axes:
        step = 1
        while step < lax.axis_size(axis):
            route = [(i, i ^ step) for i in range(lax.axis_size(axis))]
            arrived = lax.ppermute(block, axis, route)
            yield
            block, totals["token"] = summed(flag, block, arrived, totals["token"])
            step *= 2
    yield block


def local(
    boundary,
    lengths,
    neighbours,
    counts,
    coords,
    square_weights,
    up_weight,
    down_weight,
    up_bias,
    norm_gain,
    norm_bias,
    rich_terms,
):
    first = lax.axis_index("section") == 0
    core, across_x = lax.axis_index("core"), lax.axis_index("x")
    if lax.axis_size("z") != 4 or lax.axis_size("x") != 2:
        across_x = across_x * 0
    use_one = first.astype(jnp.int32)
    keep = jnp.stack([use_one, 2 * core + 1 - across_x, 2 * core + across_x])
    give = jnp.stack([use_one, 2 * (1 - core) + 1 - across_x, 2 * (1 - core) + across_x])
    places = jnp.stack([keep[2], 2 - 4 * core + keep[2], keep[1], 2 - 4 * core + keep[1]])
    documents = lengths.shape[0]
    docs = range(documents)
    rows = boundary.shape[1] // documents
    width = boundary.shape[2]
    hidden = up_weight.shape[2]
    heads = rich_terms.shape[1]
    source = boundary[0]
    squares = square_weights[0]
    up, down, bias = up_weight[0], down_weight[0], up_bias
    gains, shifts = norm_gain[0], norm_bias[0]
    near_t = neighbours.T
    counts_row, coords_row = counts[None], coords[None]
    about = [jnp.stack([lengths[doc], use_one]) for doc in docs]

    kept_one, arrived, stats_one = [], [], []
    sent = None
    for doc in docs:
        here = source if sent is None else after(source, sent)
        sent, stat, links, left, sigma, pull, resid, normed, active, slope = layer_one_forward(
            about[doc], here, doc, rows, near_t, counts_row, gains, shifts, bias, squares, up, down
        )
        kept_one.append((links, resid, slope, sigma, pull, left, normed, active))
        stats_one.append(stat)
        arrived.append(passed_along(sent, "section", 1))

    back, out_two, rich_two, kept, small_two = [], [], [], [], []
    for doc in docs:
        grad_mid, result, stat, bias_grad, gain_grad, shift_grad, rich, left, right, normed, active, pre = layer_two(
            about[doc], arrived[doc], source, doc, coords_row, rich_terms, gains, shifts, bias, squares, up, down,
            *kept_one[doc][5:]
        )
        out_two.append(result)
        kept.append([left, right, normed, active, pre])
        small_two.append((bias_grad, gain_grad, shift_grad, stat))
        rich_two.append(rich)
        back.append(passed_along(grad_mid, "section", -1))
        last_sent = grad_mid

    out_one, small_one = [], []

    def first_back(doc, grad_mid, token=None):
        links, resid, slope, sigma, pull = kept_one[doc][:5]
        grad_x, bias_grad, gain_grad, shift_grad, pre, right, *token = layer_one_backward(
            about[doc], grad_mid, source, doc, gains, counts_row, links, resid, slope, sigma, pull, squares, up, down,
            kept[doc][4], kept[doc][1], token,
        )
        out_one.append(grad_x)
        kept[doc][4], kept[doc][1] = pre, right
        small_one.append((bias_grad, gain_grad, shift_grad, stats_one[doc]))
        return grad_x, *token

    token = last_sent
    for doc in range(documents - 1):
        (token,) = first_back(doc, after(back[doc], token))
    if documents > 1:
        back[-1] = after(back[-1], token)

    quarter, stack = (rows, width), (1, rows, width)
    still, across = lambda one, q: (0, 0), lambda one, q: (0, q)
    own_rows = [functools.partial(lambda d, one, q: (d, 0), d) for d in docs]

    def left_of(one, q):
        return jnp.where(one == 1, (q + 1) // 2, q // 3), 0, 0

    def right_of(one, q):
        return jnp.where(one == 1, jnp.maximum(q - 1, 0), q), 0, 0

    def pairs_of(name):
        if name == "down":
            return (
                [(kept[d][3], quarter, across) for d in docs],
                [(source, quarter, own_rows[d]) for d in docs],
                [(back[d], quarter, still) for d in docs],
            )
        if name == "up":
            return (
                [(kept[d][2], quarter, still) for d in docs],
                [(kept[d][4], quarter, across) for d in docs],
                None,
            )
        return (
            [(kept[d][0], stack, left_of) for d in docs],
            [(kept[d][1], stack, right_of) for d in docs],
            None,
        )

    order = Ordered()
    custom = lax.axis_size("z") == 4 and lax.axis_size("x") == 2
    names = {"d": "down", "u": "up", "s": "square"}
    totals, given, made, pieces = {"token": jnp.zeros((8, 128), F32)}, {}, {}, {}

    def products(letter):
        name, pairs = names[letter], pairs_of(names[letter])
        *quarters, totals["token"] = weight_quarters(give, *pairs, None, name + "_give", totals["token"])
        given[letter] = [core_swap(v) for v in quarters]
        yield
        *made[letter], totals["token"] = weight_quarters(keep, *pairs, given[letter][0], name + "_keep", totals["token"])
        yield

    def flow(letter):
        sent, kept_own = made[letter]
        kept_other = given[letter][1]
        if custom:
            for value in chips_sum(order, sent, (kept_own, kept_other)):
                pieces[letter] = value
                yield
            return
        near, far = lax.psum(rounded_sum(kept_own, kept_other), ("z", "x")), lax.psum(sent, ("z", "x"))
        pieces[letter] = near, core_swap(near), far
        for _ in range(5):
            yield

    def place(letter, which):
        near, near_other, far = pieces[letter]
        first, blocks = {
            "a": (0, lambda: (near, near_other, far, core_swap(far))),
            "b": (0, lambda: (near, near_other, far)),
            "n": (0, lambda: (near, near_other)),
            "f": (2, lambda: (far,)),
            "o": (3, lambda: (core_swap(far),)),
        }[which]
        shape = (width, hidden) if letter == "u" else (hidden, width)
        blocks = [order.read(block) for block in blocks()]
        totals[letter], copy, totals["token"] = placed(
            places, first, blocks, shape, letter == "u", totals.get(letter), names[letter] + "_placed", totals["token"]
        )
        order.gave(copy)
        if which == "f":
            pieces[letter] = (near, near_other, copy)

    running = {letter: products(letter) for letter in names}
    running.update({letter.upper(): flow(letter) for letter in names})
    for step in STEPS:
        if step == "back":
            _, totals["token"] = first_back(documents - 1, back[-1], totals["token"])
        elif step == "pack":
            small, totals["token"] = packed_row(
                use_one[None], lengths, small_one, small_two, rich_two, totals["token"]
            )
            running["q"] = small_sum(use_one[None], small, totals, ("x", "core", "z"))
            next(running["q"])
        elif step == "rows":
            (boundary_out,) = section_rows(order.read(use_one[None]), out_one, out_two)
            order.gave(boundary_out)
        elif step[0] in "abnfo":
            place(step[1], step[0])
        elif step == "q":
            packed = next(running["q"])
        else:
            next(running[step])
    for packed in running["q"]:
        pass
    crossed = lax.ppermute(packed, "section", [(0, 1), (1, 0)])
    down_total, up_total, square_total = (totals[letter] for letter in names)

    at = hidden // width
    size = 9 + 2 * heads
    shared = packed[at + 4, :size] + crossed[at + 4, :size]
    rms = jnp.sqrt(shared[:8].reshape(2, 4) / (shared[8 + 2 * heads] * width))
    rich_total = shared[8 : 8 + 2 * heads].reshape(2, heads)
    return (
        boundary_out[None],
        square_total.reshape(1, 4, width, width),
        up_total.reshape(1, width, hidden),
        down_total[None],
        packed[:at].reshape(1, hidden),
        packed[at : at + 2][None],
        packed[at + 2 : at + 4][None],
        rich_total,
        rms,
    )


def solution(mesh):
    sections, dp = mesh.devices.shape
    split = Mesh(mesh.devices.reshape(sections, dp // 4, 2, 2), ("section", "z", "x", "core"))
    data = ("z", "x", "core")
    in_specs = (
        P("section", data, None),
        P(data),
        P(data, None),
        P(data),
        P(data),
        P("section", None, None, None),
        P("section", None, None),
        P("section", None, None),
        P("section", None),
        P("section", None, None),
        P("section", None, None),
        P(),
    )
    out_specs = (
        P("section", data, None),
        P("section", None, None, None),
        P("section", None, None),
        P("section", None, None),
        P("section", None),
        P("section", None, None),
        P("section", None, None),
        P(),
        P(),
    )
    return jax.shard_map(local, mesh=split, in_specs=in_specs, out_specs=out_specs, check_vma=False)
```

time: 445 us -> 424 us (0.953)
  Pallas kernels: 245 us -> 190 us
  waiting for transfers between devices: 115 us -> 141 us
  starting transfers between devices: 40.3 us -> 54.6 us
  other arithmetic: 25.2 us -> 12.6 us
  local copies, waits for them, and re-layouts: 9.23 us -> 15.5 us
    pallas_call x2, Pallas kernels: 91.9 us -> 14.3 us  [layer_two(): kernel_call(layer_two_body, (1,), [full, part_of((rows, width), doc, 0),...]
    ppermute x4, waiting for transfers between devices: 0.47 us -> 55.2 us  [passed_along(): return lax.ppermute(block, axis, route)]
    ppermute x4, waiting for transfers between devices: 32.7 us -> 3.97 us  [small_sum(): arrived = lax.ppermute(block, axis, route)]
    pallas_call x13 -> x19, Pallas kernels: 79.3 us -> 104 us  [the longest x18 101 us: kernel_call(): return call if token is None else lambda *operands: call(*operands, token)]
    ppermute x16, starting transfers between devices: 20.3 us -> 44.8 us  [the longest x3 25.3 us: chips_sum(): arrived = lax.ppermute(mine, 'z', partners)]
    pallas_call x2 -> x1, Pallas kernels: 35.8 us -> 18.1 us  [layer_one_backward(): kernel_call(layer_one_backward_body, (1,), [full, part_of((rows, width),...]
    pallas_call x2, Pallas kernels: 38.3 us -> 53.7 us  [layer_one_forward(): kernel_call(layer_one_forward_body, (1,), [part_of((rows, width), doc, 0)...]
    convert_element_type x12 -> x9, other arithmetic: 16.2 us -> 7.65 us  [low(): return vector.astype(BF16)]
  transfers between devices with their start and end apart: 36 -> 36, of which waited for: 13 -> 15; matrix products, arithmetic and copies ran while one was open for 7% -> 3% of each run, Pallas kernels for 49% -> 39%
where the time goes in v4:
time: 424 us; the launch traced here: 416 us
  Pallas kernels  190 us (45%)
  waiting for transfers between devices  141 us (33%)
  starting transfers between devices  54.6 us (13%)
  local copies, waits for them, and re-layouts  15.5 us (4%)
  other arithmetic  12.6 us (3%)
    pallas_call x18, Pallas kernels, kernel_call(): return call if token is None else lambda *operands: call(*operands, token)  101 us
    ppermute x4, waiting for transfers between devices, passed_along(): return lax.ppermute(block, axis, route)  55.2 us
    pallas_call x2, Pallas kernels, layer_one_forward(): kernel_call(layer_one_forward_body, (1,), [part_of((rows, width), doc, 0)...  53.7 us
    ppermute x3, waiting for transfers between devices, chips_sum(): arrived = lax.ppermute(sent, 'x', across_x)  25.9 us
    ppermute x3, starting transfers between devices, chips_sum(): arrived = lax.ppermute(mine, 'z', partners)  25.3 us
    ppermute x3, waiting for transfers between devices, chips_sum(): arrived = lax.ppermute(mine, 'z', neighbours)  21 us
    pallas_call x1, Pallas kernels, layer_one_backward(): kernel_call(layer_one_backward_body, (1,), [full, part_of((rows, width),...  18.1 us
    pallas_call x2, Pallas kernels, layer_two(): kernel_call(layer_two_body, (1,), [full, part_of((rows, width), doc, 0),...  14.3 us
  transfers between devices with their start and end apart: 36, of which 15 were waited for; matrix products, arithmetic and copies ran while one was open for 3% of the time, Pallas kernels for 39%

profile of v4, /device:TPU:0, one launch (start us, length us, event | category | flops | bytes accessed | tf_op | source)
XLA Modules:
  0.0 416.3 jit_solution(13411779262205480933)
XLA Ops:
  0.6 1.3 fusion
  2.0 1.3 pad_add_fusion.1.length_ref
  3.2 18.6 %layer_one_forward.2 = (bf16[512,768]{1,0:T(8,128)(2,1)}, f32[4,768]{1,0:T(4,128)}, bf16[256,512]{1,0:T(8,128)(2,1)}, bf16[3,512,768]{2,1,0:T(8,128)(2,1)}, bf16...) custom-call(s32[2]{0:T(128)} %pad_add_fusion.1.length_ref, ...), custom_call_target="tpu_custom_call" | custom-call | flops 7247757312 | bytes 26738688 | tf_op jit(solution)/shard_map/layer_one_forward/pallas_call | solution.py:259
  21.8 1.3 collective-permute-start
  23.1 1.3 pad_add_fusion.2.length_ref.refs_0_
  24.4 35.1 %layer_one_forward.3 = (bf16[512,768]{1,0:T(8,128)(2,1)}, f32[4,768]{1,0:T(4,128)}, bf16[256,512]{1,0:T(8,128)(2,1)}, bf16[3,512,768]{2,1,0:T(8,128)(2,1)}, bf16...) custom-call(s32[2]{0:T(128)} %pad_add_fusion.2.length_ref.refs_0_, ...), custom_call_target="tpu_custom_call" | custom-call | flops 7247757312 | bytes 26738688 | tf_op jit(solution)/shard_map/layer_one_forward/pallas_call | solution.py:259
  59.6 1.3 collective-permute-start.1
  61.8 3.8 layer_two.2
  65.6 1.3 collective-permute-start.2
  66.9 11.9 %collective-permute-done.1.mid_ref = bf16[512,768]{1,0:T(8,128)(2,1)S(1)} collective-permute-done((bf16[512,768]{1,0:T(8,128)(2,1)}, bf16[512,768]{1,0:T(8,128)(2,1)S(1)}, u32[]{:S(2)}, u32[]{:S(2)}) %collective-permute-start.1) | collective-permute-done | bytes 786464 | tf_op jit(solution)/shard_map/ppermute | solution.py:790
  79.8 10.5 %layer_two.3 = (bf16[512,768]{1,0:T(8,128)(2,1)}, bf16[512,768]{1,0:T(8,128)(2,1)}, f32[4,768]{1,0:T(4,128)}, f32[1,3072]{1,0:T(1,128)}, f32[2,768]{1,0:T(2,128)...) custom-call(s32[2]{0:T(128)} %pad_add_fusion.2.length_ref.refs_0_, ...), custom_call_target="tpu_custom_call", output_to_operand_aliasing={{7}: (11, {}), {9}: (12, {}), {10}: (13, {})} | custom-call | flops 16005464064 | bytes 28311552 | tf_op jit(solution)/shard_map/layer_two/pallas_call | solution.py:564
  90.2 1.3 collective-permute-start.3
  92.1 15.7 %collective-permute-done.2.grad_ref.refs_5_ = bf16[512,768]{1,0:T(8,128)(2,1)S(1)} collective-permute-done((bf16[512,768]{1,0:T(8,128)(2,1)}, bf16[512,768]{1,0:T(8,128)(2,1)S(1)}, u32[]{:S(2)}, u32[]{:S(2)}) %collective-permute-start.2) | collective-permute-done | bytes 786464 | tf_op jit(solution)/shard_map/ppermute | solution.py:790
  108.7 18.1 %layer_one_backward.2 = (bf16[512,768]{1,0:T(8,128)(2,1)}, f32[1,3072]{1,0:T(1,128)}, f32[2,768]{1,0:T(2,128)}, f32[2,768]{1,0:T(2,128)}, bf16[512,3072]{1,0:T(8,128)(2,1)}, /*index=5*/bf16[4,512,768]{2,1,0:T(8,128)(2,1)}) custom-call(s32[2]{0:T(128)} %pad_add_fusion.1.length_ref, ...), custom_call_target="tpu_custom_call", output_to_operand_aliasing={{4}: (13, {}), {5}: (14, {})} | custom-call | flops 7247757312 | bytes 27525120 | tf_op jit(solution)/shard_map/layer_one_backward/pallas_call | solution.py:341
  126.9 27.5 %collective-permute-done.3.refs_6_.refs_1_ = bf16[512,768]{1,0:T(8,128)(2,1)S(1)} collective-permute-done((bf16[512,768]{1,0:T(8,128)(2,1)}, bf16[512,768]{1,0:T(8,128)(2,1)S(1)}, u32[]{:S(2)}, u32[]{:S(2)}) %collective-permute-start.3) | collective-permute-done | bytes 786464 | tf_op jit(solution)/shard_map/ppermute | solution.py:790
  155.3 7.5 %down_give.1 = (bf16[768,768]{1,0:T(8,128)(2,1)}, bf16[768,768]{1,0:T(8,128)(2,1)}, f32[8,128]{1,0:T(8,128)}) custom-call(s32[3]{0:T(128)} %pad_add_fusion.3.refs_0_, bf16[512,3072]{1,0:T(8,128)(2,1)} %get-tuple-element.164.refs_1_, bf16[512,3072]{1,0:T(8,128)(2,1)} %get-tuple-element.165.refs_2_, bf16[1024,768]{1,0:T(8,128)(2,1)} %bitcast.34, ...), custom_call_target="tpu_custom_call" | custom-call | flops 2415919104 | bytes 11010048 | tf_op jit(solution)/shard_map/down_give/pallas_call | solution.py:99
  164.0 1.9 collective-permute-done.4.refs_7_
  166.9 8.1 %down_keep.1 = (bf16[768,768]{1,0:T(8,128)(2,1)}, bf16[768,768]{1,0:T(8,128)(2,1)}, f32[8,128]{1,0:T(8,128)}) custom-call(s32[3]{0:T(128)} %pad_add_fusion.refs_0_, bf16[512,3072]{1,0:T(8,128)(2,1)} %get-tuple-element.164.refs_1_, bf16[512,3072]{1,0:T(8,128)(2,1)} %get-tuple-element.165.refs_2_, bf16[1024,768]{1,0:T(8,128)(2,1)} %bitcast.36, ...), custom_call_target="tpu_custom_call" | custom-call | flops 2415919104 | bytes 11010048 | tf_op jit(solution)/shard_map/down_keep/pallas_call | solution.py:99
  175.0 1.7 collective-permute-start.11
  176.7 18.0 %layer_one_backward.3 = (bf16[512,768]{1,0:T(8,128)(2,1)}, f32[1,3072]{1,0:T(1,128)}, f32[2,768]{1,0:T(2,128)}, f32[2,768]{1,0:T(2,128)}, bf16[512,3072]{1,0:T(8...) custom-call(s32[2]{0:T(128)} %pad_add_fusion.2.length_ref.refs_0_, ...), custom_call_target="tpu_custom_call", output_to_operand_aliasing={{4}: (13, {}), {5}: (14, {})} | custom-call | flops 7247757312 | bytes 27525120 | tf_op jit(solution)/shard_map/layer_one_backward/pallas_call | solution.py:99
  194.7 1.8 packed_row.1
  196.5 7.2 %up_give.1 = (bf16[768,768]{1,0:T(8,128)(2,1)}, bf16[768,768]{1,0:T(8,128)(2,1)}, f32[8,128]{1,0:T(8,128)}) custom-call(s32[3]{0:T(128)} %pad_add_fusion.3.refs_0_, bf16[512,768]{1,0:T(8,128)(2,1)} %get-tuple-element.170.refs_1_, bf16[512,768]{1,0:T(8,128)(2,1)} %get-tuple-element.171.refs_2_, bf16[512,3072]{1,0:T(8,128)(2,1)} %get-tuple-element.172.refs_3_, ...), custom_call_target="tpu_custom_call" | custom-call | flops 2415919104 | bytes 11010048 | tf_op jit(solution)/shard_map/up_give/pallas_call | solution.py:99
  204.2 4.0 collective-permute-done.6.refs_2_
  208.2 1.4 small_sum.4
  209.7 1.3 add_convert_fusion.11
  210.9 1.6 collective-permute-start.12
  212.5 7.5 %up_keep.1 = (bf16[768,768]{1,0:T(8,128)(2,1)}, bf16[768,768]{1,0:T(8,128)(2,1)}, f32[8,128]{1,0:T(8,128)}) custom-call(s32[3]{0:T(128)} %pad_add_fusion.refs_0_, bf16[512,768]{1,0:T(8,128)(2,1)} %get-tuple-element.170.refs_1_, bf16[512,768]{1,0:T(8,128)(2,1)} %get-tuple-element.171.refs_2_, bf16[512,3072]{1,0:T(8,128)(2,1)} %get-tuple-element.172.refs_3_, ...), custom_call_target="tpu_custom_call" | custom-call | flops 2415919104 | bytes 11010048 | tf_op jit(solution)/shard_map/up_keep/pallas_call | solution.py:99
  220.5 7.2 %square_give.1 = (bf16[768,768]{1,0:T(8,128)(2,1)}, bf16[768,768]{1,0:T(8,128)(2,1)}, f32[8,128]{1,0:T(8,128)}) custom-call(s32[3]{0:T(128)} %pad_add_fusion.3.refs_0_, bf16[3,512,768]{2,1,0:T(8,128)(2,1)} %get-tuple-element.137.refs_1_, bf16[3,512,768]{2,1,0:T(8,128)(2,1)} %get-tuple-element.143.refs_2_, bf16[4,512,768]{2,1,0:T(8,128)(2,1)} %get-tuple-element.154.refs_3_, ...), custom_call_target="tpu_custom_call" | custom-call | flops 2415919104 | bytes 11010048 | tf_op jit(solution)/shard_map/square_give/pallas_call | solution.py:99
  227.8 2.5 collective-permute-start.13
  230.6 16.9 %collective-permute-done.15 = bf16[768,768]{1,0:T(8,128)(2,1)S(1)} collective-permute-done((bf16[768,768]{1,0:T(8,128)(2,1)}, bf16[768,768]{1,0:T(8,128)(2,1)S(1)}, u32[]{:S(2)}, u32[]{:S(2)}) %collective-permute-start.15) | collective-permute-done | bytes 1179680 | tf_op jit(solution)/shard_map/ppermute | solution.py:827
  247.5 1.7 add_convert_fusion.6
  250.8 7.7 %square_keep.1 = (bf16[768,768]{1,0:T(8,128)(2,1)}, bf16[768,768]{1,0:T(8,128)(2,1)}, f32[8,128]{1,0:T(8,128)}) custom-call(s32[3]{0:T(128)} %pad_add_fusion.refs_0_, bf16[3,512,768]{2,1,0:T(8,128)(2,1)} %get-tuple-element.137.refs_1_, bf16[3,512,768]{2,1,0:T(8,128)(2,1)} %get-tuple-element.143.refs_2_, bf16[4,512,768]{2,1,0:T(8,128)(2,1)} %get-tuple-element.154.refs_3_, ...), custom_call_target="tpu_custom_call" | custom-call | flops 2415919104 | bytes 11010048 | tf_op jit(solution)/shard_map/square_keep/pallas_call | solution.py:99
  258.8 1.2 add_convert_fusion.7
  260.0 1.8 collective-permute-start.16
  261.8 3.2 collective-permute-done.17
  265.1 10.6 %collective-permute-done.16 = bf16[384,768]{1,0:T(8,128)(2,1)S(1)} collective-permute-done((bf16[384,768]{1,0:T(8,128)(2,1)S(1)}, bf16[384,768]{1,0:T(8,128)(2,1)S(1)}, u32[]{:S(2)}, u32[]{:S(2)}) %collective-permute-start.16) | collective-permute-done | bytes 589856 | tf_op jit(solution)/shard_map/ppermute | solution.py:842
  275.9 9.0 %collective-permute-done.9 = bf16[768,768]{1,0:T(8,128)(2,1)S(1)} collective-permute-done((bf16[768,768]{1,0:T(8,128)(2,1)}, bf16[768,768]{1,0:T(8,128)(2,1)S(1)}, u32[]{:S(2)}, u32[]{:S(2)}) %collective-permute-start.9) | collective-permute-done | bytes 1179680 | tf_op jit(solution)/shard_map/ppermute | solution.py:827
  284.9 1.7 add_convert_fusion.3
  286.6 1.5 collective-permute-start.18
  288.2 2.5 collective-permute-start.20
  291.5 3.0 section_rows.1
  294.6 7.4 %collective-permute-done.18 = bf16[384,768]{1,0:T(8,128)(2,1)S(1)} collective-permute-done((bf16[384,768]{1,0:T(8,128)(2,1)S(1)}, bf16[384,768]{1,0:T(8,128)(2,1)S(1)}, u32[]{:S(2)}, u32[]{:S(2)}) %collective-permute-start.18) | collective-permute-done | bytes 589856 | tf_op jit(solution)/shard_map/ppermute | solution.py:835
  302.1 20.3 %collective-permute-start.19 = (bf16[384,768]{1,0:T(8,128)(2,1)S(1)}, bf16[384,768]{1,0:T(8,128)(2,1)S(1)}, u32[]{:S(2)}, u32[]{:S(2)}) collective-permute-start(bf16[384,768]{1,0:T(8,128)(2,1)S(1)} %add_convert_fusion.2), channel_id=1, source_target_pairs={{4,8},{8,4},{0,12},{12,0},{5,9},{9,5},{1,13},{13,1},{6,10},{10,6},... | collective-permute-start | bytes 1769480 | tf_op jit(solution)/shard_map/ppermute | solution.py:839
  322.3 1.2 add_convert_fusion.1
  323.6 1.8 collective-permute-start.22
  325.3 7.7 %collective-permute-done.19 = bf16[384,768]{1,0:T(8,128)(2,1)S(1)} collective-permute-done((bf16[384,768]{1,0:T(8,128)(2,1)S(1)}, bf16[384,768]{1,0:T(8,128)(2,1)S(1)}, u32[]{:S(2)}, u32[]{:S(2)}) %collective-permute-start.19) | collective-permute-done | bytes 589856 | tf_op jit(solution)/shard_map/ppermute | solution.py:839
  333.2 7.0 %collective-permute-start.21 = (bf16[384,768]{1,0:T(8,128)(2,1)S(1)}, bf16[384,768]{1,0:T(8,128)(2,1)S(1)}, u32[]{:S(2)}, u32[]{:S(2)}) collective-permute-start(bf16[384,768]{1,0:T(8,128)(2,1)S(1)} %add_convert_fusion), channel_id=1, source_target_pairs={{0,4},{4,0},{8,12},{12,8},{1,5},{5,1},{9,13},{13,9},{2,6},{6,2},{1... | collective-permute-start | bytes 1769480 | tf_op jit(solution)/shard_map/ppermute | solution.py:842
  341.5 10.4 %collective-permute-done.21 = bf16[384,768]{1,0:T(8,128)(2,1)S(1)} collective-permute-done((bf16[384,768]{1,0:T(8,128)(2,1)S(1)}, bf16[384,768]{1,0:T(8,128)(2,1)S(1)}, u32[]{:S(2)}, u32[]{:S(2)}) %collective-permute-start.21) | collective-permute-done | bytes 589856 | tf_op jit(solution)/shard_map/ppermute | solution.py:842
  353.8 1.2 collective-permute-start.23
  355.0 1.4 small_sum.5
  356.4 1.2 collective-permute-start.30
  358.3 7.4 %down_placed.1 = (f32[3072,768]{1,0:T(8,128)}, bf16[768,768]{1,0:T(8,128)(2,1)}, f32[8,128]{1,0:T(8,128)}) custom-call(s32[4]{0:T(128)} %pad_add_fusion.4.refs_0_, bf16[768,768]{1,0:T(8,128)(2,1)} %copy-done.4, bf16[768,768]{1,0:T(8,128)(2,1)} %copy-done.11, bf16[768,768]{1,0:T(8,128)(2,1)} %collective-permute-done.25.refs_3_, ...), custom_call_target="tpu_custom_call" | custom-call | bytes 14155776 | tf_op jit(solution)/shard_map/down_placed/pallas_call | solution.py:99
  366.3 1.4 small_sum.6
  367.7 1.0 collective-permute-start.32
  368.8 1.1 collective-permute-done.29.refs_3_
  369.9 6.2 %up_placed.2 = (f32[768,3072]{1,0:T(8,128)}, bf16[768,768]{1,0:T(8,128)(2,1)}, f32[8,128]{1,0:T(8,128)}) custom-call(s32[4]{0:T(128)} %pad_add_fusion.4.refs_0_, bf16[768,768]{1,0:T(8,128)(2,1)} %copy-done.2, bf16[768,768]{1,0:T(8,128)(2,1)} %collective-permute-done.28.refs_2_, bf16[768,768]{1,0:T(8,128)(2,1)} %collective-permute-done.29.refs_3_, ...), custom_call_target="tpu_custom_call" | custom-call | bytes 10616832 | tf_op jit(solution)/shard_map/up_placed/pallas_call | solution.py:99
  376.8 1.4 small_sum.7
  378.2 5.1 %square_placed.3 = (f32[3072,768]{1,0:T(8,128)}, bf16[768,768]{1,0:T(8,128)(2,1)}, f32[8,128]{1,0:T(8,128)}) custom-call(s32[4]{0:T(128)} %pad_add_fusion.4.refs_0_, bf16[768,768]{1,0:T(8,128)(2,1)} %copy-done.3, bf16[768,768]{1,0:T(8,128)(2,1)} %collective-permute-done.31.refs_2_, f32[8,128]{1,0:T(8,128)} %get-tuple-element.244.refs_3_), custom_call_target="tpu_custom_call" | custom-call | bytes 7077888 | tf_op jit(solution)/shard_map/square_placed/pallas_call | solution.py:99
  383.3 10.9 %collective-permute-done.23.refs_1_ = bf16[768,768]{1,0:T(8,128)(2,1)S(1)} collective-permute-done((bf16[768,768]{1,0:T(8,128)(2,1)S(1)}, bf16[768,768]{1,0:T(8,128)(2,1)S(1)}, u32[]{:S(2)}, u32[]{:S(2)}) %collective-permute-start.23) | collective-permute-done | bytes 1179680 | tf_op jit(solution)/shard_map/ppermute | solution.py:847
  394.2 1.0 copy-done.5
  395.2 4.1 square_placed.4
  400.5 2.9 collective-permute-done.35
  407.1 3.9 up_placed.3
  412.1 3.9 square_placed.5
  (105 shorter events, 21.4 us)
Async XLA Ops:
  21.8 39.1 %collective-permute-start = (bf16[512,768]{1,0:T(8,128)(2,1)}, bf16[512,768]{1,0:T(8,128)(2,1)S(1)}, u32[]{:S(2)}, u32[]{:S(2)}) collective-permute-start(bf16[512,768]{1,0:T(8,128)(2,1)} %get-tuple-element.133), channel_id=1, source_target_pairs={{0,16},{1,17},{2,18},{3,19},{4,20},{5,21},{6,22},{7,23},{8,24},{9,... | collective-permute-start | bytes 2359304 | tf_op jit(solution)/shard_map/ppermute | solution.py:790
  59.6 19.3 %collective-permute-start.1 = (bf16[512,768]{1,0:T(8,128)(2,1)}, bf16[512,768]{1,0:T(8,128)(2,1)S(1)}, u32[]{:S(2)}, u32[]{:S(2)}) collective-permute-start(bf16[512,768]{1,0:T(8,128)(2,1)} %get-tuple-element.139), channel_id=1, source_target_pairs={{0,16},{1,17},{2,18},{3,19},{4,20},{5,21},{6,22},{7,23},{8,24},{9,... | collective-permute-start | bytes 2359304 | tf_op jit(solution)/shard_map/ppermute | solution.py:790
  60.9 0.9 copy-start.20
  65.6 42.2 %collective-permute-start.2 = (bf16[512,768]{1,0:T(8,128)(2,1)}, bf16[512,768]{1,0:T(8,128)(2,1)S(1)}, u32[]{:S(2)}, u32[]{:S(2)}) collective-permute-start(bf16[512,768]{1,0:T(8,128)(2,1)} %get-tuple-element.144), channel_id=1, source_target_pairs={{16,0},{17,1},{18,2},{19,3},{20,4},{21,5},{22,6},{23,7},{24,8},{25... | collective-permute-start | bytes 2359304 | tf_op jit(solution)/shard_map/ppermute | solution.py:790
  78.9 0.9 copy-start.19
  90.2 64.2 %collective-permute-start.3 = (bf16[512,768]{1,0:T(8,128)(2,1)}, bf16[512,768]{1,0:T(8,128)(2,1)S(1)}, u32[]{:S(2)}, u32[]{:S(2)}) collective-permute-start(bf16[512,768]{1,0:T(8,128)(2,1)} %get-tuple-element.145), channel_id=1, source_target_pairs={{16,0},{17,1},{18,2},{19,3},{20,4},{21,5},{22,6},{23,7},{24,8},{25... | collective-permute-start | bytes 2359304 | tf_op jit(solution)/shard_map/ppermute | solution.py:790
  107.8 0.9 copy-start
  154.4 0.9 copy-start.1
  162.9 3.1 collective-permute-start.4
  163.5 46.2 %collective-permute-start.10 = (bf16[768,768]{1,0:T(8,128)(2,1)}, bf16[768,768]{1,0:T(8,128)(2,1)S(1)}, u32[]{:S(2)}, u32[]{:S(2)}) collective-permute-start(bf16[768,768]{1,0:T(8,128)(2,1)} %get-tuple-element.205), channel_id=1, source_target_pairs={{0,1},{1,0},{2,3},{3,2},{4,5},{5,4},{6,7},{7,6},{8,9},{9,8},{10,11... | collective-permute-start | bytes 3538952 | tf_op jit(solution)/shard_map/ppermute | solution.py:798
  165.9 1.0 copy-start.13
  175.0 34.7 %collective-permute-start.11 = (bf16[768,768]{1,0:T(8,128)(2,1)}, bf16[768,768]{1,0:T(8,128)(2,1)S(1)}, u32[]{:S(2)}, u32[]{:S(2)}) collective-permute-start(bf16[768,768]{1,0:T(8,128)(2,1)} %get-tuple-element.206), channel_id=1, source_target_pairs={{0,2},{2,0},{1,3},{3,1},{4,6},{6,4},{5,7},{7,5},{8,10},{10,8},{9,1... | collective-permute-start | bytes 3538952 | tf_op jit(solution)/shard_map/ppermute | solution.py:827
  196.5 13.1 %copy-start.8 = (bf16[768,768]{1,0:T(8,128)(2,1)S(1)}, bf16[768,768]{1,0:T(8,128)(2,1)}, u32[]{:S(2)}) copy-start(bf16[768,768]{1,0:T(8,128)(2,1)} %get-tuple-element.204) | copy-start | bytes 3538948
  203.7 8.8 %collective-permute-start.5 = (bf16[768,768]{1,0:T(8,128)(2,1)}, bf16[768,768]{1,0:T(8,128)(2,1)}, u32[]{:S(2)}, u32[]{:S(2)}) collective-permute-start(bf16[768,768]{1,0:T(8,128)(2,1)} %get-tuple-element.194), channel_id=1, source_target_pairs={{0,1},{1,0},{2,3},{3,2},{4,5},{5,4},{6,7},{7,6},{8,9},{9,8},{10,11... | collective-permute-start | bytes 3538952 | tf_op jit(solution)/shard_map/ppermute | solution.py:798
  203.7 4.5 %collective-permute-start.6 = (f32[16,768]{1,0:T(8,128)}, f32[16,768]{1,0:T(8,128)}, u32[]{:S(2)}, u32[]{:S(2)}) collective-permute-start(f32[16,768]{1,0:T(8,128)} %get-tuple-element.195.refs_1_), channel_id=1, source_target_pairs={{0,2},{2,0},{1,3},{3,1},{4,6},{6,4},{5,7},{7,5},{8,10},{10,8},{9,1... | collective-permute-start | bytes 147464 | tf_op jit(solution)/shard_map/ppermute | solution.py:855
  204.0 43.5 %collective-permute-start.14 = (bf16[768,768]{1,0:T(8,128)(2,1)}, bf16[768,768]{1,0:T(8,128)(2,1)}, u32[]{:S(2)}, u32[]{:S(2)}) collective-permute-start(bf16[768,768]{1,0:T(8,128)(2,1)} %get-tuple-element.209), channel_id=1, source_target_pairs={{0,1},{1,0},{2,3},{3,2},{4,5},{5,4},{6,7},{7,6},{8,9},{9,8},{10,11... | collective-permute-start | bytes 3538952 | tf_op jit(solution)/shard_map/ppermute | solution.py:798
  210.9 16.8 %collective-permute-start.12 = (bf16[384,768]{1,0:T(8,128)(2,1)}, bf16[384,768]{1,0:T(8,128)(2,1)S(1)}, u32[]{:S(2)}, u32[]{:S(2)}) collective-permute-start(bf16[384,768]{1,0:T(8,128)(2,1)} %get-tuple-element.262), channel_id=1, source_target_pairs={{0,4},{4,0},{8,12},{12,8},{1,5},{5,1},{9,13},{13,9},{2,6},{6,2},{1... | collective-permute-start | bytes 1769480 | tf_op jit(solution)/shard_map/ppermute | solution.py:835
  220.0 27.5 %collective-permute-start.15 = (bf16[768,768]{1,0:T(8,128)(2,1)}, bf16[768,768]{1,0:T(8,128)(2,1)S(1)}, u32[]{:S(2)}, u32[]{:S(2)}) collective-permute-start(bf16[768,768]{1,0:T(8,128)(2,1)} %get-tuple-element.210), channel_id=1, source_target_pairs={{0,2},{2,0},{1,3},{3,1},{4,6},{6,4},{5,7},{7,5},{8,10},{10,8},{9,1... | collective-permute-start | bytes 3538952 | tf_op jit(solution)/shard_map/ppermute | solution.py:827
  227.7 19.9 %copy-start.10 = (bf16[768,768]{1,0:T(8,128)(2,1)S(1)}, bf16[768,768]{1,0:T(8,128)(2,1)}, u32[]{:S(2)}) copy-start(bf16[768,768]{1,0:T(8,128)(2,1)} %get-tuple-element.208) | copy-start | bytes 3538948
  227.7 22.1 %collective-permute-start.7 = (bf16[768,768]{1,0:T(8,128)(2,1)}, bf16[768,768]{1,0:T(8,128)(2,1)S(1)}, u32[]{:S(2)}, u32[]{:S(2)}) collective-permute-start(bf16[768,768]{1,0:T(8,128)(2,1)} %get-tuple-element.199), channel_id=1, source_target_pairs={{0,1},{1,0},{2,3},{3,2},{4,5},{5,4},{6,7},{7,6},{8,9},{9,8},{10,11... | collective-permute-start | bytes 3538952 | tf_op jit(solution)/shard_map/ppermute | solution.py:798
  227.8 30.6 %collective-permute-start.13 = (bf16[384,768]{1,0:T(8,128)(2,1)S(1)}, bf16[384,768]{1,0:T(8,128)(2,1)}, u32[]{:S(2)}, u32[]{:S(2)}) collective-permute-start(bf16[384,768]{1,0:T(8,128)(2,1)S(1)} %add_convert_fusion.9), channel_id=1, source_target_pairs={{4,8},{8,4},{0,12},{12,0},{5,9},{9,5},{1,13},{13,1},{6,10},{10,6},... | collective-permute-start | bytes 1769480 | tf_op jit(solution)/shard_map/ppermute | solution.py:839
  230.4 54.5 %collective-permute-start.8 = (bf16[768,768]{1,0:T(8,128)(2,1)}, bf16[768,768]{1,0:T(8,128)(2,1)}, u32[]{:S(2)}, u32[]{:S(2)}) collective-permute-start(bf16[768,768]{1,0:T(8,128)(2,1)} %get-tuple-element.202), channel_id=1, source_target_pairs={{0,1},{1,0},{2,3},{3,2},{4,5},{5,4},{6,7},{7,6},{8,9},{9,8},{10,11... | collective-permute-start | bytes 3538952 | tf_op jit(solution)/shard_map/ppermute | solution.py:798
  249.2 15.8 %collective-permute-start.17 = (bf16[384,768]{1,0:T(8,128)(2,1)S(1)}, bf16[384,768]{1,0:T(8,128)(2,1)S(1)}, u32[]{:S(2)}, u32[]{:S(2)}) collective-permute-start(bf16[384,768]{1,0:T(8,128)(2,1)S(1)} %get-tuple-element.259), channel_id=1, source_target_pairs={{0,4},{4,0},{8,12},{12,8},{1,5},{5,1},{9,13},{13,9},{2,6},{6,2},{1... | collective-permute-start | bytes 1769480 | tf_op jit(solution)/shard_map/ppermute | solution.py:835
  249.8 1.0 copy-start.12
  258.4 26.4 %collective-permute-start.9 = (bf16[768,768]{1,0:T(8,128)(2,1)}, bf16[768,768]{1,0:T(8,128)(2,1)S(1)}, u32[]{:S(2)}, u32[]{:S(2)}) collective-permute-start(bf16[768,768]{1,0:T(8,128)(2,1)} %get-tuple-element.203), channel_id=1, source_target_pairs={{0,2},{2,0},{1,3},{3,1},{4,6},{6,4},{5,7},{7,5},{8,10},{10,8},{9,1... | collective-permute-start | bytes 3538952 | tf_op jit(solution)/shard_map/ppermute | solution.py:827
  260.0 15.7 %collective-permute-start.16 = (bf16[384,768]{1,0:T(8,128)(2,1)S(1)}, bf16[384,768]{1,0:T(8,128)(2,1)S(1)}, u32[]{:S(2)}, u32[]{:S(2)}) collective-permute-start(bf16[384,768]{1,0:T(8,128)(2,1)S(1)} %add_convert_fusion.7), channel_id=1, source_target_pairs={{0,4},{4,0},{8,12},{12,8},{1,5},{5,1},{9,13},{13,9},{2,6},{6,2},{1... | collective-permute-start | bytes 1769480 | tf_op jit(solution)/shard_map/ppermute | solution.py:842
  275.8 9.1 %copy-start.9 = (bf16[768,768]{1,0:T(8,128)(2,1)S(1)}, bf16[768,768]{1,0:T(8,128)(2,1)}, u32[]{:S(2)}) copy-start(bf16[768,768]{1,0:T(8,128)(2,1)} %get-tuple-element.201) | copy-start | bytes 3538948
  275.9 49.4 %copy-start.4 = (bf16[768,768]{1,0:T(8,128)(2,1)}, bf16[768,768]{1,0:T(8,128)(2,1)S(1)}, u32[]{:S(2)}) copy-start(bf16[768,768]{1,0:T(8,128)(2,1)S(1)} %pad_maximum_fusion.refs_1_) | copy-start | bytes 3538948
  286.6 15.3 %collective-permute-start.18 = (bf16[384,768]{1,0:T(8,128)(2,1)S(1)}, bf16[384,768]{1,0:T(8,128)(2,1)S(1)}, u32[]{:S(2)}, u32[]{:S(2)}) collective-permute-start(bf16[384,768]{1,0:T(8,128)(2,1)S(1)} %get-tuple-element.257), channel_id=1, source_target_pairs={{0,4},{4,0},{8,12},{12,8},{1,5},{5,1},{9,13},{13,9},{2,6},{6,2},{1... | collective-permute-start | bytes 1769480 | tf_op jit(solution)/shard_map/ppermute | solution.py:835
  288.2 34.2 %collective-permute-start.20 = (bf16[384,768]{1,0:T(8,128)(2,1)S(1)}, bf16[384,768]{1,0:T(8,128)(2,1)}, u32[]{:S(2)}, u32[]{:S(2)}) collective-permute-start(bf16[384,768]{1,0:T(8,128)(2,1)S(1)} %add_convert_fusion.5), channel_id=1, source_target_pairs={{4,8},{8,4},{0,12},{12,0},{5,9},{9,5},{1,13},{13,1},{6,10},{10,6},... | collective-permute-start | bytes 1769480 | tf_op jit(solution)/shard_map/ppermute | solution.py:839
  290.6 49.6 %collective-permute-start.25 = (bf16[768,768]{1,0:T(8,128)(2,1)S(1)}, bf16[768,768]{1,0:T(8,128)(2,1)}, u32[]{:S(2)}, u32[]{:S(2)}) collective-permute-start(bf16[768,768]{1,0:T(8,128)(2,1)S(1)} %pad_maximum_fusion.refs_1_), channel_id=1, source_target_pairs={{0,2},{2,0},{1,3},{3,1},{4,6},{6,4},{5,7},{7,5},{8,10},{10,8},{9,1... | collective-permute-start | bytes 3538952 | tf_op jit(solution)/shard_map/ppermute | solution.py:847
  302.1 31.0 %collective-permute-start.19 = (bf16[384,768]{1,0:T(8,128)(2,1)S(1)}, bf16[384,768]{1,0:T(8,128)(2,1)S(1)}, u32[]{:S(2)}, u32[]{:S(2)}) collective-permute-start(bf16[384,768]{1,0:T(8,128)(2,1)S(1)} %add_convert_fusion.2), channel_id=1, source_target_pairs={{4,8},{8,4},{0,12},{12,0},{5,9},{9,5},{1,13},{13,1},{6,10},{10,6},... | collective-permute-start | bytes 1769480 | tf_op jit(solution)/shard_map/ppermute | solution.py:839
  323.5 16.6 %copy-start.14 = (f32[16,768]{1,0:T(8,128)S(1)}, f32[16,768]{1,0:T(8,128)}, u32[]{:S(2)}) copy-start(f32[16,768]{1,0:T(8,128)} %get-tuple-element.229.refs_1_) | copy-start | bytes 147460
  323.6 17.1 %collective-permute-start.22 = (bf16[384,768]{1,0:T(8,128)(2,1)S(1)}, bf16[384,768]{1,0:T(8,128)(2,1)S(1)}, u32[]{:S(2)}, u32[]{:S(2)}) collective-permute-start(bf16[384,768]{1,0:T(8,128)(2,1)S(1)} %add_convert_fusion.1), channel_id=1, source_target_pairs={{0,4},{4,0},{8,12},{12,8},{1,5},{5,1},{9,13},{13,9},{2,6},{6,2},{1... | collective-permute-start | bytes 1769480 | tf_op jit(solution)/shard_map/ppermute | solution.py:842
  325.3 27.3 %collective-permute-start.24 = (bf16[768,768]{1,0:T(8,128)(2,1)S(1)}, bf16[768,768]{1,0:T(8,128)(2,1)S(1)}, u32[]{:S(2)}, u32[]{:S(2)}) collective-permute-start(bf16[768,768]{1,0:T(8,128)(2,1)S(1)} %pad_maximum_fusion.refs_1_), channel_id=1, source_target_pairs={{0,1},{1,0},{2,3},{3,2},{4,5},{5,4},{6,7},{7,6},{8,9},{9,8},{10,11... | collective-permute-start | bytes 3538952 | tf_op jit(solution)/shard_map/ppermute | solution.py:798
  333.2 18.7 %collective-permute-start.21 = (bf16[384,768]{1,0:T(8,128)(2,1)S(1)}, bf16[384,768]{1,0:T(8,128)(2,1)S(1)}, u32[]{:S(2)}, u32[]{:S(2)}) collective-permute-start(bf16[384,768]{1,0:T(8,128)(2,1)S(1)} %add_convert_fusion), channel_id=1, source_target_pairs={{0,4},{4,0},{8,12},{12,8},{1,5},{5,1},{9,13},{13,9},{2,6},{6,2},{1... | collective-permute-start | bytes 1769480 | tf_op jit(solution)/shard_map/ppermute | solution.py:842
  340.2 11.9 %collective-permute-start.27 = (f32[16,768]{1,0:T(8,128)S(1)}, f32[16,768]{1,0:T(8,128)S(1)}, u32[]{:S(2)}, u32[]{:S(2)}) collective-permute-start(f32[16,768]{1,0:T(8,128)S(1)} %copy-done.14), channel_id=1, source_target_pairs={{0,1},{1,0},{2,3},{3,2},{4,5},{5,4},{6,7},{7,6},{8,9},{9,8},{10,11... | collective-permute-start | bytes 147464 | tf_op jit(solution)/shard_map/ppermute | solution.py:855
  340.2 16.2 %collective-permute-start.26 = (bf16[768,768]{1,0:T(8,128)(2,1)}, bf16[768,768]{1,0:T(8,128)(2,1)}, u32[]{:S(2)}, u32[]{:S(2)}) collective-permute-start(bf16[768,768]{1,0:T(8,128)(2,1)} %collective-permute-done.25.refs_3_), channel_id=1, source_target_pairs={{0,1},{1,0},{2,3},{3,2},{4,5},{5,4},{6,7},{7,6},{8,9},{9,8},{10,11... | collective-permute-start | bytes 3538952 | tf_op jit(solution)/shard_map/ppermute | solution.py:798
  340.9 11.1 %copy-start.2 = (bf16[768,768]{1,0:T(8,128)(2,1)}, bf16[768,768]{1,0:T(8,128)(2,1)S(1)}, u32[]{:S(2)}) copy-start(bf16[768,768]{1,0:T(8,128)(2,1)S(1)} %pad_maximum_fusion.1.refs_1_) | copy-start | bytes 3538948
  340.9 29.0 %collective-permute-start.29 = (bf16[768,768]{1,0:T(8,128)(2,1)S(1)}, bf16[768,768]{1,0:T(8,128)(2,1)}, u32[]{:S(2)}, u32[]{:S(2)}) collective-permute-start(bf16[768,768]{1,0:T(8,128)(2,1)S(1)} %pad_maximum_fusion.1.refs_1_), channel_id=1, source_target_pairs={{0,2},{2,0},{1,3},{3,1},{4,6},{6,4},{5,7},{7,5},{8,10},{10,8},{9,1... | collective-permute-start | bytes 3538952 | tf_op jit(solution)/shard_map/ppermute | solution.py:847
  351.9 18.0 %collective-permute-start.28 = (bf16[768,768]{1,0:T(8,128)(2,1)S(1)}, bf16[768,768]{1,0:T(8,128)(2,1)}, u32[]{:S(2)}, u32[]{:S(2)}) collective-permute-start(bf16[768,768]{1,0:T(8,128)(2,1)S(1)} %pad_maximum_fusion.1.refs_1_), channel_id=1, source_target_pairs={{0,1},{1,0},{2,3},{3,2},{4,5},{5,4},{6,7},{7,6},{8,9},{9,8},{10,11... | collective-permute-start | bytes 3538952 | tf_op jit(solution)/shard_map/ppermute | solution.py:798
  352.1 13.6 %copy-start.3 = (bf16[768,768]{1,0:T(8,128)(2,1)}, bf16[768,768]{1,0:T(8,128)(2,1)S(1)}, u32[]{:S(2)}) copy-start(bf16[768,768]{1,0:T(8,128)(2,1)S(1)} %pad_maximum_fusion.2.refs_1_) | copy-start | bytes 3538948
  352.1 0.7 copy-start.15
  352.1 26.1 %collective-permute-start.31 = (bf16[768,768]{1,0:T(8,128)(2,1)S(1)}, bf16[768,768]{1,0:T(8,128)(2,1)}, u32[]{:S(2)}, u32[]{:S(2)}) collective-permute-start(bf16[768,768]{1,0:T(8,128)(2,1)S(1)} %pad_maximum_fusion.2.refs_1_), channel_id=1, source_target_pairs={{0,1},{1,0},{2,3},{3,2},{4,5},{5,4},{6,7},{7,6},{8,9},{9,8},{10,11... | collective-permute-start | bytes 3538952 | tf_op jit(solution)/shard_map/ppermute | solution.py:798
  352.7 1.0 copy-start.11
  353.8 40.4 %collective-permute-start.23 = (bf16[768,768]{1,0:T(8,128)(2,1)S(1)}, bf16[768,768]{1,0:T(8,128)(2,1)S(1)}, u32[]{:S(2)}, u32[]{:S(2)}) collective-permute-start(bf16[768,768]{1,0:T(8,128)(2,1)S(1)} %pad_maximum_fusion.2.refs_1_), channel_id=1, source_target_pairs={{0,2},{2,0},{1,3},{3,1},{4,6},{6,4},{5,7},{7,5},{8,10},{10,8},{9,1... | collective-permute-start | bytes 3538952 | tf_op jit(solution)/shard_map/ppermute | solution.py:847
  356.4 9.2 %collective-permute-start.30 = (f32[16,768]{1,0:T(8,128)}, f32[16,768]{1,0:T(8,128)S(1)}, u32[]{:S(2)}, u32[]{:S(2)}) collective-permute-start(f32[16,768]{1,0:T(8,128)} %get-tuple-element.236.refs_1_), channel_id=1, source_target_pairs={{0,4},{4,0},{8,12},{12,8},{1,5},{5,1},{9,13},{13,9},{2,6},{6,2},{1... | collective-permute-start | bytes 147464 | tf_op jit(solution)/shard_map/ppermute | solution.py:855
  365.7 0.6 copy-start.17
  367.7 8.4 %collective-permute-start.32 = (f32[16,768]{1,0:T(8,128)}, f32[16,768]{1,0:T(8,128)S(1)}, u32[]{:S(2)}, u32[]{:S(2)}) collective-permute-start(f32[16,768]{1,0:T(8,128)} %get-tuple-element.242.refs_1_), channel_id=1, source_target_pairs={{0,8},{4,12},{8,0},{12,4},{1,9},{5,13},{9,1},{13,5},{2,10},{6,14},... | collective-permute-start | bytes 147464 | tf_op jit(solution)/shard_map/ppermute | solution.py:855
  376.1 30.0 %collective-permute-start.34 = (bf16[768,768]{1,0:T(8,128)(2,1)}, bf16[768,768]{1,0:T(8,128)(2,1)S(1)}, u32[]{:S(2)}, u32[]{:S(2)}) collective-permute-start(bf16[768,768]{1,0:T(8,128)(2,1)} %collective-permute-done.29.refs_3_), channel_id=1, source_target_pairs={{0,1},{1,0},{2,3},{3,2},{4,5},{5,4},{6,7},{7,6},{8,9},{9,8},{10,11... | collective-permute-start | bytes 3538952 | tf_op jit(solution)/shard_map/ppermute | solution.py:798
  376.1 0.6 copy-start.16
  394.2 1.0 copy-start.5
  395.2 4.1 copy-start.18
  399.3 11.8 %collective-permute-start.33 = (bf16[768,768]{1,0:T(8,128)(2,1)}, bf16[768,768]{1,0:T(8,128)(2,1)S(1)}, u32[]{:S(2)}, u32[]{:S(2)}) collective-permute-start(bf16[768,768]{1,0:T(8,128)(2,1)} %get-tuple-element.247), channel_id=1, source_target_pairs={{0,1},{1,0},{2,3},{3,2},{4,5},{5,4},{6,7},{7,6},{8,9},{9,8},{10,11... | collective-permute-start | bytes 3538952 | tf_op jit(solution)/shard_map/ppermute | solution.py:798
  399.3 4.2 collective-permute-start.35
  406.1 1.0 copy-start.6
  411.1 1.0 copy-start.7
